TPU v7x, 32 devices: a whole 2x2x4 slice. The times are simulated.
32 devices in a mesh: batch: 4 (over z), token: 8 (over y, x, core).
Axes of the slice: x: 2, y: 2, z: 4, core: 2. Of those that a mesh axis runs over, the one named last changes fastest.
Arguments:
- tokens: bfloat16 [16384, 768], P(('batch', 'token')), may hold values from -9 to 9
- slot_weight: bfloat16 [768, 1024], replicated, may hold values from -2 to 2
- expert_in: bfloat16 [128, 768, 3072], P('token', None, 'batch'), may hold values from -1.7265625 to 1.7265625
- expert_out: bfloat16 [128, 3072, 768], P('token', 'batch'), may hold values from -0.6484375 to 0.6484375
Outputs:
- mixed: bfloat16 [16384, 768], P(('batch', 'token'))
All inputs are finite; a program needn't handle non-finite values.
Results may differ from a plain program's by a relative error of at most 0.023.
Values may be sent and summed in bfloat16 or wider, within the bound.
No kernel may reach another device: no remote copies, remote signals or barrier semaphores. Data moves between devices by JAX's collectives and lax.ppermute only.
A program may use at most 128 MiB of HBM per device.

v0:
```python
import functools

import jax
import jax.numpy as jnp
from jax import lax
from jax.experimental import pallas as pl
from jax.experimental.pallas import tpu as pltpu
from jax.sharding import PartitionSpec as P


F32, BF16 = jnp.float32, jnp.bfloat16
CHUNKS = 2
SPLIT_SUMS = False
STATS = 8


def in_vmem(x):
    return pltpu.with_memory_space_constraint(x, pltpu.VMEM)


def call(kernel, shapes, operands, *, moved, scalars=0, scratch=(), dtype=BF16, hint=1e11, limit=8 << 20):
    many = isinstance(shapes, list)
    shapes = shapes if many else [shapes]
    scalar, place = pl.BlockSpec(memory_space=pltpu.SMEM), pl.BlockSpec(memory_space=pltpu.VMEM)
    results = pl.pallas_call(
        kernel,
        out_shape=[pltpu.VMEM(shape, dtype) for shape in shapes],
        in_specs=[scalar] * scalars + [place] * (len(operands) - scalars),
        out_specs=[place] * len(shapes),
        scratch_shapes=scratch,
        cost_estimate=pl.CostEstimate(flops=int(hint), bytes_accessed=int(moved), transcendentals=0),
        compiler_params=pltpu.CompilerParams(vmem_limit_bytes=limit),
    )(*operands[:scalars], *[in_vmem(x) for x in operands[scalars:]])
    return results if many else results[0]


def normalize_kernel(x_ref, out_ref):
    x = x_ref[...].astype(F32)
    scale = lax.rsqrt(jnp.mean(x * x, axis=-1, keepdims=True) + 1e-06)
    out_ref[...] = (x * scale).astype(BF16)


def normalize(x):
    return call(normalize_kernel, x.shape, [x], moved=4 * x.size)


def partial_kernel(slots, first, which_ref, own_ref, other_ref, w_ref, *out_refs):
    if len(w_ref.shape) == 2:
        w = w_ref[:, pl.ds(pl.multiple_of(which_ref[0] * slots, slots), slots)]
    else:
        w = w_ref[which_ref[0]]
    span = out_refs[0].shape[0] - STATS
    count = span * len(out_refs)
    if count < slots:
        w = w[:, first : first + count]
    own, other = own_ref[...], other_ref[...]
    l0 = jnp.dot(own, w, preferred_element_type=F32)
    l1 = jnp.dot(other, w, preferred_element_type=F32)
    top = jnp.maximum(jnp.max(l0, axis=0, keepdims=True), jnp.max(l1, axis=0, keepdims=True))
    top = top.astype(BF16).astype(F32)
    e0, e1 = jnp.exp(l0 - top), jnp.exp(l1 - top)
    total = jnp.sum(e0, axis=0, keepdims=True) + jnp.sum(e1, axis=0, keepdims=True)
    dims = (((0,), (0,)), ((), ()))
    value = lax.dot_general(e0.astype(BF16), own, dims, preferred_element_type=F32)
    value += lax.dot_general(e1.astype(BF16), other, dims, preferred_element_type=F32)
    high = total.astype(BF16).astype(F32)
    row = lax.broadcasted_iota(jnp.int32, (STATS, count), 0)
    stats = jnp.where(row == 0, top, jnp.where(row == 1, high, total - high)).astype(BF16)
    value = value.astype(BF16)
    for n, out_ref in enumerate(out_refs):
        part = slice(n * span, (n + 1) * span)
        out_ref[:span, :] = value[part]
        out_ref[span:, :] = jnp.zeros((STATS, out_ref.shape[1]), BF16)
        out_ref[span:, :span] = stats[:, part]


def partial(which, own, other, weight, slots, first, spans):
    rows, width = own.shape
    return call(
        functools.partial(partial_kernel, slots, first),
        [(span + STATS, width) for span in spans],
        [which, own, other, weight],
        moved=4 * rows * width,
        scalars=1,
    )


def combine_kernel(count, *refs):
    parts, out_refs = refs[:count], refs[count:]
    span = out_refs[0].shape[0]
    slots = span * len(out_refs)
    tops = [p[slots : slots + 1, :slots].astype(F32) for p in parts]
    totals = [
        p[slots + 1 : slots + 2, :slots].astype(F32) + p[slots + 2 : slots + 3, :slots].astype(F32)
        for p in parts
    ]
    top = functools.reduce(jnp.maximum, tops)
    factors = [jnp.exp(t - top) for t in tops]
    total = sum(f * t for f, t in zip(factors, totals))
    inverse = 1.0 / total
    shape = (slots, slots)
    eye = lax.broadcasted_iota(jnp.int32, shape, 0) == lax.broadcasted_iota(jnp.int32, shape, 1)
    value = 0.0
    for f, p in zip(factors, parts):
        column = jnp.sum(jnp.where(eye, f * inverse, 0.0), axis=1, keepdims=True)
        value = value + p[:slots, :].astype(F32) * column
    value = value.astype(BF16)
    for n, out_ref in enumerate(out_refs):
        out_ref[...] = value[n * span : (n + 1) * span]


def combine(parts, slots, chunks):
    width = parts[0].shape[1]
    return call(
        functools.partial(combine_kernel, len(parts)),
        [(slots // chunks, width)] * chunks,
        parts,
        moved=2 * len(parts) * slots * width,
    )


def softmax_kernel(step, span, x_ref, w_ref, *out_refs):
    chunks = len(out_refs)

    @pl.loop(0, x_ref.shape[0] // step)
    def _(i):
        rows = pl.ds(pl.multiple_of(i * step, step), step)
        logits = jnp.dot(x_ref[rows, :], w_ref[...], preferred_element_type=F32)
        raised = jnp.exp(logits - jnp.max(logits, axis=1, keepdims=True))
        share = raised / jnp.sum(raised, axis=1, keepdims=True)
        for c, out_ref in enumerate(out_refs):
            pieces = [
                share[:, at : at + span] for at in range(c * span, share.shape[1], chunks * span)
            ]
            out_ref[rows, :] = jnp.concatenate(pieces, axis=1).astype(BF16)


def softmax(x, weight, span, chunks):
    rows, width = x.shape
    slots = weight.shape[1]
    return call(
        functools.partial(softmax_kernel, min(rows, 256), span),
        [(rows, slots // chunks)] * chunks,
        [x, weight],
        moved=2 * (rows * width + width * slots + rows * slots),
    )


def in_hbm(x):
    return pltpu.with_memory_space_constraint(x, pltpu.HBM)


def load_kernel(parts, *refs):
    n = len(parts)
    copies = []
    for i, (first, count) in enumerate(parts):
        copies.append(
            pltpu.make_async_copy(refs[i].at[pl.ds(first, count)], refs[n + i], refs[2 * n].at[i])
        )
        copies[-1].start()
    for copy in copies:
        copy.wait()


def load(weights, parts):
    return pl.pallas_call(
        functools.partial(load_kernel, parts),
        out_shape=[
            pltpu.VMEM((count,) + w.shape[1:], BF16) for w, (_, count) in zip(weights, parts)
        ],
        in_specs=[pl.BlockSpec(memory_space=pl.ANY)] * len(parts),
        out_specs=[pl.BlockSpec(memory_space=pltpu.VMEM)] * len(parts),
        scratch_shapes=[pltpu.SemaphoreType.DMA((len(parts),))],
        cost_estimate=pl.CostEstimate(flops=int(1e9), bytes_accessed=1, transcendentals=0),
        compiler_params=pltpu.CompilerParams(vmem_limit_bytes=1 << 20),
        name="load",
    )(*[in_hbm(w) for w in weights])


def expert_kernel(count, n, each, first, *refs):
    xs, w_in, w_out = refs[:count], refs[count], refs[count + 1]
    if first is None:
        ys = refs[-count:]
        fetch = lambda e: []
    else:
        far_out = w_out
        w_out, sems = refs[-2:]
        ys = refs[-count - 2 : -2]

        def fetch(e):
            return [pltpu.make_async_copy(far_out.at[first + e], w_out.at[e], sems.at[e])]

        for e in range(n):
            for copy in fetch(e):
                copy.start()

    @pl.loop(0, n)
    def _(e):
        at = pl.ds(pl.multiple_of(e * each, each), each)
        rows = jnp.concatenate([x[at, :] for x in xs], axis=0)
        hidden = jnp.dot(rows, w_in[e], preferred_element_type=F32)
        hidden = (0.5 * hidden * (1.0 + lax.erf(hidden * 0.7071067811865476))).astype(BF16)
        for copy in fetch(e):
            copy.wait()
        terms = jnp.dot(hidden, w_out[e], preferred_element_type=F32)
        for k, y in enumerate(ys):
            y[at, :] = terms[k * each : (k + 1) * each].astype(BF16)


def experts(xs, w_in, w_out, first, count):
    rows, width = xs[0].shape
    hidden = w_in.shape[2]
    near = pl.BlockSpec(memory_space=pltpu.VMEM)
    far = first is not None
    scratch = [
        pltpu.VMEM((count, hidden, width), BF16),
        pltpu.SemaphoreType.DMA((count,)),
    ]
    return pl.pallas_call(
        functools.partial(expert_kernel, len(xs), count, rows // count, first),
        out_shape=[pltpu.VMEM((rows, width), BF16)] * len(xs),
        in_specs=[near] * (len(xs) + 1) + [pl.BlockSpec(memory_space=pl.ANY) if far else near],
        out_specs=[near] * len(xs),
        scratch_shapes=scratch if far else [],
        cost_estimate=pl.CostEstimate(flops=int(1e9), bytes_accessed=1, transcendentals=0),
        compiler_params=pltpu.CompilerParams(
            vmem_limit_bytes=(4 << 20) + (2 * count * width * hidden if far else 0)
        ),
        name="experts",
    )(*[in_vmem(x) for x in xs], in_vmem(w_in), in_hbm(w_out) if far else in_vmem(w_out))


def total_kernel(count, *refs):
    refs[count][...] = sum(r[...].astype(F32) for r in refs[:count]).astype(BF16)


def add_up(parts):
    rows, width = parts[0].shape
    return call(
        functools.partial(total_kernel, len(parts)),
        (rows, width),
        parts,
        moved=2 * len(parts) * rows * width,
    )


def place_rows(at_ref, blocks, held):
    span = blocks[0].shape[0]
    for j, block in enumerate(blocks):
        held[pl.ds(pl.multiple_of(at_ref[j] * span, 8), span), :] = block[...]


def first_mix_kernel(at_ref, c_ref, *refs):
    *blocks, out_ref, held = refs
    place_rows(at_ref, blocks, held)
    out_ref[...] = jnp.dot(c_ref[...], held[...], preferred_element_type=F32)


def last_mix_kernel(steps, at_ref, c_ref, sum_ref, *refs):
    *blocks, out_ref, held, made, sems = refs
    place_rows(at_ref, blocks, held)
    step = c_ref.shape[0] // steps
    copies = []
    for i in range(steps):
        rows = pl.ds(i * step, step)
        total = sum_ref[rows, :] + jnp.dot(c_ref[rows, :], held[...], preferred_element_type=F32)
        made[rows, :] = total.astype(BF16)
        copies.append(pltpu.make_async_copy(made.at[rows, :], out_ref.at[rows, :], sems.at[i]))
        copies[-1].start()
    for copy in copies:
        copy.wait()


def first_mix(at, weights, blocks):
    rows, slots = weights.shape
    width = blocks[0].shape[1]
    return call(
        first_mix_kernel,
        (rows, width),
        [at, weights, *blocks],
        moved=2 * (rows * slots + slots * width + rows * width),
        scalars=1,
        scratch=[pltpu.VMEM((slots, width), BF16)],
        dtype=F32,
    )


def last_mix(at, weights, before, blocks):
    rows, slots = weights.shape
    width = blocks[0].shape[1]
    steps = 4
    place = pl.BlockSpec(memory_space=pltpu.VMEM)
    return pl.pallas_call(
        functools.partial(last_mix_kernel, steps),
        out_shape=jax.ShapeDtypeStruct((rows, width), BF16),
        in_specs=[pl.BlockSpec(memory_space=pltpu.SMEM)] + [place] * (len(blocks) + 2),
        out_specs=pl.BlockSpec(memory_space=pl.ANY),
        scratch_shapes=[
            pltpu.VMEM((slots, width), BF16),
            pltpu.VMEM((rows, width), BF16),
            pltpu.SemaphoreType.DMA((steps,)),
        ],
        compiler_params=pltpu.CompilerParams(vmem_limit_bytes=8 << 20),
        name="last_mix",
    )(at, in_vmem(weights), in_vmem(before), *[in_vmem(b) for b in blocks])


def body(tokens, slot_weight, expert_in, expert_out):
    n_token, n_batch = lax.axis_size("token"), lax.axis_size("batch")
    me = lax.axis_index("token")
    chips = n_token // 2
    experts_here = expert_in.shape[0]
    slots = slot_weight.shape[1] // n_token
    width = tokens.shape[1]
    chunk_experts, span = experts_here // CHUNKS, slots // CHUNKS

    def over_token(x, k):
        return lax.ppermute(x, "token", [(i, i ^ k) for i in range(n_token)])

    def over_batch(x, k):
        return lax.ppermute(x, "batch", [(i, i ^ k) for i in range(n_batch)])

    other = normalize(over_token(tokens, 1))
    own = normalize(tokens)
    if slots % 128:
        weight = slot_weight.reshape(width, n_token, slots).transpose(1, 0, 2)
    else:
        weight = slot_weight
    here, there = (0, chunk_experts), (chunk_experts, chunk_experts)
    (in0,) = load([expert_in], [here])
    out0, in1 = load([expert_out, expert_in], [here, there])
    ins = [in0, in1]
    groups = [[c] for c in range(CHUNKS)] if SPLIT_SUMS else [list(range(CHUNKS))]
    inputs = []
    for group in groups:
        arrived = []
        count = span * len(group)
        for k in reversed(range(chips)):
            which = jnp.bitwise_xor(me, 2 * k).astype(jnp.int32)[None]
            (sent,) = partial(which, own, other, weight, slots, group[0] * span, [count])
            arrived.append(over_token(sent, 2 * k) if k else sent)
        inputs += combine(arrived, count, len(group))
    weights = softmax(own, slot_weight, span, CHUNKS)

    order = [2 * k for k in range(chips)] + [2 * k + 1 for k in range(chips)]
    at = jnp.bitwise_xor(me, jnp.array(order, jnp.int32))
    xs = []
    for x in inputs:
        xs.append([over_batch(x, k) if k else x for k in reversed(range(n_batch))])
    parts = []
    for c in range(CHUNKS):
        far = c * chunk_experts if c else None
        ys = experts(xs[c], ins[c], expert_out if c else out0, far, chunk_experts)
        parts.append([over_batch(y, k) if k else y for k, y in zip(reversed(range(n_batch)), ys)])
    total = None
    for c in range(CHUNKS):
        rows = add_up(parts[c])
        there = [over_token(rows, 2 * k) if k else rows for k in range(chips)]
        if c < CHUNKS - 1:
            swapped = over_token(jnp.concatenate(there, axis=0), 1)
            blocks = there + [swapped[k * span : (k + 1) * span] for k in range(chips)]
            total = first_mix(at, weights[c], blocks)
        else:
            last = [over_token(there[0], 1)]
            last += [over_token(r, 1) for r in there[1:]]
            blocks = there + last
    return last_mix(at, weights[-1], total, blocks)


def solution(mesh):
    placed = (
        P(("batch", "token"), None),
        P(),
        P("token", None, "batch"),
        P("token", "batch", None),
    )

    return jax.shard_map(
        body, mesh=mesh, in_specs=placed, out_specs=P(("batch", "token"), None), check_vma=False
    )
```

profile of v0, /device:TPU:0, one launch (start us, length us, event | category | flops | bytes accessed | tf_op | source)
XLA Modules:
  0.0 90.8 jit_solution(907944414570485423)
XLA Ops:
  0.0 0.5 collective-permute-start
  0.5 1.1 %copy-done.2 = bf16[512,768]{1,0:T(8,128)(2,1)S(1)} copy-done((bf16[512,768]{1,0:T(8,128)(2,1)S(1)}, bf16[512,768]{1,0:T(8,128)(2,1)}, u32[]{:S(2)}) %copy-start.2) | copy-done | bytes 786456
  1.6 0.2 shard_map.55.x_ref.own_ref
  1.9 0.0 copy-start
  1.9 0.7 collective-permute-done.x_ref
  2.6 0.2 shard_map.57.other_ref
  2.9 0.4 copy-done
  3.3 1.9 %shard_map.58 = bf16[136,768]{1,0:T(8,128)(2,1)} custom-call(s32[1]{0:T(128)} %bitcast.which_ref, bf16[512,768]{1,0:T(8,128)(2,1)S(1)} %shard_map.55.x_ref.own_ref, bf16[512,768]{1,0:T(8,128)(2,1)S(1)} %shard_map.57.other_ref, bf16[768,1024]{1,0:T(8,128)(2,1)S(1)} %copy-done), custom_call_target="tpu_custom_call" | custom-call | flops 99999997952 | bytes 1572864 | tf_op jit(solution)/shard_map/pallas_call | solution.py:25
  5.1 3.4 %collective-permute-start.1 = (bf16[136,768]{1,0:T(8,128)(2,1)}, bf16[136,768]{1,0:T(8,128)(2,1)}, u32[]{:S(2)}, u32[]{:S(2)}) collective-permute-start(bf16[136,768]{1,0:T(8,128)(2,1)} %shard_map.58), channel_id=1, source_target_pairs={{0,6},{1,7},{2,4},{3,5},{4,2},{5,3},{6,0},{7,1},{8,14},{9,15},{10,... | collective-permute-start | bytes 626696 | tf_op jit(solution)/shard_map/ppermute | solution.py:318
  8.6 1.9 %shard_map.59 = bf16[136,768]{1,0:T(8,128)(2,1)} custom-call(s32[1]{0:T(128)} %bitcast.1.which_ref, bf16[512,768]{1,0:T(8,128)(2,1)S(1)} %shard_map.55.x_ref.own_ref, bf16[512,768]{1,0:T(8,128)(2,1)S(1)} %shard_map.57.other_ref, bf16[768,1024]{1,0:T(8,128)(2,1)S(1)} %copy-done), custom_call_target="tpu_custom_call" | custom-call | flops 99999997952 | bytes 1572864 | tf_op jit(solution)/shard_map/pallas_call | solution.py:25
  10.4 0.5 collective-permute-start.2
  10.9 1.2 %shard_map.60 = bf16[136,768]{1,0:T(8,128)(2,1)S(1)} custom-call(s32[1]{0:T(128)} %bitcast.2.which_ref, bf16[512,768]{1,0:T(8,128)(2,1)S(1)} %shard_map.55.x_ref.own_ref, bf16[512,768]{1,0:T(8,128)(2,1)S(1)} %shard_map.57.other_ref, bf16[768,1024]{1,0:T(8,128)(2,1)S(1)} %copy-done), custom_call_target="tpu_custom_call" | custom-call | flops 99999997952 | bytes 1572864 | tf_op jit(solution)/shard_map/pallas_call | solution.py:25
  12.1 0.1 collective-permute-start.3
  12.2 1.2 %shard_map.61.refs_3_ = bf16[136,768]{1,0:T(8,128)(2,1)S(1)} custom-call(s32[1]{0:T(128)} %bitcast.3.which_ref, bf16[512,768]{1,0:T(8,128)(2,1)S(1)} %shard_map.55.x_ref.own_ref, bf16[512,768]{1,0:T(8,128)(2,1)S(1)} %shard_map.57.other_ref, bf16[768,1024]{1,0:T(8,128)(2,1)S(1)} %copy-done), custom_call_target="tpu_custom_call" | custom-call | flops 99999997952 | bytes 1572864 | tf_op jit(solution)/shard_map/pallas_call | solution.py:25
  13.4 1.4 %collective-permute-done.1.refs_0_ = bf16[136,768]{1,0:T(8,128)(2,1)} collective-permute-done((bf16[136,768]{1,0:T(8,128)(2,1)}, bf16[136,768]{1,0:T(8,128)(2,1)}, u32[]{:S(2)}, u32[]{:S(2)}) %collective-permute-start.1) | collective-permute-done | bytes 208928 | tf_op jit(solution)/shard_map/ppermute | solution.py:318
  14.8 4.4 %collective-permute-done.2.refs_1_ = bf16[136,768]{1,0:T(8,128)(2,1)} collective-permute-done((bf16[136,768]{1,0:T(8,128)(2,1)}, bf16[136,768]{1,0:T(8,128)(2,1)}, u32[]{:S(2)}, u32[]{:S(2)}) %collective-permute-start.2) | collective-permute-done | bytes 208928 | tf_op jit(solution)/shard_map/ppermute | solution.py:318
  19.2 0.2 collective-permute-done.3.refs_2_
  19.4 1.9 %shard_map.62 = (bf16[64,768]{1,0:T(8,128)(2,1)S(1)}, bf16[64,768]{1,0:T(8,128)(2,1)}) custom-call(bf16[136,768]{1,0:T(8,128)(2,1)} %collective-permute-done.1.refs_0_, bf16[136,768]{1,0:T(8,128)(2,1)} %collective-permute-done.2.refs_1_, bf16[136,768]{1,0:T(8,128)(2,1)S(1)} %collective-permute-done.3.refs_2_, bf16[136,768]{1,0:T(8,128)(2,1)S(1)} %shard_map.61.refs_3_), custom_call_target="tpu_custom_call" | custom-call | flops 99999997952 | bytes 786432 | tf_op jit(solution)/shard_map/pallas_call | solution.py:25
  21.3 3.6 %collective-permute-start.4 = (bf16[64,768]{1,0:T(8,128)(2,1)S(1)}, bf16[64,768]{1,0:T(8,128)(2,1)S(1)}, u32[]{:S(2)}, u32[]{:S(2)}) collective-permute-start(bf16[64,768]{1,0:T(8,128)(2,1)S(1)} %get-tuple-element.21.refs_3_), channel_id=1, source_target_pairs={{0,24},{8,16},{16,8},{24,0},{1,25},{9,17},{17,9},{25,1},{2,26},{10... | collective-permute-start | bytes 294920 | tf_op jit(solution)/shard_map/ppermute | solution.py:321
  24.9 0.0 collective-permute-start.5
  24.9 0.8 collective-permute-start.6
  25.7 3.7 %load.2.refs_4_ = bf16[8,768,768]{2,1,0:T(8,128)(2,1)S(1)} custom-call(bf16[16,768,768]{2,1,0:T(8,128)(2,1)} %refs_1_.1), custom_call_target="tpu_custom_call" | custom-call | flops 1000000000 | bytes 1 | tf_op jit(solution)/shard_map/load/pallas_call | solution.py:166
  29.4 6.4 %load.3 = (bf16[8,768,768]{2,1,0:T(8,128)(2,1)S(1)}, bf16[8,768,768]{2,1,0:T(8,128)(2,1)S(1)}) custom-call(bf16[16,768,768]{2,1,0:T(8,128)(2,1)} %refs_5_.1, bf16[16,768,768]{2,1,0:T(8,128)(2,1)} %refs_1_.1), custom_call_target="tpu_custom_call" | custom-call | flops 1000000000 | bytes 1 | tf_op jit(solution)/shard_map/load/pallas_call | solution.py:166
  35.8 0.0 collective-permute-done.4.refs_0_
  35.8 0.0 collective-permute-done.5.refs_1_
  35.8 0.0 collective-permute-done.6.refs_2_
  35.8 4.8 %experts.2 = (bf16[64,768]{1,0:T(8,128)(2,1)S(1)}, bf16[64,768]{1,0:T(8,128)(2,1)S(1)}, bf16[64,768]{1,0:T(8,128)(2,1)S(1)}, bf16[64,768]{1,0:T(8,128)(2,1)S(1)}) custom-call(bf16[64,768]{1,0:T(8,128)(2,1)S(1)} %collective-permute-done.4.refs_0_, bf16[64,768]{1,0:T(8,128)(2,1)S(1)} %collective-permute-done.5.refs_1_, ...), custom_call_target="tpu_custom_call" | custom-call | flops 1000000000 | bytes 1 | tf_op jit(solution)/shard_map/experts/pallas_call | solution.py:219
  40.6 3.6 %collective-permute-start.7 = (bf16[64,768]{1,0:T(8,128)(2,1)S(1)}, bf16[64,768]{1,0:T(8,128)(2,1)S(1)}, u32[]{:S(2)}, u32[]{:S(2)}) collective-permute-start(bf16[64,768]{1,0:T(8,128)(2,1)S(1)} %get-tuple-element.23), channel_id=1, source_target_pairs={{0,24},{8,16},{16,8},{24,0},{1,25},{9,17},{17,9},{25,1},{2,26},{10... | collective-permute-start | bytes 294920 | tf_op jit(solution)/shard_map/ppermute | solution.py:321
  44.2 0.0 collective-permute-start.8
  44.2 0.8 collective-permute-start.9
  45.0 3.6 %collective-permute-start.14 = (bf16[64,768]{1,0:T(8,128)(2,1)}, bf16[64,768]{1,0:T(8,128)(2,1)S(1)}, u32[]{:S(2)}, u32[]{:S(2)}) collective-permute-start(bf16[64,768]{1,0:T(8,128)(2,1)} %get-tuple-element.27.refs_3_), channel_id=1, source_target_pairs={{0,24},{8,16},{16,8},{24,0},{1,25},{9,17},{17,9},{25,1},{2,26},{10... | collective-permute-start | bytes 294920 | tf_op jit(solution)/shard_map/ppermute | solution.py:321
  48.6 4.1 %collective-permute-start.16 = (bf16[64,768]{1,0:T(8,128)(2,1)}, bf16[64,768]{1,0:T(8,128)(2,1)}, u32[]{:S(2)}, u32[]{:S(2)}) collective-permute-start(bf16[64,768]{1,0:T(8,128)(2,1)} %get-tuple-element.27.refs_3_), channel_id=1, source_target_pairs={{0,8},{8,0},{16,24},{24,16},{1,9},{9,1},{17,25},{25,17},{2,10},{10... | collective-permute-start | bytes 294920 | tf_op jit(solution)/shard_map/ppermute | solution.py:321
  52.7 4.3 %collective-permute-done.8.refs_1_ = bf16[64,768]{1,0:T(8,128)(2,1)S(1)} collective-permute-done((bf16[64,768]{1,0:T(8,128)(2,1)S(1)}, bf16[64,768]{1,0:T(8,128)(2,1)S(1)}, u32[]{:S(2)}, u32[]{:S(2)}) %collective-permute-start.8) | collective-permute-done | bytes 98336 | tf_op jit(solution)/shard_map/ppermute | solution.py:321
  57.0 0.1 shard_map.63.refs_0_
  57.1 1.5 %collective-permute-start.10 = (bf16[64,768]{1,0:T(8,128)(2,1)S(1)}, bf16[64,768]{1,0:T(8,128)(2,1)S(1)}, u32[]{:S(2)}, u32[]{:S(2)}) collective-permute-start(bf16[64,768]{1,0:T(8,128)(2,1)S(1)} %shard_map.63.refs_0_), channel_id=1, source_target_pairs={{0,2},{1,3},{2,0},{3,1},{4,6},{5,7},{6,4},{7,5},{8,10},{9,11},{10,... | collective-permute-start | bytes 294920 | tf_op jit(solution)/shard_map/ppermute | solution.py:318
  58.6 1.5 %collective-permute-start.11 = (bf16[64,768]{1,0:T(8,128)(2,1)S(1)}, bf16[64,768]{1,0:T(8,128)(2,1)S(1)}, u32[]{:S(2)}, u32[]{:S(2)}) collective-permute-start(bf16[64,768]{1,0:T(8,128)(2,1)S(1)} %shard_map.63.refs_0_), channel_id=1, source_target_pairs={{0,4},{1,5},{2,6},{3,7},{4,0},{5,1},{6,2},{7,3},{8,12},{9,13},{10,... | collective-permute-start | bytes 294920 | tf_op jit(solution)/shard_map/ppermute | solution.py:318
  60.1 0.0 collective-permute-done.14.refs_0_
  60.1 0.5 collective-permute-start.12
  60.6 1.9 %shard_map.56 = (bf16[512,512]{1,0:T(8,128)(2,1)S(1)}, bf16[512,512]{1,0:T(8,128)(2,1)S(1)}) custom-call(bf16[512,768]{1,0:T(8,128)(2,1)S(1)} %shard_map.55.x_ref.own_ref, bf16[768,1024]{1,0:T(8,128)(2,1)S(1)} %copy-done.1), custom_call_target="tpu_custom_call" | custom-call | flops 99999997952 | bytes 3407872 | tf_op jit(solution)/shard_map/pallas_call | solution.py:25
  62.5 0.0 collective-permute-done.16.refs_2_
  62.5 7.6 %experts.3 = (bf16[64,768]{1,0:T(8,128)(2,1)S(1)}, bf16[64,768]{1,0:T(8,128)(2,1)S(1)}, bf16[64,768]{1,0:T(8,128)(2,1)S(1)}, bf16[64,768]{1,0:T(8,128)(2,1)S(1)}) custom-call(bf16[64,768]{1,0:T(8,128)(2,1)S(1)} %collective-permute-done.14.refs_0_, bf16[64,768]{1,0:T(8,128)(2,1)} %collective-permute-done.15.refs_1_, ...), custom_call_target="tpu_custom_call" | custom-call | flops 1000000000 | bytes 1 | tf_op jit(solution)/shard_map/experts/pallas_call | solution.py:219
  70.2 2.9 %collective-permute-start.17 = (bf16[64,768]{1,0:T(8,128)(2,1)S(1)}, bf16[64,768]{1,0:T(8,128)(2,1)S(1)}, u32[]{:S(2)}, u32[]{:S(2)}) collective-permute-start(bf16[64,768]{1,0:T(8,128)(2,1)S(1)} %get-tuple-element.29), channel_id=1, source_target_pairs={{0,24},{8,16},{16,8},{24,0},{1,25},{9,17},{17,9},{25,1},{2,26},{10... | collective-permute-start | bytes 294920 | tf_op jit(solution)/shard_map/ppermute | solution.py:321
  73.1 0.1 collective-permute-start.18
  73.2 0.0 collective-permute-done.10.refs_1_
  73.2 1.4 %collective-permute-start.19 = (bf16[64,768]{1,0:T(8,128)(2,1)S(1)}, bf16[64,768]{1,0:T(8,128)(2,1)S(1)}, u32[]{:S(2)}, u32[]{:S(2)}) collective-permute-start(bf16[64,768]{1,0:T(8,128)(2,1)S(1)} %get-tuple-element.31), channel_id=1, source_target_pairs={{0,8},{8,0},{16,24},{24,16},{1,9},{9,1},{17,25},{25,17},{2,10},{10... | collective-permute-start | bytes 294920 | tf_op jit(solution)/shard_map/ppermute | solution.py:321
  74.7 0.0 collective-permute-done.11.refs_2_
  74.7 0.0 collective-permute-done.12.refs_3_
  74.7 0.1 collective-permute-start.13
  74.8 2.0 %collective-permute-done.17.refs_0_ = bf16[64,768]{1,0:T(8,128)(2,1)S(1)} collective-permute-done((bf16[64,768]{1,0:T(8,128)(2,1)S(1)}, bf16[64,768]{1,0:T(8,128)(2,1)S(1)}, u32[]{:S(2)}, u32[]{:S(2)}) %collective-permute-start.17) | collective-permute-done | bytes 98336 | tf_op jit(solution)/shard_map/ppermute | solution.py:321
  76.8 3.2 %collective-permute-done.18.refs_1_ = bf16[64,768]{1,0:T(8,128)(2,1)S(1)} collective-permute-done((bf16[64,768]{1,0:T(8,128)(2,1)S(1)}, bf16[64,768]{1,0:T(8,128)(2,1)S(1)}, u32[]{:S(2)}, u32[]{:S(2)}) %collective-permute-start.18) | collective-permute-done | bytes 98336 | tf_op jit(solution)/shard_map/ppermute | solution.py:321
  80.0 0.0 collective-permute-done.19.refs_2_
  80.0 0.1 shard_map.65.refs_0_
  80.0 0.8 collective-permute-start.20
  80.8 1.2 %collective-permute-start.21 = (bf16[64,768]{1,0:T(8,128)(2,1)S(1)}, bf16[64,768]{1,0:T(8,128)(2,1)S(1)}, u32[]{:S(2)}, u32[]{:S(2)}) collective-permute-start(bf16[64,768]{1,0:T(8,128)(2,1)S(1)} %shard_map.65.refs_0_), channel_id=1, source_target_pairs={{0,4},{1,5},{2,6},{3,7},{4,0},{5,1},{6,2},{7,3},{8,12},{9,13},{10,... | collective-permute-start | bytes 294920 | tf_op jit(solution)/shard_map/ppermute | solution.py:318
  82.0 1.5 %collective-permute-start.22 = (bf16[64,768]{1,0:T(8,128)(2,1)S(1)}, bf16[64,768]{1,0:T(8,128)(2,1)S(1)}, u32[]{:S(2)}, u32[]{:S(2)}) collective-permute-start(bf16[64,768]{1,0:T(8,128)(2,1)S(1)} %shard_map.65.refs_0_), channel_id=1, source_target_pairs={{0,6},{1,7},{2,4},{3,5},{4,2},{5,3},{6,0},{7,1},{8,14},{9,15},{10,... | collective-permute-start | bytes 294920 | tf_op jit(solution)/shard_map/ppermute | solution.py:318
  83.6 0.0 collective-permute-start.23
  83.6 2.0 %collective-permute-done.20.refs_1_ = bf16[64,768]{1,0:T(8,128)(2,1)S(1)} collective-permute-done((bf16[64,768]{1,0:T(8,128)(2,1)S(1)}, bf16[64,768]{1,0:T(8,128)(2,1)S(1)}, u32[]{:S(2)}, u32[]{:S(2)}) %collective-permute-start.20) | collective-permute-done | bytes 98336 | tf_op jit(solution)/shard_map/ppermute | solution.py:318
  85.6 0.1 collective-permute-done.21.refs_2_
  85.7 0.5 collective-permute-start.25
  86.1 1.4 %collective-permute-done.22.refs_3_ = bf16[64,768]{1,0:T(8,128)(2,1)S(1)} collective-permute-done((bf16[64,768]{1,0:T(8,128)(2,1)S(1)}, bf16[64,768]{1,0:T(8,128)(2,1)S(1)}, u32[]{:S(2)}, u32[]{:S(2)}) %collective-permute-start.22) | collective-permute-done | bytes 98336 | tf_op jit(solution)/shard_map/ppermute | solution.py:318
  87.6 1.2 %shard_map.64.sum_ref = f32[512,768]{1,0:T(8,128)S(1)} custom-call(s32[8]{0:T(128)S(1)} %broadcast_xor_fusion.at_ref, bf16[512,512]{1,0:T(8,128)(2,1)S(1)} %get-tuple-element.20.c_ref, bf16[64,768]{1,0:T(8,128)(2,1)S(1)} %shard_map.63.refs_0_, bf16[64,768]{1,0:T(8,128)(2,1)S(1)} %collective-permute-done.10.refs_1_, ...), custom_call_target="tpu_custom_call" | custom-call | flops 99999997952 | bytes 2097152 | tf_op jit(solution)/shard_map/pallas_call | solution.py:25
  88.8 0.0 collective-permute-done.23.refs_4_
  88.8 0.1 collective-permute-done.26.refs_7_
  88.9 1.9 %last_mix.1 = bf16[512,768]{1,0:T(8,128)(2,1)} custom-call(s32[8]{0:T(128)S(1)} %broadcast_xor_fusion.at_ref, bf16[512,512]{1,0:T(8,128)(2,1)S(1)} %get-tuple-element.19.c_ref, f32[512,768]{1,0:T(8,128)S(1)} %shard_map.64.sum_ref, bf16[64,768]{1,0:T(8,128)(2,1)S(1)} %shard_map.65.refs_0_, bf16[64,768]{1,0:T(8,128)(2,1)S(1)} %collective-permute-done.20.refs_1_, ...), custom_call_target="tpu_custom_call" | custom-call | tf_op jit(solution)/shard_map/last_mix/pallas_call | solution.py:293
  (17 shorter events, 0.1 us)
Async XLA Ops:
  0.0 2.6 %collective-permute-start = (bf16[512,768]{1,0:T(8,128)(2,1)}, bf16[512,768]{1,0:T(8,128)(2,1)S(1)}, u32[]{:S(2)}, u32[]{:S(2)}) collective-permute-start(bf16[512,768]{1,0:T(8,128)(2,1)} %x_ref.1), channel_id=1, source_target_pairs={{0,1},{1,0},{2,3},{3,2},{4,5},{5,4},{6,7},{7,6},{8,9},{9,8},{10,11... | collective-permute-start | bytes 2359304 | tf_op jit(solution)/shard_map/ppermute | solution.py:318
  0.5 1.1 %copy-start.2 = (bf16[512,768]{1,0:T(8,128)(2,1)S(1)}, bf16[512,768]{1,0:T(8,128)(2,1)}, u32[]{:S(2)}) copy-start(bf16[512,768]{1,0:T(8,128)(2,1)} %x_ref.1) | copy-start | bytes 2359300
  1.9 1.4 %copy-start = (bf16[768,1024]{1,0:T(8,128)(2,1)S(1)}, bf16[768,1024]{1,0:T(8,128)(2,1)}, u32[]{:S(2)}) copy-start(bf16[768,1024]{1,0:T(8,128)(2,1)} %w_ref.9) | copy-start | bytes 4718596
  5.1 9.7 %collective-permute-start.1 = (bf16[136,768]{1,0:T(8,128)(2,1)}, bf16[136,768]{1,0:T(8,128)(2,1)}, u32[]{:S(2)}, u32[]{:S(2)}) collective-permute-start(bf16[136,768]{1,0:T(8,128)(2,1)} %shard_map.58), channel_id=1, source_target_pairs={{0,6},{1,7},{2,4},{3,5},{4,2},{5,3},{6,0},{7,1},{8,14},{9,15},{10,... | collective-permute-start | bytes 626696 | tf_op jit(solution)/shard_map/ppermute | solution.py:318
  10.4 8.8 %collective-permute-start.2 = (bf16[136,768]{1,0:T(8,128)(2,1)}, bf16[136,768]{1,0:T(8,128)(2,1)}, u32[]{:S(2)}, u32[]{:S(2)}) collective-permute-start(bf16[136,768]{1,0:T(8,128)(2,1)} %shard_map.59), channel_id=1, source_target_pairs={{0,4},{1,5},{2,6},{3,7},{4,0},{5,1},{6,2},{7,3},{8,12},{9,13},{10,... | collective-permute-start | bytes 626696 | tf_op jit(solution)/shard_map/ppermute | solution.py:318
  12.1 7.3 %collective-permute-start.3 = (bf16[136,768]{1,0:T(8,128)(2,1)S(1)}, bf16[136,768]{1,0:T(8,128)(2,1)S(1)}, u32[]{:S(2)}, u32[]{:S(2)}) collective-permute-start(bf16[136,768]{1,0:T(8,128)(2,1)S(1)} %shard_map.60), channel_id=1, source_target_pairs={{0,2},{1,3},{2,0},{3,1},{4,6},{5,7},{6,4},{7,5},{8,10},{9,11},{10,... | collective-permute-start | bytes 626696 | tf_op jit(solution)/shard_map/ppermute | solution.py:318
  21.3 14.5 %collective-permute-start.4 = (bf16[64,768]{1,0:T(8,128)(2,1)S(1)}, bf16[64,768]{1,0:T(8,128)(2,1)S(1)}, u32[]{:S(2)}, u32[]{:S(2)}) collective-permute-start(bf16[64,768]{1,0:T(8,128)(2,1)S(1)} %get-tuple-element.21.refs_3_), channel_id=1, source_target_pairs={{0,24},{8,16},{16,8},{24,0},{1,25},{9,17},{17,9},{25,1},{2,26},{10... | collective-permute-start | bytes 294920 | tf_op jit(solution)/shard_map/ppermute | solution.py:321
  24.9 10.9 %collective-permute-start.5 = (bf16[64,768]{1,0:T(8,128)(2,1)S(1)}, bf16[64,768]{1,0:T(8,128)(2,1)S(1)}, u32[]{:S(2)}, u32[]{:S(2)}) collective-permute-start(bf16[64,768]{1,0:T(8,128)(2,1)S(1)} %get-tuple-element.21.refs_3_), channel_id=1, source_target_pairs={{0,16},{8,24},{16,0},{24,8},{1,17},{9,25},{17,1},{25,9},{2,18},{10... | collective-permute-start | bytes 294920 | tf_op jit(solution)/shard_map/ppermute | solution.py:321
  24.9 10.9 %collective-permute-start.6 = (bf16[64,768]{1,0:T(8,128)(2,1)S(1)}, bf16[64,768]{1,0:T(8,128)(2,1)S(1)}, u32[]{:S(2)}, u32[]{:S(2)}) collective-permute-start(bf16[64,768]{1,0:T(8,128)(2,1)S(1)} %get-tuple-element.21.refs_3_), channel_id=1, source_target_pairs={{0,8},{8,0},{16,24},{24,16},{1,9},{9,1},{17,25},{25,17},{2,10},{10... | collective-permute-start | bytes 294920 | tf_op jit(solution)/shard_map/ppermute | solution.py:321
  40.6 8.0 %collective-permute-start.7 = (bf16[64,768]{1,0:T(8,128)(2,1)S(1)}, bf16[64,768]{1,0:T(8,128)(2,1)S(1)}, u32[]{:S(2)}, u32[]{:S(2)}) collective-permute-start(bf16[64,768]{1,0:T(8,128)(2,1)S(1)} %get-tuple-element.23), channel_id=1, source_target_pairs={{0,24},{8,16},{16,8},{24,0},{1,25},{9,17},{17,9},{25,1},{2,26},{10... | collective-permute-start | bytes 294920 | tf_op jit(solution)/shard_map/ppermute | solution.py:321
  44.2 12.8 %collective-permute-start.8 = (bf16[64,768]{1,0:T(8,128)(2,1)S(1)}, bf16[64,768]{1,0:T(8,128)(2,1)S(1)}, u32[]{:S(2)}, u32[]{:S(2)}) collective-permute-start(bf16[64,768]{1,0:T(8,128)(2,1)S(1)} %get-tuple-element.24), channel_id=1, source_target_pairs={{0,16},{8,24},{16,0},{24,8},{1,17},{9,25},{17,1},{25,9},{2,18},{10... | collective-permute-start | bytes 294920 | tf_op jit(solution)/shard_map/ppermute | solution.py:321
  44.2 12.8 %collective-permute-start.9 = (bf16[64,768]{1,0:T(8,128)(2,1)S(1)}, bf16[64,768]{1,0:T(8,128)(2,1)S(1)}, u32[]{:S(2)}, u32[]{:S(2)}) collective-permute-start(bf16[64,768]{1,0:T(8,128)(2,1)S(1)} %get-tuple-element.25), channel_id=1, source_target_pairs={{0,8},{8,0},{16,24},{24,16},{1,9},{9,1},{17,25},{25,17},{2,10},{10... | collective-permute-start | bytes 294920 | tf_op jit(solution)/shard_map/ppermute | solution.py:321
  45.0 15.2 %collective-permute-start.14 = (bf16[64,768]{1,0:T(8,128)(2,1)}, bf16[64,768]{1,0:T(8,128)(2,1)S(1)}, u32[]{:S(2)}, u32[]{:S(2)}) collective-permute-start(bf16[64,768]{1,0:T(8,128)(2,1)} %get-tuple-element.27.refs_3_), channel_id=1, source_target_pairs={{0,24},{8,16},{16,8},{24,0},{1,25},{9,17},{17,9},{25,1},{2,26},{10... | collective-permute-start | bytes 294920 | tf_op jit(solution)/shard_map/ppermute | solution.py:321
  48.6 13.9 %collective-permute-start.15 = (bf16[64,768]{1,0:T(8,128)(2,1)}, bf16[64,768]{1,0:T(8,128)(2,1)}, u32[]{:S(2)}, u32[]{:S(2)}) collective-permute-start(bf16[64,768]{1,0:T(8,128)(2,1)} %get-tuple-element.27.refs_3_), channel_id=1, source_target_pairs={{0,16},{8,24},{16,0},{24,8},{1,17},{9,25},{17,1},{25,9},{2,18},{10... | collective-permute-start | bytes 294920 | tf_op jit(solution)/shard_map/ppermute | solution.py:321
  48.6 13.9 %collective-permute-start.16 = (bf16[64,768]{1,0:T(8,128)(2,1)}, bf16[64,768]{1,0:T(8,128)(2,1)}, u32[]{:S(2)}, u32[]{:S(2)}) collective-permute-start(bf16[64,768]{1,0:T(8,128)(2,1)} %get-tuple-element.27.refs_3_), channel_id=1, source_target_pairs={{0,8},{8,0},{16,24},{24,16},{1,9},{9,1},{17,25},{25,17},{2,10},{10... | collective-permute-start | bytes 294920 | tf_op jit(solution)/shard_map/ppermute | solution.py:321
  57.0 3.6 %copy-start.1 = (bf16[768,1024]{1,0:T(8,128)(2,1)S(1)}, bf16[768,1024]{1,0:T(8,128)(2,1)}, u32[]{:S(2)}) copy-start(bf16[768,1024]{1,0:T(8,128)(2,1)} %w_ref.9) | copy-start | bytes 4718596
  57.1 16.2 %collective-permute-start.10 = (bf16[64,768]{1,0:T(8,128)(2,1)S(1)}, bf16[64,768]{1,0:T(8,128)(2,1)S(1)}, u32[]{:S(2)}, u32[]{:S(2)}) collective-permute-start(bf16[64,768]{1,0:T(8,128)(2,1)S(1)} %shard_map.63.refs_0_), channel_id=1, source_target_pairs={{0,2},{1,3},{2,0},{3,1},{4,6},{5,7},{6,4},{7,5},{8,10},{9,11},{10,... | collective-permute-start | bytes 294920 | tf_op jit(solution)/shard_map/ppermute | solution.py:318
  58.6 16.1 %collective-permute-start.11 = (bf16[64,768]{1,0:T(8,128)(2,1)S(1)}, bf16[64,768]{1,0:T(8,128)(2,1)S(1)}, u32[]{:S(2)}, u32[]{:S(2)}) collective-permute-start(bf16[64,768]{1,0:T(8,128)(2,1)S(1)} %shard_map.63.refs_0_), channel_id=1, source_target_pairs={{0,4},{1,5},{2,6},{3,7},{4,0},{5,1},{6,2},{7,3},{8,12},{9,13},{10,... | collective-permute-start | bytes 294920 | tf_op jit(solution)/shard_map/ppermute | solution.py:318
  60.1 14.5 %collective-permute-start.12 = (bf16[64,768]{1,0:T(8,128)(2,1)S(1)}, bf16[64,768]{1,0:T(8,128)(2,1)S(1)}, u32[]{:S(2)}, u32[]{:S(2)}) collective-permute-start(bf16[64,768]{1,0:T(8,128)(2,1)S(1)} %shard_map.63.refs_0_), channel_id=1, source_target_pairs={{0,6},{1,7},{2,4},{3,5},{4,2},{5,3},{6,0},{7,1},{8,14},{9,15},{10,... | collective-permute-start | bytes 294920 | tf_op jit(solution)/shard_map/ppermute | solution.py:318
  70.2 6.6 %collective-permute-start.17 = (bf16[64,768]{1,0:T(8,128)(2,1)S(1)}, bf16[64,768]{1,0:T(8,128)(2,1)S(1)}, u32[]{:S(2)}, u32[]{:S(2)}) collective-permute-start(bf16[64,768]{1,0:T(8,128)(2,1)S(1)} %get-tuple-element.29), channel_id=1, source_target_pairs={{0,24},{8,16},{16,8},{24,0},{1,25},{9,17},{17,9},{25,1},{2,26},{10... | collective-permute-start | bytes 294920 | tf_op jit(solution)/shard_map/ppermute | solution.py:321
  73.1 6.9 %collective-permute-start.18 = (bf16[64,768]{1,0:T(8,128)(2,1)S(1)}, bf16[64,768]{1,0:T(8,128)(2,1)S(1)}, u32[]{:S(2)}, u32[]{:S(2)}) collective-permute-start(bf16[64,768]{1,0:T(8,128)(2,1)S(1)} %get-tuple-element.30), channel_id=1, source_target_pairs={{0,16},{8,24},{16,0},{24,8},{1,17},{9,25},{17,1},{25,9},{2,18},{10... | collective-permute-start | bytes 294920 | tf_op jit(solution)/shard_map/ppermute | solution.py:321
  73.2 6.7 %collective-permute-start.19 = (bf16[64,768]{1,0:T(8,128)(2,1)S(1)}, bf16[64,768]{1,0:T(8,128)(2,1)S(1)}, u32[]{:S(2)}, u32[]{:S(2)}) collective-permute-start(bf16[64,768]{1,0:T(8,128)(2,1)S(1)} %get-tuple-element.31), channel_id=1, source_target_pairs={{0,8},{8,0},{16,24},{24,16},{1,9},{9,1},{17,25},{25,17},{2,10},{10... | collective-permute-start | bytes 294920 | tf_op jit(solution)/shard_map/ppermute | solution.py:321
  74.7 12.9 %collective-permute-start.13 = (bf16[256,768]{1,0:T(8,128)(2,1)S(1)}, bf16[256,768]{1,0:T(8,128)(2,1)S(1)}, u32[]{:S(2)}, u32[]{:S(2)}) collective-permute-start(bf16[256,768]{1,0:T(8,128)(2,1)S(1)} %pad_maximum_fusion), channel_id=1, source_target_pairs={{0,1},{1,0},{2,3},{3,2},{4,5},{5,4},{6,7},{7,6},{8,9},{9,8},{10,11... | collective-permute-start | bytes 1179656 | tf_op jit(solution)/shard_map/ppermute | solution.py:318
  80.0 3.6 %copy-start.3 = (s32[8]{0:T(128)S(1)}, s32[8]{0:T(128)}, u32[]{:S(2)}) copy-start(s32[8]{0:T(128)} %constant.12.clone) | copy-start | bytes 100
  80.0 5.6 %collective-permute-start.20 = (bf16[64,768]{1,0:T(8,128)(2,1)S(1)}, bf16[64,768]{1,0:T(8,128)(2,1)S(1)}, u32[]{:S(2)}, u32[]{:S(2)}) collective-permute-start(bf16[64,768]{1,0:T(8,128)(2,1)S(1)} %shard_map.65.refs_0_), channel_id=1, source_target_pairs={{0,2},{1,3},{2,0},{3,1},{4,6},{5,7},{6,4},{7,5},{8,10},{9,11},{10,... | collective-permute-start | bytes 294920 | tf_op jit(solution)/shard_map/ppermute | solution.py:318
  80.8 4.9 %collective-permute-start.21 = (bf16[64,768]{1,0:T(8,128)(2,1)S(1)}, bf16[64,768]{1,0:T(8,128)(2,1)S(1)}, u32[]{:S(2)}, u32[]{:S(2)}) collective-permute-start(bf16[64,768]{1,0:T(8,128)(2,1)S(1)} %shard_map.65.refs_0_), channel_id=1, source_target_pairs={{0,4},{1,5},{2,6},{3,7},{4,0},{5,1},{6,2},{7,3},{8,12},{9,13},{10,... | collective-permute-start | bytes 294920 | tf_op jit(solution)/shard_map/ppermute | solution.py:318
  82.0 5.5 %collective-permute-start.22 = (bf16[64,768]{1,0:T(8,128)(2,1)S(1)}, bf16[64,768]{1,0:T(8,128)(2,1)S(1)}, u32[]{:S(2)}, u32[]{:S(2)}) collective-permute-start(bf16[64,768]{1,0:T(8,128)(2,1)S(1)} %shard_map.65.refs_0_), channel_id=1, source_target_pairs={{0,6},{1,7},{2,4},{3,5},{4,2},{5,3},{6,0},{7,1},{8,14},{9,15},{10,... | collective-permute-start | bytes 294920 | tf_op jit(solution)/shard_map/ppermute | solution.py:318
  83.6 5.2 %collective-permute-start.23 = (bf16[64,768]{1,0:T(8,128)(2,1)S(1)}, bf16[64,768]{1,0:T(8,128)(2,1)S(1)}, u32[]{:S(2)}, u32[]{:S(2)}) collective-permute-start(bf16[64,768]{1,0:T(8,128)(2,1)S(1)} %shard_map.65.refs_0_), channel_id=1, source_target_pairs={{0,1},{1,0},{2,3},{3,2},{4,5},{5,4},{6,7},{7,6},{8,9},{9,8},{10,11... | collective-permute-start | bytes 294920 | tf_op jit(solution)/shard_map/ppermute | solution.py:318
  85.6 3.2 %collective-permute-start.24 = (bf16[64,768]{1,0:T(8,128)(2,1)S(1)}, bf16[64,768]{1,0:T(8,128)(2,1)S(1)}, u32[]{:S(2)}, u32[]{:S(2)}) collective-permute-start(bf16[64,768]{1,0:T(8,128)(2,1)S(1)} %collective-permute-done.20.refs_1_), channel_id=1, source_target_pairs={{0,1},{1,0},{2,3},{3,2},{4,5},{5,4},{6,7},{7,6},{8,9},{9,8},{10,11... | collective-permute-start | bytes 294920 | tf_op jit(solution)/shard_map/ppermute | solution.py:318
  85.7 3.1 %collective-permute-start.25 = (bf16[64,768]{1,0:T(8,128)(2,1)S(1)}, bf16[64,768]{1,0:T(8,128)(2,1)S(1)}, u32[]{:S(2)}, u32[]{:S(2)}) collective-permute-start(bf16[64,768]{1,0:T(8,128)(2,1)S(1)} %collective-permute-done.21.refs_2_), channel_id=1, source_target_pairs={{0,1},{1,0},{2,3},{3,2},{4,5},{5,4},{6,7},{7,6},{8,9},{9,8},{10,11... | collective-permute-start | bytes 294920 | tf_op jit(solution)/shard_map/ppermute | solution.py:318
  87.6 1.3 %collective-permute-start.26 = (bf16[64,768]{1,0:T(8,128)(2,1)S(1)}, bf16[64,768]{1,0:T(8,128)(2,1)S(1)}, u32[]{:S(2)}, u32[]{:S(2)}) collective-permute-start(bf16[64,768]{1,0:T(8,128)(2,1)S(1)} %collective-permute-done.22.refs_3_), channel_id=1, source_target_pairs={{0,1},{1,0},{2,3},{3,2},{4,5},{5,4},{6,7},{7,6},{8,9},{9,8},{10,11... | collective-permute-start | bytes 294920 | tf_op jit(solution)/shard_map/ppermute | solution.py:318
where the time goes:
time: 91.1 us; the launch traced here: 90.8 us
  Pallas kernels  36 us (40%)
  starting transfers between devices  33.2 us (36%)
  waiting for transfers between devices  19.8 us (22%)
  local copies, waits for them, and re-layouts  1.6 us (2%)
    ppermute x12, starting transfers between devices, over_batch(): return lax.ppermute(x, 'batch', [(i, i ^ k) for i in range(n_batch)])  21 us
    pallas_call x2, Pallas kernels, experts(): pl.pallas_call(functools.partial(expert_kernel, len(xs), count, rows // c...  12.4 us
    ppermute x15, starting transfers between devices, over_token(): return lax.ppermute(x, 'token', [(i, i ^ k) for i in range(n_token)])  12.2 us
    pallas_call x11, Pallas kernels, call(): pl.pallas_call(kernel, out_shape=[pltpu.VMEM(shape, dtype) for shape in s...  11.6 us
    ppermute x15, waiting for transfers between devices, over_token(): return lax.ppermute(x, 'token', [(i, i ^ k) for i in range(n_token)])  10.3 us
    pallas_call x2, Pallas kernels, load(): pl.pallas_call(functools.partial(load_kernel, parts), out_shape=[pltpu.VM...  10.1 us
    ppermute x12, waiting for transfers between devices, over_batch(): return lax.ppermute(x, 'batch', [(i, i ^ k) for i in range(n_batch)])  9.47 us
    pallas_call x1, Pallas kernels, last_mix(): pl.pallas_call(functools.partial(last_mix_kernel, steps), out_shape=jax.S...  1.94 us
  transfers between devices with their start and end apart: 27, of which 11 were waited for; matrix products, arithmetic and copies ran while one was open for 0% of the time, Pallas kernels for 28%

commit v1 on v0

--- a/solution.py
+++ b/solution.py
@@ -10,8 +10,9 @@
 
 F32, BF16 = jnp.float32, jnp.bfloat16
 CHUNKS = 2
-SPLIT_SUMS = False
+HINTS = (1e11, 1e11, 1e11, 1e6, 1e6)
 STATS = 8
+EXPERT_HINT = 1e9
 
 
 def in_vmem(x):
@@ -44,15 +45,17 @@
     return call(normalize_kernel, x.shape, [x], moved=4 * x.size)
 
 
-def partial_kernel(slots, first, which_ref, own_ref, other_ref, w_ref, *out_refs):
+def partial_kernel(slots, count, *refs):
+    which_refs, (own_ref, other_ref, w_ref), out_refs = refs[:count], refs[count : count + 3], refs[count + 3 :]
+    span = out_refs[0].shape[0] - STATS
     if len(w_ref.shape) == 2:
-        w = w_ref[:, pl.ds(pl.multiple_of(which_ref[0] * slots, slots), slots)]
+        columns = [
+            w_ref[:, pl.ds(pl.multiple_of(which_refs[n][0] * slots, slots), slots)]
+            for n in range(count)
+        ]
     else:
-        w = w_ref[which_ref[0]]
-    span = out_refs[0].shape[0] - STATS
-    count = span * len(out_refs)
-    if count < slots:
-        w = w[:, first : first + count]
+        columns = [w_ref[which_refs[n][0]] for n in range(count)]
+    w = jnp.concatenate(columns, axis=1)
     own, other = own_ref[...], other_ref[...]
     l0 = jnp.dot(own, w, preferred_element_type=F32)
     l1 = jnp.dot(other, w, preferred_element_type=F32)
@@ -64,7 +67,7 @@
     value = lax.dot_general(e0.astype(BF16), own, dims, preferred_element_type=F32)
     value += lax.dot_general(e1.astype(BF16), other, dims, preferred_element_type=F32)
     high = total.astype(BF16).astype(F32)
-    row = lax.broadcasted_iota(jnp.int32, (STATS, count), 0)
+    row = lax.broadcasted_iota(jnp.int32, (STATS, w.shape[1]), 0)
     stats = jnp.where(row == 0, top, jnp.where(row == 1, high, total - high)).astype(BF16)
     value = value.astype(BF16)
     for n, out_ref in enumerate(out_refs):
@@ -74,14 +77,16 @@
         out_ref[span:, :span] = stats[:, part]
 
 
-def partial(which, own, other, weight, slots, first, spans):
+def partial(which, own, other, weight, slots, chunks, hint):
     rows, width = own.shape
     return call(
-        functools.partial(partial_kernel, slots, first),
-        [(span + STATS, width) for span in spans],
-        [which, own, other, weight],
+        functools.partial(partial_kernel, slots, len(which)),
+        [(slots // chunks + STATS, width)] * (len(which) * chunks),
+        [*which, own, other, weight],
         moved=4 * rows * width,
-        scalars=1,
+        scalars=len(which),
+        hint=hint,
+        limit=(2 + 5 * max(1, len(which) * slots // 128)) << 20,
     )
 
 
@@ -116,6 +121,7 @@
         [(slots // chunks, width)] * chunks,
         parts,
         moved=2 * len(parts) * slots * width,
+        hint=HINTS[4],
     )
 
 
@@ -143,91 +149,34 @@
         [(rows, slots // chunks)] * chunks,
         [x, weight],
         moved=2 * (rows * width + width * slots + rows * slots),
-    )
-
-
-def in_hbm(x):
-    return pltpu.with_memory_space_constraint(x, pltpu.HBM)
-
-
-def load_kernel(parts, *refs):
-    n = len(parts)
-    copies = []
-    for i, (first, count) in enumerate(parts):
-        copies.append(
-            pltpu.make_async_copy(refs[i].at[pl.ds(first, count)], refs[n + i], refs[2 * n].at[i])
-        )
-        copies[-1].start()
-    for copy in copies:
-        copy.wait()
-
-
-def load(weights, parts):
-    return pl.pallas_call(
-        functools.partial(load_kernel, parts),
-        out_shape=[
-            pltpu.VMEM((count,) + w.shape[1:], BF16) for w, (_, count) in zip(weights, parts)
-        ],
-        in_specs=[pl.BlockSpec(memory_space=pl.ANY)] * len(parts),
-        out_specs=[pl.BlockSpec(memory_space=pltpu.VMEM)] * len(parts),
-        scratch_shapes=[pltpu.SemaphoreType.DMA((len(parts),))],
-        cost_estimate=pl.CostEstimate(flops=int(1e9), bytes_accessed=1, transcendentals=0),
-        compiler_params=pltpu.CompilerParams(vmem_limit_bytes=1 << 20),
-        name="load",
-    )(*[in_hbm(w) for w in weights])
-
-
-def expert_kernel(count, n, each, first, *refs):
-    xs, w_in, w_out = refs[:count], refs[count], refs[count + 1]
-    if first is None:
-        ys = refs[-count:]
-        fetch = lambda e: []
-    else:
-        far_out = w_out
-        w_out, sems = refs[-2:]
-        ys = refs[-count - 2 : -2]
-
-        def fetch(e):
-            return [pltpu.make_async_copy(far_out.at[first + e], w_out.at[e], sems.at[e])]
-
-        for e in range(n):
-            for copy in fetch(e):
-                copy.start()
+        hint=HINTS[3],
+    )
+
+
+def expert_kernel(count, first, n, each, *refs):
+    xs, w_in, w_out, ys = refs[:count], refs[count], refs[count + 1], refs[count + 2 :]
 
     @pl.loop(0, n)
     def _(e):
         at = pl.ds(pl.multiple_of(e * each, each), each)
         rows = jnp.concatenate([x[at, :] for x in xs], axis=0)
-        hidden = jnp.dot(rows, w_in[e], preferred_element_type=F32)
+        hidden = jnp.dot(rows, w_in[first + e], preferred_element_type=F32)
         hidden = (0.5 * hidden * (1.0 + lax.erf(hidden * 0.7071067811865476))).astype(BF16)
-        for copy in fetch(e):
-            copy.wait()
-        terms = jnp.dot(hidden, w_out[e], preferred_element_type=F32)
+        terms = jnp.dot(hidden, w_out[first + e], preferred_element_type=F32)
         for k, y in enumerate(ys):
             y[at, :] = terms[k * each : (k + 1) * each].astype(BF16)
 
 
 def experts(xs, w_in, w_out, first, count):
     rows, width = xs[0].shape
-    hidden = w_in.shape[2]
-    near = pl.BlockSpec(memory_space=pltpu.VMEM)
-    far = first is not None
-    scratch = [
-        pltpu.VMEM((count, hidden, width), BF16),
-        pltpu.SemaphoreType.DMA((count,)),
-    ]
-    return pl.pallas_call(
-        functools.partial(expert_kernel, len(xs), count, rows // count, first),
-        out_shape=[pltpu.VMEM((rows, width), BF16)] * len(xs),
-        in_specs=[near] * (len(xs) + 1) + [pl.BlockSpec(memory_space=pl.ANY) if far else near],
-        out_specs=[near] * len(xs),
-        scratch_shapes=scratch if far else [],
-        cost_estimate=pl.CostEstimate(flops=int(1e9), bytes_accessed=1, transcendentals=0),
-        compiler_params=pltpu.CompilerParams(
-            vmem_limit_bytes=(4 << 20) + (2 * count * width * hidden if far else 0)
-        ),
-        name="experts",
-    )(*[in_vmem(x) for x in xs], in_vmem(w_in), in_hbm(w_out) if far else in_vmem(w_out))
+    return call(
+        functools.partial(expert_kernel, len(xs), first, count, rows // count),
+        [(rows, width)] * len(xs),
+        [*xs, w_in, w_out],
+        moved=1,
+        hint=EXPERT_HINT,
+        limit=4 << 20,
+    )
 
 
 def total_kernel(count, *refs):
@@ -326,44 +275,43 @@
         weight = slot_weight.reshape(width, n_token, slots).transpose(1, 0, 2)
     else:
         weight = slot_weight
-    here, there = (0, chunk_experts), (chunk_experts, chunk_experts)
-    (in0,) = load([expert_in], [here])
-    out0, in1 = load([expert_out, expert_in], [here, there])
-    ins = [in0, in1]
-    groups = [[c] for c in range(CHUNKS)] if SPLIT_SUMS else [list(range(CHUNKS))]
+    away = list(reversed(range(1, chips)))
+    made = [[] for _ in range(CHUNKS)]
+    for n, ks in enumerate((away[:1], away[1:], [0])):
+        which = [jnp.bitwise_xor(me, 2 * k).astype(jnp.int32)[None] for k in ks]
+        results = partial(which, own, other, weight, slots, CHUNKS, HINTS[n])
+        for c in range(CHUNKS):
+            made[c] += [(k, results[i * CHUNKS + c]) for i, k in enumerate(ks)]
     inputs = []
-    for group in groups:
-        arrived = []
-        count = span * len(group)
-        for k in reversed(range(chips)):
-            which = jnp.bitwise_xor(me, 2 * k).astype(jnp.int32)[None]
-            (sent,) = partial(which, own, other, weight, slots, group[0] * span, [count])
-            arrived.append(over_token(sent, 2 * k) if k else sent)
-        inputs += combine(arrived, count, len(group))
+    for c in range(CHUNKS):
+        arrived = [over_token(x, 2 * k) if k else x for k, x in made[c]]
+        inputs += combine(arrived, span, 1)
     weights = softmax(own, slot_weight, span, CHUNKS)
 
     order = [2 * k for k in range(chips)] + [2 * k + 1 for k in range(chips)]
     at = jnp.bitwise_xor(me, jnp.array(order, jnp.int32))
     xs = []
     for x in inputs:
-        xs.append([over_batch(x, k) if k else x for k in reversed(range(n_batch))])
-    parts = []
+        held = {0: x}
+        bit = n_batch // 2
+        while bit:
+            for k in list(held):
+                held[k ^ bit] = over_batch(held[k], bit)
+            bit //= 2
+        xs.append([held[k] for k in range(n_batch)])
+    keys = list(range(n_batch))
+    total, parts = None, []
     for c in range(CHUNKS):
-        far = c * chunk_experts if c else None
-        ys = experts(xs[c], ins[c], expert_out if c else out0, far, chunk_experts)
-        parts.append([over_batch(y, k) if k else y for k, y in zip(reversed(range(n_batch)), ys)])
-    total = None
+        ys = experts(xs[c], expert_in, expert_out, c * chunk_experts, chunk_experts)
+        parts.append([over_batch(ys[k], k) if k else ys[k] for k in reversed(keys)])
     for c in range(CHUNKS):
         rows = add_up(parts[c])
         there = [over_token(rows, 2 * k) if k else rows for k in range(chips)]
+        swapped = [over_token(there[0], 1)]
+        swapped += [over_token(r, 1) for r in there[1:]]
+        blocks = there + swapped
         if c < CHUNKS - 1:
-            swapped = over_token(jnp.concatenate(there, axis=0), 1)
-            blocks = there + [swapped[k * span : (k + 1) * span] for k in range(chips)]
             total = first_mix(at, weights[c], blocks)
-        else:
-            last = [over_token(there[0], 1)]
-            last += [over_token(r, 1) for r in there[1:]]
-            blocks = there + last
     return last_mix(at, weights[-1], total, blocks)
 
 

time: 91.1 us -> 66.4 us (0.73)
  Pallas kernels: 36 us -> 19.4 us
  waiting for transfers between devices: 19.8 us -> 7.11 us
  starting transfers between devices: 33.2 us -> 38 us
    pallas_call x4 -> x0, Pallas kernels: 22.5 us -> none  [the longest x2 12.4 us: experts(): pl.pallas_call(functools.partial(expert_kernel, len(xs), count, rows // c...]
    ppermute x12, waiting for transfers between devices: 9.47 us -> 2.76 us  [over_batch(): return lax.ppermute(x, 'batch', [(i, i ^ k) for i in range(n_batch)])]
    ppermute x15 -> x21, starting transfers between devices: 12.2 us -> 18.6 us  [over_token(): return lax.ppermute(x, 'token', [(i, i ^ k) for i in range(n_token)])]
    ppermute x15 -> x21, waiting for transfers between devices: 10.3 us -> 4.34 us  [over_token(): return lax.ppermute(x, 'token', [(i, i ^ k) for i in range(n_token)])]
    pallas_call x11 -> x13, Pallas kernels: 11.6 us -> 17.5 us  [call(): pl.pallas_call(kernel, out_shape=[pltpu.VMEM(shape, dtype) for shape in s...]
    ppermute x12, starting transfers between devices: 21 us -> 19.3 us  [over_batch(): return lax.ppermute(x, 'batch', [(i, i ^ k) for i in range(n_batch)])]
  transfers between devices with their start and end apart: 27 -> 33, of which waited for: 11 -> 8; matrix products, arithmetic and copies ran while one was open for 0% -> 0% of each run, Pallas kernels for 28% -> 24%
where the time goes in v1:
time: 66.4 us; the launch traced here: 66.3 us
  starting transfers between devices  38 us (57%)
  Pallas kernels  19.4 us (29%)
  waiting for transfers between devices  7.11 us (11%)
  local copies, waits for them, and re-layouts  1.58 us (2%)
    ppermute x12, starting transfers between devices, over_batch(): return lax.ppermute(x, 'batch', [(i, i ^ k) for i in range(n_batch)])  19.3 us
    ppermute x21, starting transfers between devices, over_token(): return lax.ppermute(x, 'token', [(i, i ^ k) for i in range(n_token)])  18.6 us
    pallas_call x13, Pallas kernels, call(): pl.pallas_call(kernel, out_shape=[pltpu.VMEM(shape, dtype) for shape in s...  17.5 us
    ppermute x21, waiting for transfers between devices, over_token(): return lax.ppermute(x, 'token', [(i, i ^ k) for i in range(n_token)])  4.34 us
    ppermute x12, waiting for transfers between devices, over_batch(): return lax.ppermute(x, 'batch', [(i, i ^ k) for i in range(n_batch)])  2.76 us
    pallas_call x1, Pallas kernels, last_mix(): pl.pallas_call(functools.partial(last_mix_kernel, steps), out_shape=jax.S...  1.93 us
    unnamed x10, local copies, waits for them, and re-layouts  1.58 us
  transfers between devices with their start and end apart: 33, of which 8 were waited for; matrix products, arithmetic and copies ran while one was open for 0% of the time, Pallas kernels for 24%

profile of v1, /device:TPU:0, one launch (start us, length us, event | category | flops | bytes accessed | tf_op | source)
XLA Modules:
  0.0 66.3 jit_solution(2798651674731078274)
XLA Ops:
  0.0 0.5 collective-permute-start
  0.5 1.1 %copy-done.3 = bf16[512,768]{1,0:T(8,128)(2,1)S(1)} copy-done((bf16[512,768]{1,0:T(8,128)(2,1)S(1)}, bf16[512,768]{1,0:T(8,128)(2,1)}, u32[]{:S(2)}) %copy-start.3) | copy-done | bytes 786456
  1.6 0.2 shard_map.55.x_ref.refs_1_.refs_2_
  1.9 0.0 copy-start.2
  1.9 0.7 %collective-permute-done.x_ref = bf16[512,768]{1,0:T(8,128)(2,1)S(1)} collective-permute-done((bf16[512,768]{1,0:T(8,128)(2,1)}, bf16[512,768]{1,0:T(8,128)(2,1)S(1)}, u32[]{:S(2)}, u32[]{:S(2)}) %collective-permute-start) | collective-permute-done | bytes 786464 | tf_op jit(solution)/shard_map/ppermute | solution.py:267
  2.6 0.2 shard_map.57.refs_2_.refs_3_
  2.9 0.4 copy-done.2
  3.3 1.2 %shard_map.58 = (bf16[72,768]{1,0:T(8,128)(2,1)S(1)}, bf16[72,768]{1,0:T(8,128)(2,1)S(1)}) custom-call(s32[1]{0:T(128)} %bitcast.refs_0_, bf16[512,768]{1,0:T(8,128)(2,1)S(1)} %shard_map.55.x_ref.refs_1_.refs_2_, bf16[512,768]{1,0:T(8,128)(2,1)S(1)} %shard_map.57.refs_2_.refs_3_, bf16[768,1024]{1,0:T(8,128)(2,1)S(1)} %copy-done.2), custom_call_target="tpu_custom_call" | custom-call | flops 99999997952 | bytes 1572864 | tf_op jit(solution)/shard_map/pallas_call | solution.py:26
  4.5 3.5 %collective-permute-start.1 = (bf16[72,768]{1,0:T(8,128)(2,1)S(1)}, bf16[72,768]{1,0:T(8,128)(2,1)S(1)}, u32[]{:S(2)}, u32[]{:S(2)}) collective-permute-start(bf16[72,768]{1,0:T(8,128)(2,1)S(1)} %get-tuple-element.25), channel_id=1, source_target_pairs={{0,6},{1,7},{2,4},{3,5},{4,2},{5,3},{6,0},{7,1},{8,14},{9,15},{10,... | collective-permute-start | bytes 331784 | tf_op jit(solution)/shard_map/ppermute | solution.py:267
  8.0 1.6 %shard_map.59 = (bf16[72,768]{1,0:T(8,128)(2,1)S(1)}, bf16[72,768]{1,0:T(8,128)(2,1)S(1)}, bf16[72,768]{1,0:T(8,128)(2,1)S(1)}, bf16[72,768]{1,0:T(8,128)(2,1)S(1)}) custom-call(s32[1]{0:T(128)} %bitcast.1.refs_0_, s32[1]{0:T(128)} %bitcast.2.refs_1_, bf16[512,768]{1,0:T(8,128)(2,1)S(1)} %shard_map.55.x_ref.refs_1_.refs_2_, ...), custom_call_target="tpu_custom_call" | custom-call | flops 99999997952 | bytes 1572864 | tf_op jit(solution)/shard_map/pallas_call | solution.py:26
  9.6 0.6 collective-permute-start.2
  10.2 0.1 collective-permute-start.3
  10.3 2.9 %collective-permute-start.17 = (bf16[72,768]{1,0:T(8,128)(2,1)S(1)}, bf16[72,768]{1,0:T(8,128)(2,1)S(1)}, u32[]{:S(2)}, u32[]{:S(2)}) collective-permute-start(bf16[72,768]{1,0:T(8,128)(2,1)S(1)} %get-tuple-element.33), channel_id=1, source_target_pairs={{0,6},{1,7},{2,4},{3,5},{4,2},{5,3},{6,0},{7,1},{8,14},{9,15},{10,... | collective-permute-start | bytes 331784 | tf_op jit(solution)/shard_map/ppermute | solution.py:267
  13.1 0.5 collective-permute-start.18
  13.7 0.0 collective-permute-done.1.refs_0_
  13.7 0.1 collective-permute-start.19
  13.8 1.2 %shard_map.60 = (bf16[72,768]{1,0:T(8,128)(2,1)S(1)}, bf16[72,768]{1,0:T(8,128)(2,1)S(1)}) custom-call(s32[1]{0:T(128)} %bitcast.3.refs_0_, bf16[512,768]{1,0:T(8,128)(2,1)S(1)} %shard_map.55.x_ref.refs_1_.refs_2_, bf16[512,768]{1,0:T(8,128)(2,1)S(1)} %shard_map.57.refs_2_.refs_3_, bf16[768,1024]{1,0:T(8,128)(2,1)S(1)} %copy-done.2), custom_call_target="tpu_custom_call" | custom-call | flops 99999997952 | bytes 1572864 | tf_op jit(solution)/shard_map/pallas_call | solution.py:26
  15.0 0.0 collective-permute-done.2.refs_1_
  15.0 1.1 %collective-permute-done.3.refs_2_ = bf16[72,768]{1,0:T(8,128)(2,1)S(1)} collective-permute-done((bf16[72,768]{1,0:T(8,128)(2,1)S(1)}, bf16[72,768]{1,0:T(8,128)(2,1)S(1)}, u32[]{:S(2)}, u32[]{:S(2)}) %collective-permute-start.3) | collective-permute-done | bytes 110624 | tf_op jit(solution)/shard_map/ppermute | solution.py:267
  16.1 0.2 shard_map.61.refs_0_
  16.3 2.6 %collective-permute-start.5 = (bf16[64,768]{1,0:T(8,128)(2,1)S(1)}, bf16[64,768]{1,0:T(8,128)(2,1)S(1)}, u32[]{:S(2)}, u32[]{:S(2)}) collective-permute-start(bf16[64,768]{1,0:T(8,128)(2,1)S(1)} %shard_map.61.refs_0_), channel_id=1, source_target_pairs={{0,16},{8,24},{16,0},{24,8},{1,17},{9,25},{17,1},{25,9},{2,18},{10... | collective-permute-start | bytes 294920 | tf_op jit(solution)/shard_map/ppermute | solution.py:270
  18.9 0.5 collective-permute-done.17.refs_0_
  19.4 0.4 collective-permute-done.18.refs_1_
  19.8 0.0 collective-permute-done.19.refs_2_
  19.8 0.2 shard_map.65.refs_0_
  20.0 2.7 %collective-permute-start.21 = (bf16[64,768]{1,0:T(8,128)(2,1)S(1)}, bf16[64,768]{1,0:T(8,128)(2,1)S(1)}, u32[]{:S(2)}, u32[]{:S(2)}) collective-permute-start(bf16[64,768]{1,0:T(8,128)(2,1)S(1)} %shard_map.65.refs_0_), channel_id=1, source_target_pairs={{0,16},{8,24},{16,0},{24,8},{1,17},{9,25},{17,1},{25,9},{2,18},{10... | collective-permute-start | bytes 294920 | tf_op jit(solution)/shard_map/ppermute | solution.py:270
  22.7 1.6 %collective-permute-start.4 = (bf16[64,768]{1,0:T(8,128)(2,1)S(1)}, bf16[64,768]{1,0:T(8,128)(2,1)S(1)}, u32[]{:S(2)}, u32[]{:S(2)}) collective-permute-start(bf16[64,768]{1,0:T(8,128)(2,1)S(1)} %shard_map.61.refs_0_), channel_id=1, source_target_pairs={{0,8},{8,0},{16,24},{24,16},{1,9},{9,1},{17,25},{25,17},{2,10},{10... | collective-permute-start | bytes 294920 | tf_op jit(solution)/shard_map/ppermute | solution.py:270
  24.2 0.5 collective-permute-start.6
  24.7 1.6 %collective-permute-start.20 = (bf16[64,768]{1,0:T(8,128)(2,1)S(1)}, bf16[64,768]{1,0:T(8,128)(2,1)S(1)}, u32[]{:S(2)}, u32[]{:S(2)}) collective-permute-start(bf16[64,768]{1,0:T(8,128)(2,1)S(1)} %shard_map.65.refs_0_), channel_id=1, source_target_pairs={{0,8},{8,0},{16,24},{24,16},{1,9},{9,1},{17,25},{25,17},{2,10},{10... | collective-permute-start | bytes 294920 | tf_op jit(solution)/shard_map/ppermute | solution.py:270
  26.3 0.3 collective-permute-done.21.refs_2_
  26.6 1.6 %collective-permute-start.22 = (bf16[64,768]{1,0:T(8,128)(2,1)S(1)}, bf16[64,768]{1,0:T(8,128)(2,1)S(1)}, u32[]{:S(2)}, u32[]{:S(2)}) collective-permute-start(bf16[64,768]{1,0:T(8,128)(2,1)S(1)} %collective-permute-done.21.refs_2_), channel_id=1, source_target_pairs={{0,8},{8,0},{16,24},{24,16},{1,9},{9,1},{17,25},{25,17},{2,10},{10... | collective-permute-start | bytes 294920 | tf_op jit(solution)/shard_map/ppermute | solution.py:270
  28.2 0.3 collective-permute-done.4.refs_1_
  28.5 2.1 %collective-permute-done.6.refs_3_ = bf16[64,768]{1,0:T(8,128)(2,1)S(1)} collective-permute-done((bf16[64,768]{1,0:T(8,128)(2,1)S(1)}, bf16[64,768]{1,0:T(8,128)(2,1)S(1)}, u32[]{:S(2)}, u32[]{:S(2)}) %collective-permute-start.6) | collective-permute-done | bytes 98336 | tf_op jit(solution)/shard_map/ppermute | solution.py:270
  30.6 4.8 %shard_map.62 = (bf16[64,768]{1,0:T(8,128)(2,1)S(1)}, bf16[64,768]{1,0:T(8,128)(2,1)S(1)}, bf16[64,768]{1,0:T(8,128)(2,1)S(1)}, bf16[64,768]{1,0:T(8,128)(2,1)S(1)}) custom-call(bf16[64,768]{1,0:T(8,128)(2,1)S(1)} %shard_map.61.refs_0_, bf16[64,768]{1,0:T(8,128)(2,1)S(1)} %collective-permute-done.4.refs_1_, ...), custom_call_target="tpu_custom_call" | custom-call | flops 1000000000 | bytes 1 | tf_op jit(solution)/shard_map/pallas_call | solution.py:26
  35.4 3.3 %collective-permute-start.7 = (bf16[64,768]{1,0:T(8,128)(2,1)S(1)}, bf16[64,768]{1,0:T(8,128)(2,1)S(1)}, u32[]{:S(2)}, u32[]{:S(2)}) collective-permute-start(bf16[64,768]{1,0:T(8,128)(2,1)S(1)} %get-tuple-element.29), channel_id=1, source_target_pairs={{0,24},{8,16},{16,8},{24,0},{1,25},{9,17},{17,9},{25,1},{2,26},{10... | collective-permute-start | bytes 294920 | tf_op jit(solution)/shard_map/ppermute | solution.py:270
  38.6 0.2 collective-permute-start.8
  38.8 1.0 %collective-permute-start.9 = (bf16[64,768]{1,0:T(8,128)(2,1)S(1)}, bf16[64,768]{1,0:T(8,128)(2,1)S(1)}, u32[]{:S(2)}, u32[]{:S(2)}) collective-permute-start(bf16[64,768]{1,0:T(8,128)(2,1)S(1)} %get-tuple-element.31), channel_id=1, source_target_pairs={{0,8},{8,0},{16,24},{24,16},{1,9},{9,1},{17,25},{25,17},{2,10},{10... | collective-permute-start | bytes 294920 | tf_op jit(solution)/shard_map/ppermute | solution.py:270
  39.8 0.0 collective-permute-done.20.refs_1_
  39.8 4.8 %shard_map.66 = (bf16[64,768]{1,0:T(8,128)(2,1)S(1)}, bf16[64,768]{1,0:T(8,128)(2,1)S(1)}, bf16[64,768]{1,0:T(8,128)(2,1)S(1)}, bf16[64,768]{1,0:T(8,128)(2,1)S(1)}) custom-call(bf16[64,768]{1,0:T(8,128)(2,1)S(1)} %shard_map.65.refs_0_, bf16[64,768]{1,0:T(8,128)(2,1)S(1)} %collective-permute-done.20.refs_1_, ...), custom_call_target="tpu_custom_call" | custom-call | flops 1000000000 | bytes 1 | tf_op jit(solution)/shard_map/pallas_call | solution.py:26
  44.6 3.3 %collective-permute-start.23 = (bf16[64,768]{1,0:T(8,128)(2,1)S(1)}, bf16[64,768]{1,0:T(8,128)(2,1)S(1)}, u32[]{:S(2)}, u32[]{:S(2)}) collective-permute-start(bf16[64,768]{1,0:T(8,128)(2,1)S(1)} %get-tuple-element.37), channel_id=1, source_target_pairs={{0,24},{8,16},{16,8},{24,0},{1,25},{9,17},{17,9},{25,1},{2,26},{10... | collective-permute-start | bytes 294920 | tf_op jit(solution)/shard_map/ppermute | solution.py:270
  47.8 0.0 collective-permute-start.24
  47.8 0.0 collective-permute-done.7.refs_0_
  47.8 1.1 %collective-permute-start.25 = (bf16[64,768]{1,0:T(8,128)(2,1)S(1)}, bf16[64,768]{1,0:T(8,128)(2,1)S(1)}, u32[]{:S(2)}, u32[]{:S(2)}) collective-permute-start(bf16[64,768]{1,0:T(8,128)(2,1)S(1)} %get-tuple-element.39), channel_id=1, source_target_pairs={{0,8},{8,0},{16,24},{24,16},{1,9},{9,1},{17,25},{25,17},{2,10},{10... | collective-permute-start | bytes 294920 | tf_op jit(solution)/shard_map/ppermute | solution.py:270
  49.0 0.0 collective-permute-done.8.refs_1_
  49.0 0.0 collective-permute-done.9.refs_2_
  49.0 0.1 shard_map.63.refs_0_
  49.0 0.8 %collective-permute-start.10 = (bf16[64,768]{1,0:T(8,128)(2,1)S(1)}, bf16[64,768]{1,0:T(8,128)(2,1)S(1)}, u32[]{:S(2)}, u32[]{:S(2)}) collective-permute-start(bf16[64,768]{1,0:T(8,128)(2,1)S(1)} %shard_map.63.refs_0_), channel_id=1, source_target_pairs={{0,2},{1,3},{2,0},{3,1},{4,6},{5,7},{6,4},{7,5},{8,10},{9,11},{10,... | collective-permute-start | bytes 294920 | tf_op jit(solution)/shard_map/ppermute | solution.py:267
  49.9 2.1 %collective-permute-start.11 = (bf16[64,768]{1,0:T(8,128)(2,1)S(1)}, bf16[64,768]{1,0:T(8,128)(2,1)S(1)}, u32[]{:S(2)}, u32[]{:S(2)}) collective-permute-start(bf16[64,768]{1,0:T(8,128)(2,1)S(1)} %shard_map.63.refs_0_), channel_id=1, source_target_pairs={{0,4},{1,5},{2,6},{3,7},{4,0},{5,1},{6,2},{7,3},{8,12},{9,13},{10,... | collective-permute-start | bytes 294920 | tf_op jit(solution)/shard_map/ppermute | solution.py:267
  51.9 2.3 %collective-permute-start.12 = (bf16[64,768]{1,0:T(8,128)(2,1)S(1)}, bf16[64,768]{1,0:T(8,128)(2,1)S(1)}, u32[]{:S(2)}, u32[]{:S(2)}) collective-permute-start(bf16[64,768]{1,0:T(8,128)(2,1)S(1)} %shard_map.63.refs_0_), channel_id=1, source_target_pairs={{0,6},{1,7},{2,4},{3,5},{4,2},{5,3},{6,0},{7,1},{8,14},{9,15},{10,... | collective-permute-start | bytes 294920 | tf_op jit(solution)/shard_map/ppermute | solution.py:267
  54.3 0.0 copy-start.4
  54.3 0.1 shard_map.67.refs_0_
  54.3 0.2 collective-permute-start.26
  54.5 2.4 %collective-permute-start.27 = (bf16[64,768]{1,0:T(8,128)(2,1)S(1)}, bf16[64,768]{1,0:T(8,128)(2,1)S(1)}, u32[]{:S(2)}, u32[]{:S(2)}) collective-permute-start(bf16[64,768]{1,0:T(8,128)(2,1)S(1)} %shard_map.67.refs_0_), channel_id=1, source_target_pairs={{0,4},{1,5},{2,6},{3,7},{4,0},{5,1},{6,2},{7,3},{8,12},{9,13},{10,... | collective-permute-start | bytes 294920 | tf_op jit(solution)/shard_map/ppermute | solution.py:267
  56.9 1.0 %collective-permute-start.28 = (bf16[64,768]{1,0:T(8,128)(2,1)S(1)}, bf16[64,768]{1,0:T(8,128)(2,1)S(1)}, u32[]{:S(2)}, u32[]{:S(2)}) collective-permute-start(bf16[64,768]{1,0:T(8,128)(2,1)S(1)} %shard_map.67.refs_0_), channel_id=1, source_target_pairs={{0,6},{1,7},{2,4},{3,5},{4,2},{5,3},{6,0},{7,1},{8,14},{9,15},{10,... | collective-permute-start | bytes 294920 | tf_op jit(solution)/shard_map/ppermute | solution.py:267
  57.9 0.5 collective-permute-start.15
  58.4 1.6 %collective-permute-done.26.refs_1_ = bf16[64,768]{1,0:T(8,128)(2,1)S(1)} collective-permute-done((bf16[64,768]{1,0:T(8,128)(2,1)S(1)}, bf16[64,768]{1,0:T(8,128)(2,1)S(1)}, u32[]{:S(2)}, u32[]{:S(2)}) %collective-permute-start.26) | collective-permute-done | bytes 98336 | tf_op jit(solution)/shard_map/ppermute | solution.py:267
  60.0 1.9 %shard_map.56 = (bf16[512,512]{1,0:T(8,128)(2,1)S(1)}, bf16[512,512]{1,0:T(8,128)(2,1)S(1)}) custom-call(bf16[512,768]{1,0:T(8,128)(2,1)S(1)} %shard_map.55.x_ref.refs_1_.refs_2_, bf16[768,1024]{1,0:T(8,128)(2,1)S(1)} %copy-done.2), custom_call_target="tpu_custom_call" | custom-call | flops 1000000 | bytes 3407872 | tf_op jit(solution)/shard_map/pallas_call | solution.py:26
  61.9 0.6 collective-permute-start.29
  62.5 0.1 collective-permute-start.30
  62.6 0.4 collective-permute-start.31
  63.0 0.1 collective-permute-start.32
  63.1 1.2 %shard_map.64.sum_ref = f32[512,768]{1,0:T(8,128)S(1)} custom-call(s32[8]{0:T(128)S(1)} %broadcast_xor_fusion.at_ref, bf16[512,512]{1,0:T(8,128)(2,1)S(1)} %get-tuple-element.24.c_ref, bf16[64,768]{1,0:T(8,128)(2,1)S(1)} %shard_map.63.refs_0_, bf16[64,768]{1,0:T(8,128)(2,1)S(1)} %collective-permute-done.10.refs_1_, ...), custom_call_target="tpu_custom_call" | custom-call | flops 99999997952 | bytes 2097152 | tf_op jit(solution)/shard_map/pallas_call | solution.py:26
  64.3 0.0 collective-permute-done.32.refs_7_
  64.3 1.9 %last_mix.1 = bf16[512,768]{1,0:T(8,128)(2,1)} custom-call(s32[8]{0:T(128)S(1)} %broadcast_xor_fusion.at_ref, bf16[512,512]{1,0:T(8,128)(2,1)S(1)} %get-tuple-element.23.c_ref, f32[512,768]{1,0:T(8,128)S(1)} %shard_map.64.sum_ref, bf16[64,768]{1,0:T(8,128)(2,1)S(1)} %shard_map.67.refs_0_, bf16[64,768]{1,0:T(8,128)(2,1)S(1)} %collective-permute-done.26.refs_1_, ...), custom_call_target="tpu_custom_call" | custom-call | tf_op jit(solution)/shard_map/last_mix/pallas_call | solution.py:242
  (27 shorter events, 0.1 us)
Async XLA Ops:
  0.0 2.6 %collective-permute-start = (bf16[512,768]{1,0:T(8,128)(2,1)}, bf16[512,768]{1,0:T(8,128)(2,1)S(1)}, u32[]{:S(2)}, u32[]{:S(2)}) collective-permute-start(bf16[512,768]{1,0:T(8,128)(2,1)} %x_ref.1), channel_id=1, source_target_pairs={{0,1},{1,0},{2,3},{3,2},{4,5},{5,4},{6,7},{7,6},{8,9},{9,8},{10,11... | collective-permute-start | bytes 2359304 | tf_op jit(solution)/shard_map/ppermute | solution.py:267
  0.5 1.1 %copy-start.3 = (bf16[512,768]{1,0:T(8,128)(2,1)S(1)}, bf16[512,768]{1,0:T(8,128)(2,1)}, u32[]{:S(2)}) copy-start(bf16[512,768]{1,0:T(8,128)(2,1)} %x_ref.1) | copy-start | bytes 2359300
  1.9 1.4 %copy-start.2 = (bf16[768,1024]{1,0:T(8,128)(2,1)S(1)}, bf16[768,1024]{1,0:T(8,128)(2,1)}, u32[]{:S(2)}) copy-start(bf16[768,1024]{1,0:T(8,128)(2,1)} %refs_3_.3) | copy-start | bytes 4718596
  4.5 9.2 %collective-permute-start.1 = (bf16[72,768]{1,0:T(8,128)(2,1)S(1)}, bf16[72,768]{1,0:T(8,128)(2,1)S(1)}, u32[]{:S(2)}, u32[]{:S(2)}) collective-permute-start(bf16[72,768]{1,0:T(8,128)(2,1)S(1)} %get-tuple-element.25), channel_id=1, source_target_pairs={{0,6},{1,7},{2,4},{3,5},{4,2},{5,3},{6,0},{7,1},{8,14},{9,15},{10,... | collective-permute-start | bytes 331784 | tf_op jit(solution)/shard_map/ppermute | solution.py:267
  9.6 5.4 %collective-permute-start.2 = (bf16[72,768]{1,0:T(8,128)(2,1)S(1)}, bf16[72,768]{1,0:T(8,128)(2,1)S(1)}, u32[]{:S(2)}, u32[]{:S(2)}) collective-permute-start(bf16[72,768]{1,0:T(8,128)(2,1)S(1)} %get-tuple-element.26), channel_id=1, source_target_pairs={{0,4},{1,5},{2,6},{3,7},{4,0},{5,1},{6,2},{7,3},{8,12},{9,13},{10,... | collective-permute-start | bytes 331784 | tf_op jit(solution)/shard_map/ppermute | solution.py:267
  10.2 5.9 %collective-permute-start.3 = (bf16[72,768]{1,0:T(8,128)(2,1)S(1)}, bf16[72,768]{1,0:T(8,128)(2,1)S(1)}, u32[]{:S(2)}, u32[]{:S(2)}) collective-permute-start(bf16[72,768]{1,0:T(8,128)(2,1)S(1)} %get-tuple-element.27), channel_id=1, source_target_pairs={{0,2},{1,3},{2,0},{3,1},{4,6},{5,7},{6,4},{7,5},{8,10},{9,11},{10,... | collective-permute-start | bytes 331784 | tf_op jit(solution)/shard_map/ppermute | solution.py:267
  10.3 9.1 %collective-permute-start.17 = (bf16[72,768]{1,0:T(8,128)(2,1)S(1)}, bf16[72,768]{1,0:T(8,128)(2,1)S(1)}, u32[]{:S(2)}, u32[]{:S(2)}) collective-permute-start(bf16[72,768]{1,0:T(8,128)(2,1)S(1)} %get-tuple-element.33), channel_id=1, source_target_pairs={{0,6},{1,7},{2,4},{3,5},{4,2},{5,3},{6,0},{7,1},{8,14},{9,15},{10,... | collective-permute-start | bytes 331784 | tf_op jit(solution)/shard_map/ppermute | solution.py:267
  13.1 6.7 %collective-permute-start.18 = (bf16[72,768]{1,0:T(8,128)(2,1)S(1)}, bf16[72,768]{1,0:T(8,128)(2,1)S(1)}, u32[]{:S(2)}, u32[]{:S(2)}) collective-permute-start(bf16[72,768]{1,0:T(8,128)(2,1)S(1)} %get-tuple-element.34), channel_id=1, source_target_pairs={{0,4},{1,5},{2,6},{3,7},{4,0},{5,1},{6,2},{7,3},{8,12},{9,13},{10,... | collective-permute-start | bytes 331784 | tf_op jit(solution)/shard_map/ppermute | solution.py:267
  13.7 6.2 %collective-permute-start.19 = (bf16[72,768]{1,0:T(8,128)(2,1)S(1)}, bf16[72,768]{1,0:T(8,128)(2,1)S(1)}, u32[]{:S(2)}, u32[]{:S(2)}) collective-permute-start(bf16[72,768]{1,0:T(8,128)(2,1)S(1)} %get-tuple-element.35), channel_id=1, source_target_pairs={{0,2},{1,3},{2,0},{3,1},{4,6},{5,7},{6,4},{7,5},{8,10},{9,11},{10,... | collective-permute-start | bytes 331784 | tf_op jit(solution)/shard_map/ppermute | solution.py:267
  13.8 16.9 %copy-start = (bf16[16,768,768]{2,1,0:T(8,128)(2,1)S(1)}, bf16[16,768,768]{2,1,0:T(8,128)(2,1)}, u32[]{:S(2)}) copy-start(bf16[16,768,768]{2,1,0:T(8,128)(2,1)} %refs_4_.5) | copy-start | bytes 56623108
  13.8 16.9 %copy-start.1 = (bf16[16,768,768]{2,1,0:T(8,128)(2,1)S(1)}, bf16[16,768,768]{2,1,0:T(8,128)(2,1)}, u32[]{:S(2)}) copy-start(bf16[16,768,768]{2,1,0:T(8,128)(2,1)} %refs_5_.3) | copy-start | bytes 56623108
  16.3 8.0 %collective-permute-start.5 = (bf16[64,768]{1,0:T(8,128)(2,1)S(1)}, bf16[64,768]{1,0:T(8,128)(2,1)S(1)}, u32[]{:S(2)}, u32[]{:S(2)}) collective-permute-start(bf16[64,768]{1,0:T(8,128)(2,1)S(1)} %shard_map.61.refs_0_), channel_id=1, source_target_pairs={{0,16},{8,24},{16,0},{24,8},{1,17},{9,25},{17,1},{25,9},{2,18},{10... | collective-permute-start | bytes 294920 | tf_op jit(solution)/shard_map/ppermute | solution.py:270
  20.0 6.6 %collective-permute-start.21 = (bf16[64,768]{1,0:T(8,128)(2,1)S(1)}, bf16[64,768]{1,0:T(8,128)(2,1)S(1)}, u32[]{:S(2)}, u32[]{:S(2)}) collective-permute-start(bf16[64,768]{1,0:T(8,128)(2,1)S(1)} %shard_map.65.refs_0_), channel_id=1, source_target_pairs={{0,16},{8,24},{16,0},{24,8},{1,17},{9,25},{17,1},{25,9},{2,18},{10... | collective-permute-start | bytes 294920 | tf_op jit(solution)/shard_map/ppermute | solution.py:270
  22.7 5.8 %collective-permute-start.4 = (bf16[64,768]{1,0:T(8,128)(2,1)S(1)}, bf16[64,768]{1,0:T(8,128)(2,1)S(1)}, u32[]{:S(2)}, u32[]{:S(2)}) collective-permute-start(bf16[64,768]{1,0:T(8,128)(2,1)S(1)} %shard_map.61.refs_0_), channel_id=1, source_target_pairs={{0,8},{8,0},{16,24},{24,16},{1,9},{9,1},{17,25},{25,17},{2,10},{10... | collective-permute-start | bytes 294920 | tf_op jit(solution)/shard_map/ppermute | solution.py:270
  24.2 6.4 %collective-permute-start.6 = (bf16[64,768]{1,0:T(8,128)(2,1)S(1)}, bf16[64,768]{1,0:T(8,128)(2,1)S(1)}, u32[]{:S(2)}, u32[]{:S(2)}) collective-permute-start(bf16[64,768]{1,0:T(8,128)(2,1)S(1)} %collective-permute-done.5.refs_2_), channel_id=1, source_target_pairs={{0,8},{8,0},{16,24},{24,16},{1,9},{9,1},{17,25},{25,17},{2,10},{10... | collective-permute-start | bytes 294920 | tf_op jit(solution)/shard_map/ppermute | solution.py:270
  24.7 15.1 %collective-permute-start.20 = (bf16[64,768]{1,0:T(8,128)(2,1)S(1)}, bf16[64,768]{1,0:T(8,128)(2,1)S(1)}, u32[]{:S(2)}, u32[]{:S(2)}) collective-permute-start(bf16[64,768]{1,0:T(8,128)(2,1)S(1)} %shard_map.65.refs_0_), channel_id=1, source_target_pairs={{0,8},{8,0},{16,24},{24,16},{1,9},{9,1},{17,25},{25,17},{2,10},{10... | collective-permute-start | bytes 294920 | tf_op jit(solution)/shard_map/ppermute | solution.py:270
  26.6 13.2 %collective-permute-start.22 = (bf16[64,768]{1,0:T(8,128)(2,1)S(1)}, bf16[64,768]{1,0:T(8,128)(2,1)S(1)}, u32[]{:S(2)}, u32[]{:S(2)}) collective-permute-start(bf16[64,768]{1,0:T(8,128)(2,1)S(1)} %collective-permute-done.21.refs_2_), channel_id=1, source_target_pairs={{0,8},{8,0},{16,24},{24,16},{1,9},{9,1},{17,25},{25,17},{2,10},{10... | collective-permute-start | bytes 294920 | tf_op jit(solution)/shard_map/ppermute | solution.py:270
  35.4 12.4 %collective-permute-start.7 = (bf16[64,768]{1,0:T(8,128)(2,1)S(1)}, bf16[64,768]{1,0:T(8,128)(2,1)S(1)}, u32[]{:S(2)}, u32[]{:S(2)}) collective-permute-start(bf16[64,768]{1,0:T(8,128)(2,1)S(1)} %get-tuple-element.29), channel_id=1, source_target_pairs={{0,24},{8,16},{16,8},{24,0},{1,25},{9,17},{17,9},{25,1},{2,26},{10... | collective-permute-start | bytes 294920 | tf_op jit(solution)/shard_map/ppermute | solution.py:270
  38.6 10.3 %collective-permute-start.8 = (bf16[64,768]{1,0:T(8,128)(2,1)S(1)}, bf16[64,768]{1,0:T(8,128)(2,1)S(1)}, u32[]{:S(2)}, u32[]{:S(2)}) collective-permute-start(bf16[64,768]{1,0:T(8,128)(2,1)S(1)} %get-tuple-element.30), channel_id=1, source_target_pairs={{0,16},{8,24},{16,0},{24,8},{1,17},{9,25},{17,1},{25,9},{2,18},{10... | collective-permute-start | bytes 294920 | tf_op jit(solution)/shard_map/ppermute | solution.py:270
  38.8 10.2 %collective-permute-start.9 = (bf16[64,768]{1,0:T(8,128)(2,1)S(1)}, bf16[64,768]{1,0:T(8,128)(2,1)S(1)}, u32[]{:S(2)}, u32[]{:S(2)}) collective-permute-start(bf16[64,768]{1,0:T(8,128)(2,1)S(1)} %get-tuple-element.31), channel_id=1, source_target_pairs={{0,8},{8,0},{16,24},{24,16},{1,9},{9,1},{17,25},{25,17},{2,10},{10... | collective-permute-start | bytes 294920 | tf_op jit(solution)/shard_map/ppermute | solution.py:270
  44.6 7.4 %collective-permute-start.23 = (bf16[64,768]{1,0:T(8,128)(2,1)S(1)}, bf16[64,768]{1,0:T(8,128)(2,1)S(1)}, u32[]{:S(2)}, u32[]{:S(2)}) collective-permute-start(bf16[64,768]{1,0:T(8,128)(2,1)S(1)} %get-tuple-element.37), channel_id=1, source_target_pairs={{0,24},{8,16},{16,8},{24,0},{1,25},{9,17},{17,9},{25,1},{2,26},{10... | collective-permute-start | bytes 294920 | tf_op jit(solution)/shard_map/ppermute | solution.py:270
  47.8 6.4 %collective-permute-start.24 = (bf16[64,768]{1,0:T(8,128)(2,1)S(1)}, bf16[64,768]{1,0:T(8,128)(2,1)S(1)}, u32[]{:S(2)}, u32[]{:S(2)}) collective-permute-start(bf16[64,768]{1,0:T(8,128)(2,1)S(1)} %get-tuple-element.38), channel_id=1, source_target_pairs={{0,16},{8,24},{16,0},{24,8},{1,17},{9,25},{17,1},{25,9},{2,18},{10... | collective-permute-start | bytes 294920 | tf_op jit(solution)/shard_map/ppermute | solution.py:270
  47.8 6.4 %collective-permute-start.25 = (bf16[64,768]{1,0:T(8,128)(2,1)S(1)}, bf16[64,768]{1,0:T(8,128)(2,1)S(1)}, u32[]{:S(2)}, u32[]{:S(2)}) collective-permute-start(bf16[64,768]{1,0:T(8,128)(2,1)S(1)} %get-tuple-element.39), channel_id=1, source_target_pairs={{0,8},{8,0},{16,24},{24,16},{1,9},{9,1},{17,25},{25,17},{2,10},{10... | collective-permute-start | bytes 294920 | tf_op jit(solution)/shard_map/ppermute | solution.py:270
  49.0 5.5 %collective-permute-start.10 = (bf16[64,768]{1,0:T(8,128)(2,1)S(1)}, bf16[64,768]{1,0:T(8,128)(2,1)S(1)}, u32[]{:S(2)}, u32[]{:S(2)}) collective-permute-start(bf16[64,768]{1,0:T(8,128)(2,1)S(1)} %shard_map.63.refs_0_), channel_id=1, source_target_pairs={{0,2},{1,3},{2,0},{3,1},{4,6},{5,7},{6,4},{7,5},{8,10},{9,11},{10,... | collective-permute-start | bytes 294920 | tf_op jit(solution)/shard_map/ppermute | solution.py:267
  49.9 7.0 %collective-permute-start.11 = (bf16[64,768]{1,0:T(8,128)(2,1)S(1)}, bf16[64,768]{1,0:T(8,128)(2,1)S(1)}, u32[]{:S(2)}, u32[]{:S(2)}) collective-permute-start(bf16[64,768]{1,0:T(8,128)(2,1)S(1)} %shard_map.63.refs_0_), channel_id=1, source_target_pairs={{0,4},{1,5},{2,6},{3,7},{4,0},{5,1},{6,2},{7,3},{8,12},{9,13},{10,... | collective-permute-start | bytes 294920 | tf_op jit(solution)/shard_map/ppermute | solution.py:267
  51.9 6.0 %collective-permute-start.12 = (bf16[64,768]{1,0:T(8,128)(2,1)S(1)}, bf16[64,768]{1,0:T(8,128)(2,1)S(1)}, u32[]{:S(2)}, u32[]{:S(2)}) collective-permute-start(bf16[64,768]{1,0:T(8,128)(2,1)S(1)} %shard_map.63.refs_0_), channel_id=1, source_target_pairs={{0,6},{1,7},{2,4},{3,5},{4,2},{5,3},{6,0},{7,1},{8,14},{9,15},{10,... | collective-permute-start | bytes 294920 | tf_op jit(solution)/shard_map/ppermute | solution.py:267
  54.3 3.7 %collective-permute-start.13 = (bf16[64,768]{1,0:T(8,128)(2,1)S(1)}, bf16[64,768]{1,0:T(8,128)(2,1)S(1)}, u32[]{:S(2)}, u32[]{:S(2)}) collective-permute-start(bf16[64,768]{1,0:T(8,128)(2,1)S(1)} %shard_map.63.refs_0_), channel_id=1, source_target_pairs={{0,1},{1,0},{2,3},{3,2},{4,5},{5,4},{6,7},{7,6},{8,9},{9,8},{10,11... | collective-permute-start | bytes 294920 | tf_op jit(solution)/shard_map/ppermute | solution.py:267
  54.3 5.7 %copy-start.4 = (s32[8]{0:T(128)S(1)}, s32[8]{0:T(128)}, u32[]{:S(2)}) copy-start(s32[8]{0:T(128)} %constant.12.clone) | copy-start | bytes 100
  54.3 5.6 %collective-permute-start.26 = (bf16[64,768]{1,0:T(8,128)(2,1)S(1)}, bf16[64,768]{1,0:T(8,128)(2,1)S(1)}, u32[]{:S(2)}, u32[]{:S(2)}) collective-permute-start(bf16[64,768]{1,0:T(8,128)(2,1)S(1)} %shard_map.67.refs_0_), channel_id=1, source_target_pairs={{0,2},{1,3},{2,0},{3,1},{4,6},{5,7},{6,4},{7,5},{8,10},{9,11},{10,... | collective-permute-start | bytes 294920 | tf_op jit(solution)/shard_map/ppermute | solution.py:267
  54.5 7.4 %collective-permute-start.27 = (bf16[64,768]{1,0:T(8,128)(2,1)S(1)}, bf16[64,768]{1,0:T(8,128)(2,1)S(1)}, u32[]{:S(2)}, u32[]{:S(2)}) collective-permute-start(bf16[64,768]{1,0:T(8,128)(2,1)S(1)} %shard_map.67.refs_0_), channel_id=1, source_target_pairs={{0,4},{1,5},{2,6},{3,7},{4,0},{5,1},{6,2},{7,3},{8,12},{9,13},{10,... | collective-permute-start | bytes 294920 | tf_op jit(solution)/shard_map/ppermute | solution.py:267
  56.9 5.6 %collective-permute-start.28 = (bf16[64,768]{1,0:T(8,128)(2,1)S(1)}, bf16[64,768]{1,0:T(8,128)(2,1)S(1)}, u32[]{:S(2)}, u32[]{:S(2)}) collective-permute-start(bf16[64,768]{1,0:T(8,128)(2,1)S(1)} %shard_map.67.refs_0_), channel_id=1, source_target_pairs={{0,6},{1,7},{2,4},{3,5},{4,2},{5,3},{6,0},{7,1},{8,14},{9,15},{10,... | collective-permute-start | bytes 294920 | tf_op jit(solution)/shard_map/ppermute | solution.py:267
  57.9 4.7 %collective-permute-start.14 = (bf16[64,768]{1,0:T(8,128)(2,1)S(1)}, bf16[64,768]{1,0:T(8,128)(2,1)S(1)}, u32[]{:S(2)}, u32[]{:S(2)}) collective-permute-start(bf16[64,768]{1,0:T(8,128)(2,1)S(1)} %collective-permute-done.10.refs_1_), channel_id=1, source_target_pairs={{0,1},{1,0},{2,3},{3,2},{4,5},{5,4},{6,7},{7,6},{8,9},{9,8},{10,11... | collective-permute-start | bytes 294920 | tf_op jit(solution)/shard_map/ppermute | solution.py:267
  57.9 5.1 %collective-permute-start.15 = (bf16[64,768]{1,0:T(8,128)(2,1)S(1)}, bf16[64,768]{1,0:T(8,128)(2,1)S(1)}, u32[]{:S(2)}, u32[]{:S(2)}) collective-permute-start(bf16[64,768]{1,0:T(8,128)(2,1)S(1)} %collective-permute-done.11.refs_2_), channel_id=1, source_target_pairs={{0,1},{1,0},{2,3},{3,2},{4,5},{5,4},{6,7},{7,6},{8,9},{9,8},{10,11... | collective-permute-start | bytes 294920 | tf_op jit(solution)/shard_map/ppermute | solution.py:267
  60.0 3.1 %collective-permute-start.16 = (bf16[64,768]{1,0:T(8,128)(2,1)S(1)}, bf16[64,768]{1,0:T(8,128)(2,1)S(1)}, u32[]{:S(2)}, u32[]{:S(2)}) collective-permute-start(bf16[64,768]{1,0:T(8,128)(2,1)S(1)} %collective-permute-done.12.refs_3_), channel_id=1, source_target_pairs={{0,1},{1,0},{2,3},{3,2},{4,5},{5,4},{6,7},{7,6},{8,9},{9,8},{10,11... | collective-permute-start | bytes 294920 | tf_op jit(solution)/shard_map/ppermute | solution.py:267
  61.9 2.4 %collective-permute-start.29 = (bf16[64,768]{1,0:T(8,128)(2,1)S(1)}, bf16[64,768]{1,0:T(8,128)(2,1)S(1)}, u32[]{:S(2)}, u32[]{:S(2)}) collective-permute-start(bf16[64,768]{1,0:T(8,128)(2,1)S(1)} %shard_map.67.refs_0_), channel_id=1, source_target_pairs={{0,1},{1,0},{2,3},{3,2},{4,5},{5,4},{6,7},{7,6},{8,9},{9,8},{10,11... | collective-permute-start | bytes 294920 | tf_op jit(solution)/shard_map/ppermute | solution.py:267
  62.5 1.8 %collective-permute-start.30 = (bf16[64,768]{1,0:T(8,128)(2,1)S(1)}, bf16[64,768]{1,0:T(8,128)(2,1)S(1)}, u32[]{:S(2)}, u32[]{:S(2)}) collective-permute-start(bf16[64,768]{1,0:T(8,128)(2,1)S(1)} %collective-permute-done.26.refs_1_), channel_id=1, source_target_pairs={{0,1},{1,0},{2,3},{3,2},{4,5},{5,4},{6,7},{7,6},{8,9},{9,8},{10,11... | collective-permute-start | bytes 294920 | tf_op jit(solution)/shard_map/ppermute | solution.py:267
  62.6 1.7 %collective-permute-start.31 = (bf16[64,768]{1,0:T(8,128)(2,1)S(1)}, bf16[64,768]{1,0:T(8,128)(2,1)S(1)}, u32[]{:S(2)}, u32[]{:S(2)}) collective-permute-start(bf16[64,768]{1,0:T(8,128)(2,1)S(1)} %collective-permute-done.27.refs_2_), channel_id=1, source_target_pairs={{0,1},{1,0},{2,3},{3,2},{4,5},{5,4},{6,7},{7,6},{8,9},{9,8},{10,11... | collective-permute-start | bytes 294920 | tf_op jit(solution)/shard_map/ppermute | solution.py:267
  63.0 1.3 %collective-permute-start.32 = (bf16[64,768]{1,0:T(8,128)(2,1)S(1)}, bf16[64,768]{1,0:T(8,128)(2,1)S(1)}, u32[]{:S(2)}, u32[]{:S(2)}) collective-permute-start(bf16[64,768]{1,0:T(8,128)(2,1)S(1)} %collective-permute-done.28.refs_3_), channel_id=1, source_target_pairs={{0,1},{1,0},{2,3},{3,2},{4,5},{5,4},{6,7},{7,6},{8,9},{9,8},{10,11... | collective-permute-start | bytes 294920 | tf_op jit(solution)/shard_map/ppermute | solution.py:267

commit v2 on v1

--- a/solution.py
+++ b/solution.py
@@ -9,8 +9,9 @@
 
 
 F32, BF16 = jnp.float32, jnp.bfloat16
-CHUNKS = 2
-HINTS = (1e11, 1e11, 1e11, 1e6, 1e6)
+SHARE = 0.5
+RELAYED = (True, False)
+HINTS = (1e11, 1e11, 1e6, 1e6, 1e6)
 STATS = 8
 EXPERT_HINT = 1e9
 
@@ -47,7 +48,6 @@
 
 def partial_kernel(slots, count, *refs):
     which_refs, (own_ref, other_ref, w_ref), out_refs = refs[:count], refs[count : count + 3], refs[count + 3 :]
-    span = out_refs[0].shape[0] - STATS
     if len(w_ref.shape) == 2:
         columns = [
             w_ref[:, pl.ds(pl.multiple_of(which_refs[n][0] * slots, slots), slots)]
@@ -70,18 +70,22 @@
     row = lax.broadcasted_iota(jnp.int32, (STATS, w.shape[1]), 0)
     stats = jnp.where(row == 0, top, jnp.where(row == 1, high, total - high)).astype(BF16)
     value = value.astype(BF16)
-    for n, out_ref in enumerate(out_refs):
-        part = slice(n * span, (n + 1) * span)
+    at = 0
+    for out_ref in out_refs:
+        span = out_ref.shape[0] - STATS
+        part = slice(at, at + span)
         out_ref[:span, :] = value[part]
         out_ref[span:, :] = jnp.zeros((STATS, out_ref.shape[1]), BF16)
         out_ref[span:, :span] = stats[:, part]
-
-
-def partial(which, own, other, weight, slots, chunks, hint):
+        at += span
+
+
+def partial(which, own, other, weight, spans, hint):
+    slots = sum(spans)
     rows, width = own.shape
     return call(
         functools.partial(partial_kernel, slots, len(which)),
-        [(slots // chunks + STATS, width)] * (len(which) * chunks),
+        [(span + STATS, width) for span in spans] * len(which),
         [*which, own, other, weight],
         moved=4 * rows * width,
         scalars=len(which),
@@ -125,8 +129,8 @@
     )
 
 
-def softmax_kernel(step, span, x_ref, w_ref, *out_refs):
-    chunks = len(out_refs)
+def softmax_kernel(step, spans, x_ref, w_ref, *out_refs):
+    slots = sum(spans)
 
     @pl.loop(0, x_ref.shape[0] // step)
     def _(i):
@@ -134,27 +138,37 @@
         logits = jnp.dot(x_ref[rows, :], w_ref[...], preferred_element_type=F32)
         raised = jnp.exp(logits - jnp.max(logits, axis=1, keepdims=True))
         share = raised / jnp.sum(raised, axis=1, keepdims=True)
-        for c, out_ref in enumerate(out_refs):
+        first = 0
+        for span, out_ref in zip(spans, out_refs):
             pieces = [
-                share[:, at : at + span] for at in range(c * span, share.shape[1], chunks * span)
+                share[:, at : at + span] for at in range(first, share.shape[1], slots)
             ]
             out_ref[rows, :] = jnp.concatenate(pieces, axis=1).astype(BF16)
-
-
-def softmax(x, weight, span, chunks):
+            first += span
+
+
+def softmax(x, weight, spans):
     rows, width = x.shape
     slots = weight.shape[1]
     return call(
-        functools.partial(softmax_kernel, min(rows, 256), span),
-        [(rows, slots // chunks)] * chunks,
+        functools.partial(softmax_kernel, min(rows, 256), spans),
+        [(rows, slots // sum(spans) * span) for span in spans],
         [x, weight],
         moved=2 * (rows * width + width * slots + rows * slots),
         hint=HINTS[3],
     )
 
 
+def marker_kernel(x_ref, out_ref):
+    out_ref[...] = x_ref[:8, :]
+
+
+def marker(x):
+    return call(marker_kernel, (8, x.shape[1]), [x], moved=1, hint=1e11, limit=1 << 20)
+
+
 def expert_kernel(count, first, n, each, *refs):
-    xs, w_in, w_out, ys = refs[:count], refs[count], refs[count + 1], refs[count + 2 :]
+    xs, w_in, w_out, ys = refs[:count], refs[count], refs[count + 1], refs[count + 3 :]
 
     @pl.loop(0, n)
     def _(e):
@@ -167,12 +181,12 @@
             y[at, :] = terms[k * each : (k + 1) * each].astype(BF16)
 
 
-def experts(xs, w_in, w_out, first, count):
+def experts(xs, w_in, w_out, mark, first, count):
     rows, width = xs[0].shape
     return call(
         functools.partial(expert_kernel, len(xs), first, count, rows // count),
         [(rows, width)] * len(xs),
-        [*xs, w_in, w_out],
+        [*xs, w_in, w_out, mark],
         moved=1,
         hint=EXPERT_HINT,
         limit=4 << 20,
@@ -261,7 +275,10 @@
     experts_here = expert_in.shape[0]
     slots = slot_weight.shape[1] // n_token
     width = tokens.shape[1]
-    chunk_experts, span = experts_here // CHUNKS, slots // CHUNKS
+    first = max(1, min(experts_here - 1, round(experts_here * SHARE)))
+    counts = [first, experts_here - first]
+    spans = [n * (slots // experts_here) for n in counts]
+    chunks = len(counts)
 
     def over_token(x, k):
         return lax.ppermute(x, "token", [(i, i ^ k) for i in range(n_token)])
@@ -276,41 +293,48 @@
     else:
         weight = slot_weight
     away = list(reversed(range(1, chips)))
-    made = [[] for _ in range(CHUNKS)]
+    made = [[] for _ in range(chunks)]
     for n, ks in enumerate((away[:1], away[1:], [0])):
         which = [jnp.bitwise_xor(me, 2 * k).astype(jnp.int32)[None] for k in ks]
-        results = partial(which, own, other, weight, slots, CHUNKS, HINTS[n])
-        for c in range(CHUNKS):
-            made[c] += [(k, results[i * CHUNKS + c]) for i, k in enumerate(ks)]
+        results = partial(which, own, other, weight, spans, HINTS[n])
+        for c in range(chunks):
+            made[c] += [(k, results[i * chunks + c]) for i, k in enumerate(ks)]
     inputs = []
-    for c in range(CHUNKS):
+    for c in range(chunks):
         arrived = [over_token(x, 2 * k) if k else x for k, x in made[c]]
-        inputs += combine(arrived, span, 1)
-    weights = softmax(own, slot_weight, span, CHUNKS)
+        inputs += combine(arrived, spans[c], 1)
+    mark = marker(inputs[0])
+    weights = softmax(own, slot_weight, spans)
 
     order = [2 * k for k in range(chips)] + [2 * k + 1 for k in range(chips)]
     at = jnp.bitwise_xor(me, jnp.array(order, jnp.int32))
     xs = []
-    for x in inputs:
+    for c, x in enumerate(inputs):
         held = {0: x}
-        bit = n_batch // 2
-        while bit:
-            for k in list(held):
-                held[k ^ bit] = over_batch(held[k], bit)
-            bit //= 2
+        if RELAYED[c]:
+            bit = n_batch // 2
+            while bit:
+                for k in list(held):
+                    held[k ^ bit] = over_batch(held[k], bit)
+                bit //= 2
+        else:
+            for k in reversed(range(1, n_batch)):
+                held[k] = over_batch(x, k)
         xs.append([held[k] for k in range(n_batch)])
     keys = list(range(n_batch))
     total, parts = None, []
-    for c in range(CHUNKS):
-        ys = experts(xs[c], expert_in, expert_out, c * chunk_experts, chunk_experts)
+    for c in range(chunks):
+        ys = experts(xs[c], expert_in, expert_out, mark, sum(counts[:c]), counts[c])
         parts.append([over_batch(ys[k], k) if k else ys[k] for k in reversed(keys)])
-    for c in range(CHUNKS):
+    for c in range(chunks):
         rows = add_up(parts[c])
-        there = [over_token(rows, 2 * k) if k else rows for k in range(chips)]
+        there = [rows]
+        for k in range(1, chips):
+            there.append(over_token(rows, 2 * k))
         swapped = [over_token(there[0], 1)]
         swapped += [over_token(r, 1) for r in there[1:]]
         blocks = there + swapped
-        if c < CHUNKS - 1:
+        if c < chunks - 1:
             total = first_mix(at, weights[c], blocks)
     return last_mix(at, weights[-1], total, blocks)
 

time: 66.4 us -> 72.2 us (1.087)
  waiting for transfers between devices: 7.11 us -> 14.5 us
  starting transfers between devices: 38 us -> 35.5 us
  local copies, waits for them, and re-layouts: 1.58 us -> 2.34 us
    ppermute x12, waiting for transfers between devices: 2.76 us -> 9.88 us  [over_batch(): return lax.ppermute(x, 'batch', [(i, i ^ k) for i in range(n_batch)])]
    ppermute x12, starting transfers between devices: 19.3 us -> 17.5 us  [over_batch(): return lax.ppermute(x, 'batch', [(i, i ^ k) for i in range(n_batch)])]
    unnamed x10 -> x28, local copies, waits for them, and re-layouts: 1.58 us -> 2.34 us
    pallas_call x13 -> x14, Pallas kernels: 17.5 us -> 17.5 us  [call(): pl.pallas_call(kernel, out_shape=[pltpu.VMEM(shape, dtype) for shape in s...]
  transfers between devices with their start and end apart: 33 -> 33, of which waited for: 8 -> 9; matrix products, arithmetic and copies ran while one was open for 0% -> 0% of each run, Pallas kernels for 24% -> 22%
where the time goes in v2:
time: 72.2 us; the launch traced here: 72.1 us
  starting transfers between devices  35.5 us (49%)
  Pallas kernels  19.4 us (27%)
  waiting for transfers between devices  14.5 us (20%)
  local copies, waits for them, and re-layouts  2.34 us (3%)
    ppermute x21, starting transfers between devices, over_token(): return lax.ppermute(x, 'token', [(i, i ^ k) for i in range(n_token)])  18 us
    ppermute x12, starting transfers between devices, over_batch(): return lax.ppermute(x, 'batch', [(i, i ^ k) for i in range(n_batch)])  17.5 us
    pallas_call x14, Pallas kernels, call(): pl.pallas_call(kernel, out_shape=[pltpu.VMEM(shape, dtype) for shape in s...  17.5 us
    ppermute x12, waiting for transfers between devices, over_batch(): return lax.ppermute(x, 'batch', [(i, i ^ k) for i in range(n_batch)])  9.88 us
    ppermute x21, waiting for transfers between devices, over_token(): return lax.ppermute(x, 'token', [(i, i ^ k) for i in range(n_token)])  4.61 us
    unnamed x28, local copies, waits for them, and re-layouts  2.34 us
    pallas_call x1, Pallas kernels, last_mix(): pl.pallas_call(functools.partial(last_mix_kernel, steps), out_shape=jax.S...  1.93 us
  transfers between devices with their start and end apart: 33, of which 9 were waited for; matrix products, arithmetic and copies ran while one was open for 0% of the time, Pallas kernels for 22%

profile of v2, /device:TPU:0, one launch (start us, length us, event | category | flops | bytes accessed | tf_op | source)
XLA Modules:
  0.0 72.1 jit_solution(1095956659119645729)
XLA Ops:
  0.0 0.5 collective-permute-start
  0.5 1.1 %copy-done.2 = bf16[512,768]{1,0:T(8,128)(2,1)S(1)} copy-done((bf16[512,768]{1,0:T(8,128)(2,1)S(1)}, bf16[512,768]{1,0:T(8,128)(2,1)}, u32[]{:S(2)}) %copy-start.2) | copy-done | bytes 786456
  1.6 0.2 shard_map.55.x_ref.refs_1_.refs_2_
  1.9 0.0 copy-start
  1.9 0.7 %collective-permute-done.x_ref = bf16[512,768]{1,0:T(8,128)(2,1)S(1)} collective-permute-done((bf16[512,768]{1,0:T(8,128)(2,1)}, bf16[512,768]{1,0:T(8,128)(2,1)S(1)}, u32[]{:S(2)}, u32[]{:S(2)}) %collective-permute-start) | collective-permute-done | bytes 786464 | tf_op jit(solution)/shard_map/ppermute | solution.py:284
  2.6 0.2 shard_map.57.refs_2_.refs_3_
  2.9 0.4 copy-done
  3.3 1.2 %shard_map.58 = (bf16[72,768]{1,0:T(8,128)(2,1)S(1)}, bf16[72,768]{1,0:T(8,128)(2,1)S(1)}) custom-call(s32[1]{0:T(128)} %bitcast.refs_0_, bf16[512,768]{1,0:T(8,128)(2,1)S(1)} %shard_map.55.x_ref.refs_1_.refs_2_, bf16[512,768]{1,0:T(8,128)(2,1)S(1)} %shard_map.57.refs_2_.refs_3_, bf16[768,1024]{1,0:T(8,128)(2,1)S(1)} %copy-done), custom_call_target="tpu_custom_call" | custom-call | flops 99999997952 | bytes 1572864 | tf_op jit(solution)/shard_map/pallas_call | solution.py:27
  4.5 3.5 %collective-permute-start.1 = (bf16[72,768]{1,0:T(8,128)(2,1)S(1)}, bf16[72,768]{1,0:T(8,128)(2,1)S(1)}, u32[]{:S(2)}, u32[]{:S(2)}) collective-permute-start(bf16[72,768]{1,0:T(8,128)(2,1)S(1)} %get-tuple-element.25), channel_id=1, source_target_pairs={{0,6},{1,7},{2,4},{3,5},{4,2},{5,3},{6,0},{7,1},{8,14},{9,15},{10,... | collective-permute-start | bytes 331784 | tf_op jit(solution)/shard_map/ppermute | solution.py:284
  8.0 1.6 %shard_map.59 = (bf16[72,768]{1,0:T(8,128)(2,1)S(1)}, bf16[72,768]{1,0:T(8,128)(2,1)S(1)}, bf16[72,768]{1,0:T(8,128)(2,1)S(1)}, bf16[72,768]{1,0:T(8,128)(2,1)S(1)}) custom-call(s32[1]{0:T(128)} %bitcast.1.refs_0_, s32[1]{0:T(128)} %bitcast.2.refs_1_, bf16[512,768]{1,0:T(8,128)(2,1)S(1)} %shard_map.55.x_ref.refs_1_.refs_2_, ...), custom_call_target="tpu_custom_call" | custom-call | flops 99999997952 | bytes 1572864 | tf_op jit(solution)/shard_map/pallas_call | solution.py:27
  9.6 0.6 collective-permute-start.2
  10.2 0.1 collective-permute-start.3
  10.3 2.9 %collective-permute-start.17 = (bf16[72,768]{1,0:T(8,128)(2,1)S(1)}, bf16[72,768]{1,0:T(8,128)(2,1)S(1)}, u32[]{:S(2)}, u32[]{:S(2)}) collective-permute-start(bf16[72,768]{1,0:T(8,128)(2,1)S(1)} %get-tuple-element.33), channel_id=1, source_target_pairs={{0,6},{1,7},{2,4},{3,5},{4,2},{5,3},{6,0},{7,1},{8,14},{9,15},{10,... | collective-permute-start | bytes 331784 | tf_op jit(solution)/shard_map/ppermute | solution.py:284
  13.1 0.5 collective-permute-start.18
  13.7 0.1 collective-permute-start.19
  13.8 1.2 %shard_map.60 = (bf16[72,768]{1,0:T(8,128)(2,1)S(1)}, bf16[72,768]{1,0:T(8,128)(2,1)S(1)}) custom-call(s32[1]{0:T(128)} %bitcast.3.refs_0_, bf16[512,768]{1,0:T(8,128)(2,1)S(1)} %shard_map.55.x_ref.refs_1_.refs_2_, bf16[512,768]{1,0:T(8,128)(2,1)S(1)} %shard_map.57.refs_2_.refs_3_, bf16[768,1024]{1,0:T(8,128)(2,1)S(1)} %copy-done), custom_call_target="tpu_custom_call" | custom-call | flops 1000000 | bytes 1572864 | tf_op jit(solution)/shard_map/pallas_call | solution.py:27
  14.9 0.0 collective-permute-done.2.refs_1_
  14.9 1.2 %collective-permute-done.3.refs_2_ = bf16[72,768]{1,0:T(8,128)(2,1)S(1)} collective-permute-done((bf16[72,768]{1,0:T(8,128)(2,1)S(1)}, bf16[72,768]{1,0:T(8,128)(2,1)S(1)}, u32[]{:S(2)}, u32[]{:S(2)}) %collective-permute-start.3) | collective-permute-done | bytes 110624 | tf_op jit(solution)/shard_map/ppermute | solution.py:284
  16.1 0.2 shard_map.61.x_ref.refs_0_
  16.3 1.6 %collective-permute-start.4 = (bf16[64,768]{1,0:T(8,128)(2,1)S(1)}, bf16[64,768]{1,0:T(8,128)(2,1)S(1)}, u32[]{:S(2)}, u32[]{:S(2)}) collective-permute-start(bf16[64,768]{1,0:T(8,128)(2,1)S(1)} %shard_map.61.x_ref.refs_0_), channel_id=1, source_target_pairs={{0,8},{8,0},{16,24},{24,16},{1,9},{9,1},{17,25},{25,17},{2,10},{10... | collective-permute-start | bytes 294920 | tf_op jit(solution)/shard_map/ppermute | solution.py:287
  17.9 2.6 %collective-permute-start.5 = (bf16[64,768]{1,0:T(8,128)(2,1)S(1)}, bf16[64,768]{1,0:T(8,128)(2,1)S(1)}, u32[]{:S(2)}, u32[]{:S(2)}) collective-permute-start(bf16[64,768]{1,0:T(8,128)(2,1)S(1)} %shard_map.61.x_ref.refs_0_), channel_id=1, source_target_pairs={{0,16},{8,24},{16,0},{24,8},{1,17},{9,25},{17,1},{25,9},{2,18},{10... | collective-permute-start | bytes 294920 | tf_op jit(solution)/shard_map/ppermute | solution.py:287
  20.5 0.0 collective-permute-done.17.refs_0_
  20.5 0.0 collective-permute-done.18.refs_1_
  20.5 0.0 slice-start
  20.5 0.0 slice-start.5
  20.6 0.2 shard_map.66.refs_0_
  20.7 0.0 slice-start.1
  20.7 0.0 slice-start.2
  20.8 0.0 slice-start.3
  20.8 0.0 slice-start.6
  20.8 0.9 %collective-permute-start.20 = (bf16[64,768]{1,0:T(8,128)(2,1)S(1)}, bf16[64,768]{1,0:T(8,128)(2,1)S(1)}, u32[]{:S(2)}, u32[]{:S(2)}) collective-permute-start(bf16[64,768]{1,0:T(8,128)(2,1)S(1)} %shard_map.66.refs_0_), channel_id=1, source_target_pairs={{0,8},{8,0},{16,24},{24,16},{1,9},{9,1},{17,25},{25,17},{2,10},{10... | collective-permute-start | bytes 294920 | tf_op jit(solution)/shard_map/ppermute | solution.py:287
  21.7 2.6 %collective-permute-start.21 = (bf16[64,768]{1,0:T(8,128)(2,1)S(1)}, bf16[64,768]{1,0:T(8,128)(2,1)S(1)}, u32[]{:S(2)}, u32[]{:S(2)}) collective-permute-start(bf16[64,768]{1,0:T(8,128)(2,1)S(1)} %shard_map.66.refs_0_), channel_id=1, source_target_pairs={{0,16},{8,24},{16,0},{24,8},{1,17},{9,25},{17,1},{25,9},{2,18},{10... | collective-permute-start | bytes 294920 | tf_op jit(solution)/shard_map/ppermute | solution.py:287
  24.3 1.0 %collective-permute-start.22 = (bf16[64,768]{1,0:T(8,128)(2,1)S(1)}, bf16[64,768]{1,0:T(8,128)(2,1)S(1)}, u32[]{:S(2)}, u32[]{:S(2)}) collective-permute-start(bf16[64,768]{1,0:T(8,128)(2,1)S(1)} %shard_map.66.refs_0_), channel_id=1, source_target_pairs={{0,24},{8,16},{16,8},{24,0},{1,25},{9,17},{17,9},{25,1},{2,26},{10... | collective-permute-start | bytes 294920 | tf_op jit(solution)/shard_map/ppermute | solution.py:287
  25.3 2.9 %collective-permute-done.20.refs_1_ = bf16[64,768]{1,0:T(8,128)(2,1)S(1)} collective-permute-done((bf16[64,768]{1,0:T(8,128)(2,1)S(1)}, bf16[64,768]{1,0:T(8,128)(2,1)S(1)}, u32[]{:S(2)}, u32[]{:S(2)}) %collective-permute-start.20) | collective-permute-done | bytes 98336 | tf_op jit(solution)/shard_map/ppermute | solution.py:287
  28.2 3.4 %collective-permute-done.21.refs_2_ = bf16[64,768]{1,0:T(8,128)(2,1)S(1)} collective-permute-done((bf16[64,768]{1,0:T(8,128)(2,1)S(1)}, bf16[64,768]{1,0:T(8,128)(2,1)S(1)}, u32[]{:S(2)}, u32[]{:S(2)}) %collective-permute-start.21) | collective-permute-done | bytes 98336 | tf_op jit(solution)/shard_map/ppermute | solution.py:287
  31.7 0.7 slice-done.9
  32.4 4.8 %shard_map.67 = (bf16[64,768]{1,0:T(8,128)(2,1)S(1)}, bf16[64,768]{1,0:T(8,128)(2,1)S(1)}, bf16[64,768]{1,0:T(8,128)(2,1)S(1)}, bf16[64,768]{1,0:T(8,128)(2,1)S(1)}) custom-call(bf16[64,768]{1,0:T(8,128)(2,1)S(1)} %shard_map.66.refs_0_, bf16[64,768]{1,0:T(8,128)(2,1)S(1)} %collective-permute-done.20.refs_1_, ...), custom_call_target="tpu_custom_call" | custom-call | flops 1000000000 | bytes 1 | tf_op jit(solution)/shard_map/pallas_call | solution.py:27
  37.2 2.9 %collective-permute-start.23 = (bf16[64,768]{1,0:T(8,128)(2,1)S(1)}, bf16[64,768]{1,0:T(8,128)(2,1)S(1)}, u32[]{:S(2)}, u32[]{:S(2)}) collective-permute-start(bf16[64,768]{1,0:T(8,128)(2,1)S(1)} %get-tuple-element.37), channel_id=1, source_target_pairs={{0,24},{8,16},{16,8},{24,0},{1,25},{9,17},{17,9},{25,1},{2,26},{10... | collective-permute-start | bytes 294920 | tf_op jit(solution)/shard_map/ppermute | solution.py:287
  40.1 1.5 %collective-permute-start.25 = (bf16[64,768]{1,0:T(8,128)(2,1)S(1)}, bf16[64,768]{1,0:T(8,128)(2,1)S(1)}, u32[]{:S(2)}, u32[]{:S(2)}) collective-permute-start(bf16[64,768]{1,0:T(8,128)(2,1)S(1)} %get-tuple-element.39), channel_id=1, source_target_pairs={{0,8},{8,0},{16,24},{24,16},{1,9},{9,1},{17,25},{25,17},{2,10},{10... | collective-permute-start | bytes 294920 | tf_op jit(solution)/shard_map/ppermute | solution.py:287
  41.6 4.8 %shard_map.63 = (bf16[64,768]{1,0:T(8,128)(2,1)S(1)}, bf16[64,768]{1,0:T(8,128)(2,1)S(1)}, bf16[64,768]{1,0:T(8,128)(2,1)S(1)}, bf16[64,768]{1,0:T(8,128)(2,1)S(1)}) custom-call(bf16[64,768]{1,0:T(8,128)(2,1)S(1)} %shard_map.61.x_ref.refs_0_, bf16[64,768]{1,0:T(8,128)(2,1)S(1)} %collective-permute-done.4.refs_1_, ...), custom_call_target="tpu_custom_call" | custom-call | flops 1000000000 | bytes 1 | tf_op jit(solution)/shard_map/pallas_call | solution.py:27
  46.3 2.9 %collective-permute-start.7 = (bf16[64,768]{1,0:T(8,128)(2,1)S(1)}, bf16[64,768]{1,0:T(8,128)(2,1)S(1)}, u32[]{:S(2)}, u32[]{:S(2)}) collective-permute-start(bf16[64,768]{1,0:T(8,128)(2,1)S(1)} %get-tuple-element.29), channel_id=1, source_target_pairs={{0,24},{8,16},{16,8},{24,0},{1,25},{9,17},{17,9},{25,1},{2,26},{10... | collective-permute-start | bytes 294920 | tf_op jit(solution)/shard_map/ppermute | solution.py:287
  49.2 1.5 %collective-permute-start.9 = (bf16[64,768]{1,0:T(8,128)(2,1)S(1)}, bf16[64,768]{1,0:T(8,128)(2,1)S(1)}, u32[]{:S(2)}, u32[]{:S(2)}) collective-permute-start(bf16[64,768]{1,0:T(8,128)(2,1)S(1)} %get-tuple-element.31), channel_id=1, source_target_pairs={{0,8},{8,0},{16,24},{24,16},{1,9},{9,1},{17,25},{25,17},{2,10},{10... | collective-permute-start | bytes 294920 | tf_op jit(solution)/shard_map/ppermute | solution.py:287
  50.7 0.1 collective-permute-done.24.refs_1_
  50.8 0.1 shard_map.68.refs_0_
  50.9 0.8 %collective-permute-start.26 = (bf16[64,768]{1,0:T(8,128)(2,1)S(1)}, bf16[64,768]{1,0:T(8,128)(2,1)S(1)}, u32[]{:S(2)}, u32[]{:S(2)}) collective-permute-start(bf16[64,768]{1,0:T(8,128)(2,1)S(1)} %shard_map.68.refs_0_), channel_id=1, source_target_pairs={{0,2},{1,3},{2,0},{3,1},{4,6},{5,7},{6,4},{7,5},{8,10},{9,11},{10,... | collective-permute-start | bytes 294920 | tf_op jit(solution)/shard_map/ppermute | solution.py:284
  51.7 1.4 %collective-permute-start.27 = (bf16[64,768]{1,0:T(8,128)(2,1)S(1)}, bf16[64,768]{1,0:T(8,128)(2,1)S(1)}, u32[]{:S(2)}, u32[]{:S(2)}) collective-permute-start(bf16[64,768]{1,0:T(8,128)(2,1)S(1)} %shard_map.68.refs_0_), channel_id=1, source_target_pairs={{0,4},{1,5},{2,6},{3,7},{4,0},{5,1},{6,2},{7,3},{8,12},{9,13},{10,... | collective-permute-start | bytes 294920 | tf_op jit(solution)/shard_map/ppermute | solution.py:284
  53.2 0.5 collective-permute-done.7.refs_0_
  53.6 3.0 %collective-permute-done.8.refs_1_ = bf16[64,768]{1,0:T(8,128)(2,1)S(1)} collective-permute-done((bf16[64,768]{1,0:T(8,128)(2,1)S(1)}, bf16[64,768]{1,0:T(8,128)(2,1)S(1)}, u32[]{:S(2)}, u32[]{:S(2)}) %collective-permute-start.8) | collective-permute-done | bytes 98336 | tf_op jit(solution)/shard_map/ppermute | solution.py:287
  56.6 0.1 shard_map.64.refs_0_
  56.7 0.9 %collective-permute-start.10 = (bf16[64,768]{1,0:T(8,128)(2,1)S(1)}, bf16[64,768]{1,0:T(8,128)(2,1)S(1)}, u32[]{:S(2)}, u32[]{:S(2)}) collective-permute-start(bf16[64,768]{1,0:T(8,128)(2,1)S(1)} %shard_map.64.refs_0_), channel_id=1, source_target_pairs={{0,2},{1,3},{2,0},{3,1},{4,6},{5,7},{6,4},{7,5},{8,10},{9,11},{10,... | collective-permute-start | bytes 294920 | tf_op jit(solution)/shard_map/ppermute | solution.py:284
  57.6 1.7 %collective-permute-start.11 = (bf16[64,768]{1,0:T(8,128)(2,1)S(1)}, bf16[64,768]{1,0:T(8,128)(2,1)S(1)}, u32[]{:S(2)}, u32[]{:S(2)}) collective-permute-start(bf16[64,768]{1,0:T(8,128)(2,1)S(1)} %shard_map.64.refs_0_), channel_id=1, source_target_pairs={{0,4},{1,5},{2,6},{3,7},{4,0},{5,1},{6,2},{7,3},{8,12},{9,13},{10,... | collective-permute-start | bytes 294920 | tf_op jit(solution)/shard_map/ppermute | solution.py:284
  59.3 0.9 %collective-permute-start.12 = (bf16[64,768]{1,0:T(8,128)(2,1)S(1)}, bf16[64,768]{1,0:T(8,128)(2,1)S(1)}, u32[]{:S(2)}, u32[]{:S(2)}) collective-permute-start(bf16[64,768]{1,0:T(8,128)(2,1)S(1)} %shard_map.64.refs_0_), channel_id=1, source_target_pairs={{0,6},{1,7},{2,4},{3,5},{4,2},{5,3},{6,0},{7,1},{8,14},{9,15},{10,... | collective-permute-start | bytes 294920 | tf_op jit(solution)/shard_map/ppermute | solution.py:284
  60.2 2.0 %collective-permute-start.28 = (bf16[64,768]{1,0:T(8,128)(2,1)S(1)}, bf16[64,768]{1,0:T(8,128)(2,1)S(1)}, u32[]{:S(2)}, u32[]{:S(2)}) collective-permute-start(bf16[64,768]{1,0:T(8,128)(2,1)S(1)} %shard_map.68.refs_0_), channel_id=1, source_target_pairs={{0,6},{1,7},{2,4},{3,5},{4,2},{5,3},{6,0},{7,1},{8,14},{9,15},{10,... | collective-permute-start | bytes 294920 | tf_op jit(solution)/shard_map/ppermute | solution.py:284
  62.3 0.5 collective-permute-start.14
  62.8 2.6 %collective-permute-done.11.refs_2_ = bf16[64,768]{1,0:T(8,128)(2,1)S(1)} collective-permute-done((bf16[64,768]{1,0:T(8,128)(2,1)S(1)}, bf16[64,768]{1,0:T(8,128)(2,1)S(1)}, u32[]{:S(2)}, u32[]{:S(2)}) %collective-permute-start.11) | collective-permute-done | bytes 98336 | tf_op jit(solution)/shard_map/ppermute | solution.py:284
  65.4 0.1 collective-permute-done.12.refs_3_
  65.5 0.4 collective-permute-start.16
  65.9 1.9 %shard_map.56 = (bf16[512,512]{1,0:T(8,128)(2,1)S(1)}, bf16[512,512]{1,0:T(8,128)(2,1)S(1)}) custom-call(bf16[512,768]{1,0:T(8,128)(2,1)S(1)} %shard_map.55.x_ref.refs_1_.refs_2_, bf16[768,1024]{1,0:T(8,128)(2,1)S(1)} %copy-done.1), custom_call_target="tpu_custom_call" | custom-call | flops 1000000 | bytes 3407872 | tf_op jit(solution)/shard_map/pallas_call | solution.py:27
  67.8 0.2 collective-permute-start.29
  68.0 0.4 collective-permute-start.30
  68.4 0.1 collective-permute-start.31
  68.5 0.4 collective-permute-start.32
  68.9 1.2 %shard_map.65.sum_ref = f32[512,768]{1,0:T(8,128)S(1)} custom-call(s32[8]{0:T(128)S(1)} %broadcast_xor_fusion.at_ref, bf16[512,512]{1,0:T(8,128)(2,1)S(1)} %get-tuple-element.24.c_ref, bf16[64,768]{1,0:T(8,128)(2,1)S(1)} %shard_map.64.refs_0_, bf16[64,768]{1,0:T(8,128)(2,1)S(1)} %collective-permute-done.10.refs_1_, ...), custom_call_target="tpu_custom_call" | custom-call | flops 99999997952 | bytes 2097152 | tf_op jit(solution)/shard_map/pallas_call | solution.py:27
  70.1 1.9 %last_mix.1 = bf16[512,768]{1,0:T(8,128)(2,1)} custom-call(s32[8]{0:T(128)S(1)} %broadcast_xor_fusion.at_ref, bf16[512,512]{1,0:T(8,128)(2,1)S(1)} %get-tuple-element.23.c_ref, f32[512,768]{1,0:T(8,128)S(1)} %shard_map.65.sum_ref, bf16[64,768]{1,0:T(8,128)(2,1)S(1)} %shard_map.68.refs_0_, bf16[64,768]{1,0:T(8,128)(2,1)S(1)} %collective-permute-done.26.refs_1_, ...), custom_call_target="tpu_custom_call" | custom-call | tf_op jit(solution)/shard_map/last_mix/pallas_call | solution.py:256
  (48 shorter events, 0.1 us)
Async XLA Ops:
  0.0 2.6 %collective-permute-start = (bf16[512,768]{1,0:T(8,128)(2,1)}, bf16[512,768]{1,0:T(8,128)(2,1)S(1)}, u32[]{:S(2)}, u32[]{:S(2)}) collective-permute-start(bf16[512,768]{1,0:T(8,128)(2,1)} %x_ref.1), channel_id=1, source_target_pairs={{0,1},{1,0},{2,3},{3,2},{4,5},{5,4},{6,7},{7,6},{8,9},{9,8},{10,11... | collective-permute-start | bytes 2359304 | tf_op jit(solution)/shard_map/ppermute | solution.py:284
  0.5 1.1 %copy-start.2 = (bf16[512,768]{1,0:T(8,128)(2,1)S(1)}, bf16[512,768]{1,0:T(8,128)(2,1)}, u32[]{:S(2)}) copy-start(bf16[512,768]{1,0:T(8,128)(2,1)} %x_ref.1) | copy-start | bytes 2359300
  1.9 1.4 %copy-start = (bf16[768,1024]{1,0:T(8,128)(2,1)S(1)}, bf16[768,1024]{1,0:T(8,128)(2,1)}, u32[]{:S(2)}) copy-start(bf16[768,1024]{1,0:T(8,128)(2,1)} %refs_3_.3) | copy-start | bytes 4718596
  4.5 9.2 %collective-permute-start.1 = (bf16[72,768]{1,0:T(8,128)(2,1)S(1)}, bf16[72,768]{1,0:T(8,128)(2,1)S(1)}, u32[]{:S(2)}, u32[]{:S(2)}) collective-permute-start(bf16[72,768]{1,0:T(8,128)(2,1)S(1)} %get-tuple-element.25), channel_id=1, source_target_pairs={{0,6},{1,7},{2,4},{3,5},{4,2},{5,3},{6,0},{7,1},{8,14},{9,15},{10,... | collective-permute-start | bytes 331784 | tf_op jit(solution)/shard_map/ppermute | solution.py:284
  9.6 5.3 %collective-permute-start.2 = (bf16[72,768]{1,0:T(8,128)(2,1)S(1)}, bf16[72,768]{1,0:T(8,128)(2,1)S(1)}, u32[]{:S(2)}, u32[]{:S(2)}) collective-permute-start(bf16[72,768]{1,0:T(8,128)(2,1)S(1)} %get-tuple-element.26), channel_id=1, source_target_pairs={{0,4},{1,5},{2,6},{3,7},{4,0},{5,1},{6,2},{7,3},{8,12},{9,13},{10,... | collective-permute-start | bytes 331784 | tf_op jit(solution)/shard_map/ppermute | solution.py:284
  10.2 5.9 %collective-permute-start.3 = (bf16[72,768]{1,0:T(8,128)(2,1)S(1)}, bf16[72,768]{1,0:T(8,128)(2,1)S(1)}, u32[]{:S(2)}, u32[]{:S(2)}) collective-permute-start(bf16[72,768]{1,0:T(8,128)(2,1)S(1)} %get-tuple-element.27), channel_id=1, source_target_pairs={{0,2},{1,3},{2,0},{3,1},{4,6},{5,7},{6,4},{7,5},{8,10},{9,11},{10,... | collective-permute-start | bytes 331784 | tf_op jit(solution)/shard_map/ppermute | solution.py:284
  10.3 10.2 %collective-permute-start.17 = (bf16[72,768]{1,0:T(8,128)(2,1)S(1)}, bf16[72,768]{1,0:T(8,128)(2,1)S(1)}, u32[]{:S(2)}, u32[]{:S(2)}) collective-permute-start(bf16[72,768]{1,0:T(8,128)(2,1)S(1)} %get-tuple-element.33), channel_id=1, source_target_pairs={{0,6},{1,7},{2,4},{3,5},{4,2},{5,3},{6,0},{7,1},{8,14},{9,15},{10,... | collective-permute-start | bytes 331784 | tf_op jit(solution)/shard_map/ppermute | solution.py:284
  13.1 7.4 %collective-permute-start.18 = (bf16[72,768]{1,0:T(8,128)(2,1)S(1)}, bf16[72,768]{1,0:T(8,128)(2,1)S(1)}, u32[]{:S(2)}, u32[]{:S(2)}) collective-permute-start(bf16[72,768]{1,0:T(8,128)(2,1)S(1)} %get-tuple-element.34), channel_id=1, source_target_pairs={{0,4},{1,5},{2,6},{3,7},{4,0},{5,1},{6,2},{7,3},{8,12},{9,13},{10,... | collective-permute-start | bytes 331784 | tf_op jit(solution)/shard_map/ppermute | solution.py:284
  13.7 6.9 %collective-permute-start.19 = (bf16[72,768]{1,0:T(8,128)(2,1)S(1)}, bf16[72,768]{1,0:T(8,128)(2,1)S(1)}, u32[]{:S(2)}, u32[]{:S(2)}) collective-permute-start(bf16[72,768]{1,0:T(8,128)(2,1)S(1)} %get-tuple-element.35), channel_id=1, source_target_pairs={{0,2},{1,3},{2,0},{3,1},{4,6},{5,7},{6,4},{7,5},{8,10},{9,11},{10,... | collective-permute-start | bytes 331784 | tf_op jit(solution)/shard_map/ppermute | solution.py:284
  16.3 25.3 %collective-permute-start.4 = (bf16[64,768]{1,0:T(8,128)(2,1)S(1)}, bf16[64,768]{1,0:T(8,128)(2,1)S(1)}, u32[]{:S(2)}, u32[]{:S(2)}) collective-permute-start(bf16[64,768]{1,0:T(8,128)(2,1)S(1)} %shard_map.61.x_ref.refs_0_), channel_id=1, source_target_pairs={{0,8},{8,0},{16,24},{24,16},{1,9},{9,1},{17,25},{25,17},{2,10},{10... | collective-permute-start | bytes 294920 | tf_op jit(solution)/shard_map/ppermute | solution.py:287
  17.9 7.4 %collective-permute-start.5 = (bf16[64,768]{1,0:T(8,128)(2,1)S(1)}, bf16[64,768]{1,0:T(8,128)(2,1)S(1)}, u32[]{:S(2)}, u32[]{:S(2)}) collective-permute-start(bf16[64,768]{1,0:T(8,128)(2,1)S(1)} %shard_map.61.x_ref.refs_0_), channel_id=1, source_target_pairs={{0,16},{8,24},{16,0},{24,8},{1,17},{9,25},{17,1},{25,9},{2,18},{10... | collective-permute-start | bytes 294920 | tf_op jit(solution)/shard_map/ppermute | solution.py:287
  20.5 11.1 %slice-start = ((s8[18874368]{0:T(1024)(128)(4,1)}), s8[4194304]{0:T(1024)(128)(4,1)S(1)}, s32[]{:S(2)}) async-start(s8[18874368]{0:T(1024)(128)(4,1)} %bitcast.4), calls=%async_computation | async-start | bytes 8388608
  20.5 11.1 %slice-start.5 = ((s8[18874368]{0:T(1024)(128)(4,1)}), s8[2097152]{0:T(1024)(128)(4,1)S(1)}, s32[]{:S(2)}) async-start(s8[18874368]{0:T(1024)(128)(4,1)} %bitcast.6), calls=%async_computation.5 | async-start | bytes 4194304
  20.7 10.9 %slice-start.1 = ((s8[18874368]{0:T(1024)(128)(4,1)}), s8[4194304]{0:T(1024)(128)(4,1)S(1)}, s32[]{:S(2)}) async-start(s8[18874368]{0:T(1024)(128)(4,1)} %bitcast.4), calls=%async_computation.1 | async-start | bytes 8388608
  20.7 10.9 %slice-start.2 = ((s8[18874368]{0:T(1024)(128)(4,1)}), s8[4194304]{0:T(1024)(128)(4,1)S(1)}, s32[]{:S(2)}) async-start(s8[18874368]{0:T(1024)(128)(4,1)} %bitcast.4), calls=%async_computation.2 | async-start | bytes 8388608
  20.8 10.9 %slice-start.3 = ((s8[18874368]{0:T(1024)(128)(4,1)}), s8[4194304]{0:T(1024)(128)(4,1)S(1)}, s32[]{:S(2)}) async-start(s8[18874368]{0:T(1024)(128)(4,1)} %bitcast.4), calls=%async_computation.3 | async-start | bytes 8388608
  20.8 10.9 %slice-start.4 = ((s8[18874368]{0:T(1024)(128)(4,1)}), s8[2097152]{0:T(1024)(128)(4,1)S(1)}, s32[]{:S(2)}) async-start(s8[18874368]{0:T(1024)(128)(4,1)} %bitcast.4), calls=%async_computation.4 | async-start | bytes 4194304
  20.8 10.9 %slice-start.6 = ((s8[18874368]{0:T(1024)(128)(4,1)}), s8[4194304]{0:T(1024)(128)(4,1)S(1)}, s32[]{:S(2)}) async-start(s8[18874368]{0:T(1024)(128)(4,1)} %bitcast.6), calls=%async_computation.6 | async-start | bytes 8388608
  20.8 10.9 %slice-start.7 = ((s8[18874368]{0:T(1024)(128)(4,1)}), s8[4194304]{0:T(1024)(128)(4,1)S(1)}, s32[]{:S(2)}) async-start(s8[18874368]{0:T(1024)(128)(4,1)} %bitcast.6), calls=%async_computation.7 | async-start | bytes 8388608
  20.8 10.9 %slice-start.8 = ((s8[18874368]{0:T(1024)(128)(4,1)}), s8[4194304]{0:T(1024)(128)(4,1)S(1)}, s32[]{:S(2)}) async-start(s8[18874368]{0:T(1024)(128)(4,1)} %bitcast.6), calls=%async_computation.8 | async-start | bytes 8388608
  20.8 11.6 %slice-start.9 = ((s8[18874368]{0:T(1024)(128)(4,1)}), s8[4194304]{0:T(1024)(128)(4,1)S(1)}, s32[]{:S(2)}) async-start(s8[18874368]{0:T(1024)(128)(4,1)} %bitcast.6), calls=%async_computation.9 | async-start | bytes 8388608
  20.8 7.4 %collective-permute-start.20 = (bf16[64,768]{1,0:T(8,128)(2,1)S(1)}, bf16[64,768]{1,0:T(8,128)(2,1)S(1)}, u32[]{:S(2)}, u32[]{:S(2)}) collective-permute-start(bf16[64,768]{1,0:T(8,128)(2,1)S(1)} %shard_map.66.refs_0_), channel_id=1, source_target_pairs={{0,8},{8,0},{16,24},{24,16},{1,9},{9,1},{17,25},{25,17},{2,10},{10... | collective-permute-start | bytes 294920 | tf_op jit(solution)/shard_map/ppermute | solution.py:287
  21.7 9.9 %collective-permute-start.21 = (bf16[64,768]{1,0:T(8,128)(2,1)S(1)}, bf16[64,768]{1,0:T(8,128)(2,1)S(1)}, u32[]{:S(2)}, u32[]{:S(2)}) collective-permute-start(bf16[64,768]{1,0:T(8,128)(2,1)S(1)} %shard_map.66.refs_0_), channel_id=1, source_target_pairs={{0,16},{8,24},{16,0},{24,8},{1,17},{9,25},{17,1},{25,9},{2,18},{10... | collective-permute-start | bytes 294920 | tf_op jit(solution)/shard_map/ppermute | solution.py:287
  24.3 7.3 %collective-permute-start.22 = (bf16[64,768]{1,0:T(8,128)(2,1)S(1)}, bf16[64,768]{1,0:T(8,128)(2,1)S(1)}, u32[]{:S(2)}, u32[]{:S(2)}) collective-permute-start(bf16[64,768]{1,0:T(8,128)(2,1)S(1)} %shard_map.66.refs_0_), channel_id=1, source_target_pairs={{0,24},{8,16},{16,8},{24,0},{1,25},{9,17},{17,9},{25,1},{2,26},{10... | collective-permute-start | bytes 294920 | tf_op jit(solution)/shard_map/ppermute | solution.py:287
  25.3 16.3 %collective-permute-start.6 = (bf16[64,768]{1,0:T(8,128)(2,1)S(1)}, bf16[64,768]{1,0:T(8,128)(2,1)S(1)}, u32[]{:S(2)}, u32[]{:S(2)}) collective-permute-start(bf16[64,768]{1,0:T(8,128)(2,1)S(1)} %collective-permute-done.5.refs_2_), channel_id=1, source_target_pairs={{0,8},{8,0},{16,24},{24,16},{1,9},{9,1},{17,25},{25,17},{2,10},{10... | collective-permute-start | bytes 294920 | tf_op jit(solution)/shard_map/ppermute | solution.py:287
  37.2 12.1 %collective-permute-start.23 = (bf16[64,768]{1,0:T(8,128)(2,1)S(1)}, bf16[64,768]{1,0:T(8,128)(2,1)S(1)}, u32[]{:S(2)}, u32[]{:S(2)}) collective-permute-start(bf16[64,768]{1,0:T(8,128)(2,1)S(1)} %get-tuple-element.37), channel_id=1, source_target_pairs={{0,24},{8,16},{16,8},{24,0},{1,25},{9,17},{17,9},{25,1},{2,26},{10... | collective-permute-start | bytes 294920 | tf_op jit(solution)/shard_map/ppermute | solution.py:287
  40.1 10.7 %collective-permute-start.24 = (bf16[64,768]{1,0:T(8,128)(2,1)S(1)}, bf16[64,768]{1,0:T(8,128)(2,1)S(1)}, u32[]{:S(2)}, u32[]{:S(2)}) collective-permute-start(bf16[64,768]{1,0:T(8,128)(2,1)S(1)} %get-tuple-element.38), channel_id=1, source_target_pairs={{0,16},{8,24},{16,0},{24,8},{1,17},{9,25},{17,1},{25,9},{2,18},{10... | collective-permute-start | bytes 294920 | tf_op jit(solution)/shard_map/ppermute | solution.py:287
  40.1 10.7 %collective-permute-start.25 = (bf16[64,768]{1,0:T(8,128)(2,1)S(1)}, bf16[64,768]{1,0:T(8,128)(2,1)S(1)}, u32[]{:S(2)}, u32[]{:S(2)}) collective-permute-start(bf16[64,768]{1,0:T(8,128)(2,1)S(1)} %get-tuple-element.39), channel_id=1, source_target_pairs={{0,8},{8,0},{16,24},{24,16},{1,9},{9,1},{17,25},{25,17},{2,10},{10... | collective-permute-start | bytes 294920 | tf_op jit(solution)/shard_map/ppermute | solution.py:287
  46.3 7.3 %collective-permute-start.7 = (bf16[64,768]{1,0:T(8,128)(2,1)S(1)}, bf16[64,768]{1,0:T(8,128)(2,1)S(1)}, u32[]{:S(2)}, u32[]{:S(2)}) collective-permute-start(bf16[64,768]{1,0:T(8,128)(2,1)S(1)} %get-tuple-element.29), channel_id=1, source_target_pairs={{0,24},{8,16},{16,8},{24,0},{1,25},{9,17},{17,9},{25,1},{2,26},{10... | collective-permute-start | bytes 294920 | tf_op jit(solution)/shard_map/ppermute | solution.py:287
  49.2 7.4 %collective-permute-start.8 = (bf16[64,768]{1,0:T(8,128)(2,1)S(1)}, bf16[64,768]{1,0:T(8,128)(2,1)S(1)}, u32[]{:S(2)}, u32[]{:S(2)}) collective-permute-start(bf16[64,768]{1,0:T(8,128)(2,1)S(1)} %get-tuple-element.30), channel_id=1, source_target_pairs={{0,16},{8,24},{16,0},{24,8},{1,17},{9,25},{17,1},{25,9},{2,18},{10... | collective-permute-start | bytes 294920 | tf_op jit(solution)/shard_map/ppermute | solution.py:287
  49.2 7.4 %collective-permute-start.9 = (bf16[64,768]{1,0:T(8,128)(2,1)S(1)}, bf16[64,768]{1,0:T(8,128)(2,1)S(1)}, u32[]{:S(2)}, u32[]{:S(2)}) collective-permute-start(bf16[64,768]{1,0:T(8,128)(2,1)S(1)} %get-tuple-element.31), channel_id=1, source_target_pairs={{0,8},{8,0},{16,24},{24,16},{1,9},{9,1},{17,25},{25,17},{2,10},{10... | collective-permute-start | bytes 294920 | tf_op jit(solution)/shard_map/ppermute | solution.py:287
  50.9 9.3 %collective-permute-start.26 = (bf16[64,768]{1,0:T(8,128)(2,1)S(1)}, bf16[64,768]{1,0:T(8,128)(2,1)S(1)}, u32[]{:S(2)}, u32[]{:S(2)}) collective-permute-start(bf16[64,768]{1,0:T(8,128)(2,1)S(1)} %shard_map.68.refs_0_), channel_id=1, source_target_pairs={{0,2},{1,3},{2,0},{3,1},{4,6},{5,7},{6,4},{7,5},{8,10},{9,11},{10,... | collective-permute-start | bytes 294920 | tf_op jit(solution)/shard_map/ppermute | solution.py:284
  51.7 10.5 %collective-permute-start.27 = (bf16[64,768]{1,0:T(8,128)(2,1)S(1)}, bf16[64,768]{1,0:T(8,128)(2,1)S(1)}, u32[]{:S(2)}, u32[]{:S(2)}) collective-permute-start(bf16[64,768]{1,0:T(8,128)(2,1)S(1)} %shard_map.68.refs_0_), channel_id=1, source_target_pairs={{0,4},{1,5},{2,6},{3,7},{4,0},{5,1},{6,2},{7,3},{8,12},{9,13},{10,... | collective-permute-start | bytes 294920 | tf_op jit(solution)/shard_map/ppermute | solution.py:284
  56.6 9.3 %copy-start.3 = (s32[8]{0:T(128)S(1)}, s32[8]{0:T(128)}, u32[]{:S(2)}) copy-start(s32[8]{0:T(128)} %constant.12.clone) | copy-start | bytes 100
  56.6 9.3 %copy-start.1 = (bf16[768,1024]{1,0:T(8,128)(2,1)S(1)}, bf16[768,1024]{1,0:T(8,128)(2,1)}, u32[]{:S(2)}) copy-start(bf16[768,1024]{1,0:T(8,128)(2,1)} %refs_3_.3) | copy-start | bytes 4718596
  56.7 5.6 %collective-permute-start.10 = (bf16[64,768]{1,0:T(8,128)(2,1)S(1)}, bf16[64,768]{1,0:T(8,128)(2,1)S(1)}, u32[]{:S(2)}, u32[]{:S(2)}) collective-permute-start(bf16[64,768]{1,0:T(8,128)(2,1)S(1)} %shard_map.64.refs_0_), channel_id=1, source_target_pairs={{0,2},{1,3},{2,0},{3,1},{4,6},{5,7},{6,4},{7,5},{8,10},{9,11},{10,... | collective-permute-start | bytes 294920 | tf_op jit(solution)/shard_map/ppermute | solution.py:284
  57.6 7.8 %collective-permute-start.11 = (bf16[64,768]{1,0:T(8,128)(2,1)S(1)}, bf16[64,768]{1,0:T(8,128)(2,1)S(1)}, u32[]{:S(2)}, u32[]{:S(2)}) collective-permute-start(bf16[64,768]{1,0:T(8,128)(2,1)S(1)} %shard_map.64.refs_0_), channel_id=1, source_target_pairs={{0,4},{1,5},{2,6},{3,7},{4,0},{5,1},{6,2},{7,3},{8,12},{9,13},{10,... | collective-permute-start | bytes 294920 | tf_op jit(solution)/shard_map/ppermute | solution.py:284
  59.3 6.1 %collective-permute-start.12 = (bf16[64,768]{1,0:T(8,128)(2,1)S(1)}, bf16[64,768]{1,0:T(8,128)(2,1)S(1)}, u32[]{:S(2)}, u32[]{:S(2)}) collective-permute-start(bf16[64,768]{1,0:T(8,128)(2,1)S(1)} %shard_map.64.refs_0_), channel_id=1, source_target_pairs={{0,6},{1,7},{2,4},{3,5},{4,2},{5,3},{6,0},{7,1},{8,14},{9,15},{10,... | collective-permute-start | bytes 294920 | tf_op jit(solution)/shard_map/ppermute | solution.py:284
  60.2 7.6 %collective-permute-start.28 = (bf16[64,768]{1,0:T(8,128)(2,1)S(1)}, bf16[64,768]{1,0:T(8,128)(2,1)S(1)}, u32[]{:S(2)}, u32[]{:S(2)}) collective-permute-start(bf16[64,768]{1,0:T(8,128)(2,1)S(1)} %shard_map.68.refs_0_), channel_id=1, source_target_pairs={{0,6},{1,7},{2,4},{3,5},{4,2},{5,3},{6,0},{7,1},{8,14},{9,15},{10,... | collective-permute-start | bytes 294920 | tf_op jit(solution)/shard_map/ppermute | solution.py:284
  62.3 5.7 %collective-permute-start.13 = (bf16[64,768]{1,0:T(8,128)(2,1)S(1)}, bf16[64,768]{1,0:T(8,128)(2,1)S(1)}, u32[]{:S(2)}, u32[]{:S(2)}) collective-permute-start(bf16[64,768]{1,0:T(8,128)(2,1)S(1)} %shard_map.64.refs_0_), channel_id=1, source_target_pairs={{0,1},{1,0},{2,3},{3,2},{4,5},{5,4},{6,7},{7,6},{8,9},{9,8},{10,11... | collective-permute-start | bytes 294920 | tf_op jit(solution)/shard_map/ppermute | solution.py:284
  62.3 6.1 %collective-permute-start.14 = (bf16[64,768]{1,0:T(8,128)(2,1)S(1)}, bf16[64,768]{1,0:T(8,128)(2,1)S(1)}, u32[]{:S(2)}, u32[]{:S(2)}) collective-permute-start(bf16[64,768]{1,0:T(8,128)(2,1)S(1)} %collective-permute-done.10.refs_1_), channel_id=1, source_target_pairs={{0,1},{1,0},{2,3},{3,2},{4,5},{5,4},{6,7},{7,6},{8,9},{9,8},{10,11... | collective-permute-start | bytes 294920 | tf_op jit(solution)/shard_map/ppermute | solution.py:284
  65.4 3.1 %collective-permute-start.15 = (bf16[64,768]{1,0:T(8,128)(2,1)S(1)}, bf16[64,768]{1,0:T(8,128)(2,1)S(1)}, u32[]{:S(2)}, u32[]{:S(2)}) collective-permute-start(bf16[64,768]{1,0:T(8,128)(2,1)S(1)} %collective-permute-done.11.refs_2_), channel_id=1, source_target_pairs={{0,1},{1,0},{2,3},{3,2},{4,5},{5,4},{6,7},{7,6},{8,9},{9,8},{10,11... | collective-permute-start | bytes 294920 | tf_op jit(solution)/shard_map/ppermute | solution.py:284
  65.5 3.4 %collective-permute-start.16 = (bf16[64,768]{1,0:T(8,128)(2,1)S(1)}, bf16[64,768]{1,0:T(8,128)(2,1)S(1)}, u32[]{:S(2)}, u32[]{:S(2)}) collective-permute-start(bf16[64,768]{1,0:T(8,128)(2,1)S(1)} %collective-permute-done.12.refs_3_), channel_id=1, source_target_pairs={{0,1},{1,0},{2,3},{3,2},{4,5},{5,4},{6,7},{7,6},{8,9},{9,8},{10,11... | collective-permute-start | bytes 294920 | tf_op jit(solution)/shard_map/ppermute | solution.py:284
  67.8 2.3 %collective-permute-start.29 = (bf16[64,768]{1,0:T(8,128)(2,1)S(1)}, bf16[64,768]{1,0:T(8,128)(2,1)S(1)}, u32[]{:S(2)}, u32[]{:S(2)}) collective-permute-start(bf16[64,768]{1,0:T(8,128)(2,1)S(1)} %shard_map.68.refs_0_), channel_id=1, source_target_pairs={{0,1},{1,0},{2,3},{3,2},{4,5},{5,4},{6,7},{7,6},{8,9},{9,8},{10,11... | collective-permute-start | bytes 294920 | tf_op jit(solution)/shard_map/ppermute | solution.py:284
  68.0 2.1 %collective-permute-start.30 = (bf16[64,768]{1,0:T(8,128)(2,1)S(1)}, bf16[64,768]{1,0:T(8,128)(2,1)S(1)}, u32[]{:S(2)}, u32[]{:S(2)}) collective-permute-start(bf16[64,768]{1,0:T(8,128)(2,1)S(1)} %collective-permute-done.26.refs_1_), channel_id=1, source_target_pairs={{0,1},{1,0},{2,3},{3,2},{4,5},{5,4},{6,7},{7,6},{8,9},{9,8},{10,11... | collective-permute-start | bytes 294920 | tf_op jit(solution)/shard_map/ppermute | solution.py:284
  68.4 1.7 %collective-permute-start.31 = (bf16[64,768]{1,0:T(8,128)(2,1)S(1)}, bf16[64,768]{1,0:T(8,128)(2,1)S(1)}, u32[]{:S(2)}, u32[]{:S(2)}) collective-permute-start(bf16[64,768]{1,0:T(8,128)(2,1)S(1)} %collective-permute-done.27.refs_2_), channel_id=1, source_target_pairs={{0,1},{1,0},{2,3},{3,2},{4,5},{5,4},{6,7},{7,6},{8,9},{9,8},{10,11... | collective-permute-start | bytes 294920 | tf_op jit(solution)/shard_map/ppermute | solution.py:284
  68.5 1.6 %collective-permute-start.32 = (bf16[64,768]{1,0:T(8,128)(2,1)S(1)}, bf16[64,768]{1,0:T(8,128)(2,1)S(1)}, u32[]{:S(2)}, u32[]{:S(2)}) collective-permute-start(bf16[64,768]{1,0:T(8,128)(2,1)S(1)} %collective-permute-done.28.refs_3_), channel_id=1, source_target_pairs={{0,1},{1,0},{2,3},{3,2},{4,5},{5,4},{6,7},{7,6},{8,9},{9,8},{10,11... | collective-permute-start | bytes 294920 | tf_op jit(solution)/shard_map/ppermute | solution.py:284

commit v3 on v2

--- a/solution.py
+++ b/solution.py
@@ -13,6 +13,7 @@
 RELAYED = (True, False)
 HINTS = (1e11, 1e11, 1e6, 1e6, 1e6)
 STATS = 8
+UNROLL = 4
 EXPERT_HINT = 1e9
 
 
@@ -42,8 +43,8 @@
     out_ref[...] = (x * scale).astype(BF16)
 
 
-def normalize(x):
-    return call(normalize_kernel, x.shape, [x], moved=4 * x.size)
+def normalize(x, hint):
+    return call(normalize_kernel, x.shape, [x], moved=4 * x.size, hint=hint)
 
 
 def partial_kernel(slots, count, *refs):
@@ -170,15 +171,24 @@
 def expert_kernel(count, first, n, each, *refs):
     xs, w_in, w_out, ys = refs[:count], refs[count], refs[count + 1], refs[count + 3 :]
 
-    @pl.loop(0, n)
-    def _(e):
-        at = pl.ds(pl.multiple_of(e * each, each), each)
-        rows = jnp.concatenate([x[at, :] for x in xs], axis=0)
-        hidden = jnp.dot(rows, w_in[first + e], preferred_element_type=F32)
-        hidden = (0.5 * hidden * (1.0 + lax.erf(hidden * 0.7071067811865476))).astype(BF16)
-        terms = jnp.dot(hidden, w_out[first + e], preferred_element_type=F32)
-        for k, y in enumerate(ys):
-            y[at, :] = terms[k * each : (k + 1) * each].astype(BF16)
+    group = next(g for g in (UNROLL, 2, 1) if n % g == 0)
+
+    @pl.loop(0, n // group)
+    def _(step):
+        hiddens = []
+        for i in range(group):
+            e = step * group + i
+            at = pl.ds(pl.multiple_of(e * each, each), each)
+            rows = jnp.concatenate([x[at, :] for x in xs], axis=0)
+            hidden = jnp.dot(rows, w_in[first + e], preferred_element_type=F32)
+            hidden = 0.5 * hidden * (1.0 + lax.erf(hidden * 0.7071067811865476))
+            hiddens.append(hidden.astype(BF16))
+        for i, hidden in enumerate(hiddens):
+            e = step * group + i
+            at = pl.ds(pl.multiple_of(e * each, each), each)
+            terms = jnp.dot(hidden, w_out[first + e], preferred_element_type=F32)
+            for k, y in enumerate(ys):
+                y[at, :] = terms[k * each : (k + 1) * each].astype(BF16)
 
 
 def experts(xs, w_in, w_out, mark, first, count):
@@ -251,7 +261,7 @@
 def last_mix(at, weights, before, blocks):
     rows, slots = weights.shape
     width = blocks[0].shape[1]
-    steps = 4
+    steps = 2
     place = pl.BlockSpec(memory_space=pltpu.VMEM)
     return pl.pallas_call(
         functools.partial(last_mix_kernel, steps),
@@ -286,8 +296,8 @@
     def over_batch(x, k):
         return lax.ppermute(x, "batch", [(i, i ^ k) for i in range(n_batch)])
 
-    other = normalize(over_token(tokens, 1))
-    own = normalize(tokens)
+    other = normalize(over_token(tokens, 1), 1e6)
+    own = normalize(tokens, 1e11)
     if slots % 128:
         weight = slot_weight.reshape(width, n_token, slots).transpose(1, 0, 2)
     else:
@@ -325,7 +335,10 @@
     total, parts = None, []
     for c in range(chunks):
         ys = experts(xs[c], expert_in, expert_out, mark, sum(counts[:c]), counts[c])
-        parts.append([over_batch(ys[k], k) if k else ys[k] for k in reversed(keys)])
+        part = []
+        for k in keys:
+            part.append(over_batch(ys[k], k) if k else ys[k])
+        parts.append(part)
     for c in range(chunks):
         rows = add_up(parts[c])
         there = [rows]

time: 72.2 us -> 70.9 us (0.982)
  Pallas kernels: 19.4 us -> 16.8 us
  waiting for transfers between devices: 14.5 us -> 15.3 us
    pallas_call x14, Pallas kernels: 17.5 us -> 14.9 us  [call(): pl.pallas_call(kernel, out_shape=[pltpu.VMEM(shape, dtype) for shape in s...]
    ppermute x12, waiting for transfers between devices: 9.88 us -> 11.3 us  [over_batch(): return lax.ppermute(x, 'batch', [(i, i ^ k) for i in range(n_batch)])]
    unnamed x28 -> x26, local copies, waits for them, and re-layouts: 2.34 us -> 1.89 us
  transfers between devices with their start and end apart: 33 -> 33, of which waited for: 9 -> 8; matrix products, arithmetic and copies ran while one was open for 0% -> 0% of each run, Pallas kernels for 22% -> 19%
where the time goes in v3:
time: 70.9 us; the launch traced here: 70.1 us
  starting transfers between devices  35.8 us (50%)
  Pallas kernels  16.8 us (24%)
  waiting for transfers between devices  15.3 us (22%)
  local copies, waits for them, and re-layouts  1.89 us (3%)
    ppermute x21, starting transfers between devices, over_token(): return lax.ppermute(x, 'token', [(i, i ^ k) for i in range(n_token)])  18 us
    ppermute x12, starting transfers between devices, over_batch(): return lax.ppermute(x, 'batch', [(i, i ^ k) for i in range(n_batch)])  17.7 us
    pallas_call x14, Pallas kernels, call(): pl.pallas_call(kernel, out_shape=[pltpu.VMEM(shape, dtype) for shape in s...  14.9 us
    ppermute x12, waiting for transfers between devices, over_batch(): return lax.ppermute(x, 'batch', [(i, i ^ k) for i in range(n_batch)])  11.3 us
    ppermute x21, waiting for transfers between devices, over_token(): return lax.ppermute(x, 'token', [(i, i ^ k) for i in range(n_token)])  3.99 us
    pallas_call x1, Pallas kernels, last_mix(): pl.pallas_call(functools.partial(last_mix_kernel, steps), out_shape=jax.S...  1.95 us
    unnamed x26, local copies, waits for them, and re-layouts  1.89 us
  transfers between devices with their start and end apart: 33, of which 8 were waited for; matrix products, arithmetic and copies ran while one was open for 0% of the time, Pallas kernels for 19%

profile of v3, /device:TPU:0, one launch (start us, length us, event | category | flops | bytes accessed | tf_op | source)
XLA Modules:
  0.0 70.1 jit_solution(14105087243156531464)
XLA Ops:
  0.0 0.5 collective-permute-start
  0.5 1.1 %copy-done.1 = bf16[512,768]{1,0:T(8,128)(2,1)S(1)} copy-done((bf16[512,768]{1,0:T(8,128)(2,1)S(1)}, bf16[512,768]{1,0:T(8,128)(2,1)}, u32[]{:S(2)}) %copy-start.1) | copy-done | bytes 786456
  1.6 0.2 shard_map.55.x_ref.refs_1_.refs_2_
  1.9 0.7 %collective-permute-done.x_ref = bf16[512,768]{1,0:T(8,128)(2,1)S(1)} collective-permute-done((bf16[512,768]{1,0:T(8,128)(2,1)}, bf16[512,768]{1,0:T(8,128)(2,1)S(1)}, u32[]{:S(2)}, u32[]{:S(2)}) %collective-permute-start) | collective-permute-done | bytes 786464 | tf_op jit(solution)/shard_map/ppermute | solution.py:294
  2.6 0.2 shard_map.57.refs_2_.refs_3_
  2.9 1.2 %shard_map.58 = (bf16[72,768]{1,0:T(8,128)(2,1)S(1)}, bf16[72,768]{1,0:T(8,128)(2,1)S(1)}) custom-call(s32[1]{0:T(128)} %bitcast.refs_0_, bf16[512,768]{1,0:T(8,128)(2,1)S(1)} %shard_map.55.x_ref.refs_1_.refs_2_, bf16[512,768]{1,0:T(8,128)(2,1)S(1)} %shard_map.57.refs_2_.refs_3_, bf16[768,1024]{1,0:T(8,128)(2,1)S(1)} %copy-done), custom_call_target="tpu_custom_call" | custom-call | flops 99999997952 | bytes 1572864 | tf_op jit(solution)/shard_map/pallas_call | solution.py:28
  4.1 3.9 %collective-permute-start.1 = (bf16[72,768]{1,0:T(8,128)(2,1)S(1)}, bf16[72,768]{1,0:T(8,128)(2,1)S(1)}, u32[]{:S(2)}, u32[]{:S(2)}) collective-permute-start(bf16[72,768]{1,0:T(8,128)(2,1)S(1)} %get-tuple-element.25), channel_id=1, source_target_pairs={{0,6},{1,7},{2,4},{3,5},{4,2},{5,3},{6,0},{7,1},{8,14},{9,15},{10,... | collective-permute-start | bytes 331784 | tf_op jit(solution)/shard_map/ppermute | solution.py:294
  7.9 1.6 %shard_map.59 = (bf16[72,768]{1,0:T(8,128)(2,1)S(1)}, bf16[72,768]{1,0:T(8,128)(2,1)S(1)}, bf16[72,768]{1,0:T(8,128)(2,1)S(1)}, bf16[72,768]{1,0:T(8,128)(2,1)S(1)}) custom-call(s32[1]{0:T(128)} %bitcast.1.refs_0_, s32[1]{0:T(128)} %bitcast.2.refs_1_, bf16[512,768]{1,0:T(8,128)(2,1)S(1)} %shard_map.55.x_ref.refs_1_.refs_2_, ...), custom_call_target="tpu_custom_call" | custom-call | flops 99999997952 | bytes 1572864 | tf_op jit(solution)/shard_map/pallas_call | solution.py:28
  9.6 0.6 collective-permute-start.2
  10.1 0.1 collective-permute-start.3
  10.2 2.9 %collective-permute-start.17 = (bf16[72,768]{1,0:T(8,128)(2,1)S(1)}, bf16[72,768]{1,0:T(8,128)(2,1)S(1)}, u32[]{:S(2)}, u32[]{:S(2)}) collective-permute-start(bf16[72,768]{1,0:T(8,128)(2,1)S(1)} %get-tuple-element.33), channel_id=1, source_target_pairs={{0,6},{1,7},{2,4},{3,5},{4,2},{5,3},{6,0},{7,1},{8,14},{9,15},{10,... | collective-permute-start | bytes 331784 | tf_op jit(solution)/shard_map/ppermute | solution.py:294
  13.1 0.5 collective-permute-start.18
  13.6 0.0 collective-permute-done.1.refs_0_
  13.6 0.1 collective-permute-start.19
  13.7 1.2 %shard_map.60 = (bf16[72,768]{1,0:T(8,128)(2,1)S(1)}, bf16[72,768]{1,0:T(8,128)(2,1)S(1)}) custom-call(s32[1]{0:T(128)} %bitcast.3.refs_0_, bf16[512,768]{1,0:T(8,128)(2,1)S(1)} %shard_map.55.x_ref.refs_1_.refs_2_, bf16[512,768]{1,0:T(8,128)(2,1)S(1)} %shard_map.57.refs_2_.refs_3_, bf16[768,1024]{1,0:T(8,128)(2,1)S(1)} %copy-done), custom_call_target="tpu_custom_call" | custom-call | flops 1000000 | bytes 1572864 | tf_op jit(solution)/shard_map/pallas_call | solution.py:28
  14.9 1.1 %collective-permute-done.3.refs_2_ = bf16[72,768]{1,0:T(8,128)(2,1)S(1)} collective-permute-done((bf16[72,768]{1,0:T(8,128)(2,1)S(1)}, bf16[72,768]{1,0:T(8,128)(2,1)S(1)}, u32[]{:S(2)}, u32[]{:S(2)}) %collective-permute-start.3) | collective-permute-done | bytes 110624 | tf_op jit(solution)/shard_map/ppermute | solution.py:294
  16.1 0.2 shard_map.61.x_ref.refs_0_
  16.2 1.6 %collective-permute-start.4 = (bf16[64,768]{1,0:T(8,128)(2,1)S(1)}, bf16[64,768]{1,0:T(8,128)(2,1)S(1)}, u32[]{:S(2)}, u32[]{:S(2)}) collective-permute-start(bf16[64,768]{1,0:T(8,128)(2,1)S(1)} %shard_map.61.x_ref.refs_0_), channel_id=1, source_target_pairs={{0,8},{8,0},{16,24},{24,16},{1,9},{9,1},{17,25},{25,17},{2,10},{10... | collective-permute-start | bytes 294920 | tf_op jit(solution)/shard_map/ppermute | solution.py:297
  17.9 2.6 %collective-permute-start.5 = (bf16[64,768]{1,0:T(8,128)(2,1)S(1)}, bf16[64,768]{1,0:T(8,128)(2,1)S(1)}, u32[]{:S(2)}, u32[]{:S(2)}) collective-permute-start(bf16[64,768]{1,0:T(8,128)(2,1)S(1)} %shard_map.61.x_ref.refs_0_), channel_id=1, source_target_pairs={{0,16},{8,24},{16,0},{24,8},{1,17},{9,25},{17,1},{25,9},{2,18},{10... | collective-permute-start | bytes 294920 | tf_op jit(solution)/shard_map/ppermute | solution.py:297
  20.5 0.0 collective-permute-done.17.refs_0_
  20.5 0.0 collective-permute-done.18.refs_1_
  20.5 0.0 collective-permute-done.19.refs_2_
  20.5 0.0 slice-start
  20.5 0.0 slice-start.5
  20.5 0.2 shard_map.66.refs_0_
  20.7 0.0 slice-start.1
  20.7 0.0 slice-start.2
  20.7 0.0 slice-start.6
  20.8 0.6 collective-permute-start.20
  21.4 2.6 %collective-permute-start.21 = (bf16[64,768]{1,0:T(8,128)(2,1)S(1)}, bf16[64,768]{1,0:T(8,128)(2,1)S(1)}, u32[]{:S(2)}, u32[]{:S(2)}) collective-permute-start(bf16[64,768]{1,0:T(8,128)(2,1)S(1)} %shard_map.66.refs_0_), channel_id=1, source_target_pairs={{0,16},{8,24},{16,0},{24,8},{1,17},{9,25},{17,1},{25,9},{2,18},{10... | collective-permute-start | bytes 294920 | tf_op jit(solution)/shard_map/ppermute | solution.py:297
  23.9 1.3 %collective-permute-start.22 = (bf16[64,768]{1,0:T(8,128)(2,1)S(1)}, bf16[64,768]{1,0:T(8,128)(2,1)S(1)}, u32[]{:S(2)}, u32[]{:S(2)}) collective-permute-start(bf16[64,768]{1,0:T(8,128)(2,1)S(1)} %shard_map.66.refs_0_), channel_id=1, source_target_pairs={{0,24},{8,16},{16,8},{24,0},{1,25},{9,17},{17,9},{25,1},{2,26},{10... | collective-permute-start | bytes 294920 | tf_op jit(solution)/shard_map/ppermute | solution.py:297
  25.2 0.2 collective-permute-start.6
  25.4 2.9 %collective-permute-done.20.refs_1_ = bf16[64,768]{1,0:T(8,128)(2,1)S(1)} collective-permute-done((bf16[64,768]{1,0:T(8,128)(2,1)S(1)}, bf16[64,768]{1,0:T(8,128)(2,1)S(1)}, u32[]{:S(2)}, u32[]{:S(2)}) %collective-permute-start.20) | collective-permute-done | bytes 98336 | tf_op jit(solution)/shard_map/ppermute | solution.py:297
  28.3 3.3 %collective-permute-done.21.refs_2_ = bf16[64,768]{1,0:T(8,128)(2,1)S(1)} collective-permute-done((bf16[64,768]{1,0:T(8,128)(2,1)S(1)}, bf16[64,768]{1,0:T(8,128)(2,1)S(1)}, u32[]{:S(2)}, u32[]{:S(2)}) %collective-permute-start.21) | collective-permute-done | bytes 98336 | tf_op jit(solution)/shard_map/ppermute | solution.py:297
  31.7 0.7 slice-done.9
  32.4 3.5 %shard_map.67 = (bf16[64,768]{1,0:T(8,128)(2,1)S(1)}, bf16[64,768]{1,0:T(8,128)(2,1)S(1)}, bf16[64,768]{1,0:T(8,128)(2,1)S(1)}, bf16[64,768]{1,0:T(8,128)(2,1)S(1)}) custom-call(bf16[64,768]{1,0:T(8,128)(2,1)S(1)} %shard_map.66.refs_0_, bf16[64,768]{1,0:T(8,128)(2,1)S(1)} %collective-permute-done.20.refs_1_, ...), custom_call_target="tpu_custom_call" | custom-call | flops 1000000000 | bytes 1 | tf_op jit(solution)/shard_map/pallas_call | solution.py:28
  35.8 1.2 %collective-permute-start.23 = (bf16[64,768]{1,0:T(8,128)(2,1)S(1)}, bf16[64,768]{1,0:T(8,128)(2,1)S(1)}, u32[]{:S(2)}, u32[]{:S(2)}) collective-permute-start(bf16[64,768]{1,0:T(8,128)(2,1)S(1)} %get-tuple-element.38), channel_id=1, source_target_pairs={{0,8},{8,0},{16,24},{24,16},{1,9},{9,1},{17,25},{25,17},{2,10},{10... | collective-permute-start | bytes 294920 | tf_op jit(solution)/shard_map/ppermute | solution.py:297
  37.0 2.0 %collective-permute-start.24 = (bf16[64,768]{1,0:T(8,128)(2,1)S(1)}, bf16[64,768]{1,0:T(8,128)(2,1)S(1)}, u32[]{:S(2)}, u32[]{:S(2)}) collective-permute-start(bf16[64,768]{1,0:T(8,128)(2,1)S(1)} %get-tuple-element.39), channel_id=1, source_target_pairs={{0,16},{8,24},{16,0},{24,8},{1,17},{9,25},{17,1},{25,9},{2,18},{10... | collective-permute-start | bytes 294920 | tf_op jit(solution)/shard_map/ppermute | solution.py:297
  39.0 1.3 %collective-permute-start.25 = (bf16[64,768]{1,0:T(8,128)(2,1)S(1)}, bf16[64,768]{1,0:T(8,128)(2,1)S(1)}, u32[]{:S(2)}, u32[]{:S(2)}) collective-permute-start(bf16[64,768]{1,0:T(8,128)(2,1)S(1)} %get-tuple-element.40), channel_id=1, source_target_pairs={{0,24},{8,16},{16,8},{24,0},{1,25},{9,17},{17,9},{25,1},{2,26},{10... | collective-permute-start | bytes 294920 | tf_op jit(solution)/shard_map/ppermute | solution.py:297
  40.3 3.5 %shard_map.63 = (bf16[64,768]{1,0:T(8,128)(2,1)S(1)}, bf16[64,768]{1,0:T(8,128)(2,1)S(1)}, bf16[64,768]{1,0:T(8,128)(2,1)S(1)}, bf16[64,768]{1,0:T(8,128)(2,1)S(1)}) custom-call(bf16[64,768]{1,0:T(8,128)(2,1)S(1)} %shard_map.61.x_ref.refs_0_, bf16[64,768]{1,0:T(8,128)(2,1)S(1)} %collective-permute-done.4.refs_1_, ...), custom_call_target="tpu_custom_call" | custom-call | flops 1000000000 | bytes 1 | tf_op jit(solution)/shard_map/pallas_call | solution.py:28
  43.7 0.3 collective-permute-start.7
  44.0 2.8 %collective-permute-start.8 = (bf16[64,768]{1,0:T(8,128)(2,1)S(1)}, bf16[64,768]{1,0:T(8,128)(2,1)S(1)}, u32[]{:S(2)}, u32[]{:S(2)}) collective-permute-start(bf16[64,768]{1,0:T(8,128)(2,1)S(1)} %get-tuple-element.31), channel_id=1, source_target_pairs={{0,16},{8,24},{16,0},{24,8},{1,17},{9,25},{17,1},{25,9},{2,18},{10... | collective-permute-start | bytes 294920 | tf_op jit(solution)/shard_map/ppermute | solution.py:297
  46.9 1.3 %collective-permute-start.9 = (bf16[64,768]{1,0:T(8,128)(2,1)S(1)}, bf16[64,768]{1,0:T(8,128)(2,1)S(1)}, u32[]{:S(2)}, u32[]{:S(2)}) collective-permute-start(bf16[64,768]{1,0:T(8,128)(2,1)S(1)} %get-tuple-element.32), channel_id=1, source_target_pairs={{0,24},{8,16},{16,8},{24,0},{1,25},{9,17},{17,9},{25,1},{2,26},{10... | collective-permute-start | bytes 294920 | tf_op jit(solution)/shard_map/ppermute | solution.py:297
  48.2 0.2 collective-permute-done.24.refs_2_
  48.4 0.1 shard_map.68.refs_0_
  48.5 0.8 %collective-permute-start.26 = (bf16[64,768]{1,0:T(8,128)(2,1)S(1)}, bf16[64,768]{1,0:T(8,128)(2,1)S(1)}, u32[]{:S(2)}, u32[]{:S(2)}) collective-permute-start(bf16[64,768]{1,0:T(8,128)(2,1)S(1)} %shard_map.68.refs_0_), channel_id=1, source_target_pairs={{0,2},{1,3},{2,0},{3,1},{4,6},{5,7},{6,4},{7,5},{8,10},{9,11},{10,... | collective-permute-start | bytes 294920 | tf_op jit(solution)/shard_map/ppermute | solution.py:294
  49.3 1.3 %collective-permute-start.27 = (bf16[64,768]{1,0:T(8,128)(2,1)S(1)}, bf16[64,768]{1,0:T(8,128)(2,1)S(1)}, u32[]{:S(2)}, u32[]{:S(2)}) collective-permute-start(bf16[64,768]{1,0:T(8,128)(2,1)S(1)} %shard_map.68.refs_0_), channel_id=1, source_target_pairs={{0,4},{1,5},{2,6},{3,7},{4,0},{5,1},{6,2},{7,3},{8,12},{9,13},{10,... | collective-permute-start | bytes 294920 | tf_op jit(solution)/shard_map/ppermute | solution.py:294
  50.6 4.9 %collective-permute-done.8.refs_2_ = bf16[64,768]{1,0:T(8,128)(2,1)S(1)} collective-permute-done((bf16[64,768]{1,0:T(8,128)(2,1)S(1)}, bf16[64,768]{1,0:T(8,128)(2,1)S(1)}, u32[]{:S(2)}, u32[]{:S(2)}) %collective-permute-start.8) | collective-permute-done | bytes 98336 | tf_op jit(solution)/shard_map/ppermute | solution.py:297
  55.5 0.1 shard_map.64.refs_0_
  55.5 0.8 %collective-permute-start.10 = (bf16[64,768]{1,0:T(8,128)(2,1)S(1)}, bf16[64,768]{1,0:T(8,128)(2,1)S(1)}, u32[]{:S(2)}, u32[]{:S(2)}) collective-permute-start(bf16[64,768]{1,0:T(8,128)(2,1)S(1)} %shard_map.64.refs_0_), channel_id=1, source_target_pairs={{0,2},{1,3},{2,0},{3,1},{4,6},{5,7},{6,4},{7,5},{8,10},{9,11},{10,... | collective-permute-start | bytes 294920 | tf_op jit(solution)/shard_map/ppermute | solution.py:294
  56.3 2.0 %collective-permute-start.11 = (bf16[64,768]{1,0:T(8,128)(2,1)S(1)}, bf16[64,768]{1,0:T(8,128)(2,1)S(1)}, u32[]{:S(2)}, u32[]{:S(2)}) collective-permute-start(bf16[64,768]{1,0:T(8,128)(2,1)S(1)} %shard_map.64.refs_0_), channel_id=1, source_target_pairs={{0,4},{1,5},{2,6},{3,7},{4,0},{5,1},{6,2},{7,3},{8,12},{9,13},{10,... | collective-permute-start | bytes 294920 | tf_op jit(solution)/shard_map/ppermute | solution.py:294
  58.3 0.8 %collective-permute-start.12 = (bf16[64,768]{1,0:T(8,128)(2,1)S(1)}, bf16[64,768]{1,0:T(8,128)(2,1)S(1)}, u32[]{:S(2)}, u32[]{:S(2)}) collective-permute-start(bf16[64,768]{1,0:T(8,128)(2,1)S(1)} %shard_map.64.refs_0_), channel_id=1, source_target_pairs={{0,6},{1,7},{2,4},{3,5},{4,2},{5,3},{6,0},{7,1},{8,14},{9,15},{10,... | collective-permute-start | bytes 294920 | tf_op jit(solution)/shard_map/ppermute | solution.py:294
  59.1 2.2 %collective-permute-start.28 = (bf16[64,768]{1,0:T(8,128)(2,1)S(1)}, bf16[64,768]{1,0:T(8,128)(2,1)S(1)}, u32[]{:S(2)}, u32[]{:S(2)}) collective-permute-start(bf16[64,768]{1,0:T(8,128)(2,1)S(1)} %shard_map.68.refs_0_), channel_id=1, source_target_pairs={{0,6},{1,7},{2,4},{3,5},{4,2},{5,3},{6,0},{7,1},{8,14},{9,15},{10,... | collective-permute-start | bytes 294920 | tf_op jit(solution)/shard_map/ppermute | solution.py:294
  61.3 0.5 collective-permute-start.14
  61.8 0.3 collective-permute-done.11.refs_2_
  62.1 1.7 %collective-permute-done.12.refs_3_ = bf16[64,768]{1,0:T(8,128)(2,1)S(1)} collective-permute-done((bf16[64,768]{1,0:T(8,128)(2,1)S(1)}, bf16[64,768]{1,0:T(8,128)(2,1)S(1)}, u32[]{:S(2)}, u32[]{:S(2)}) %collective-permute-start.12) | collective-permute-done | bytes 98336 | tf_op jit(solution)/shard_map/ppermute | solution.py:294
  63.8 1.9 %shard_map.56 = (bf16[512,512]{1,0:T(8,128)(2,1)S(1)}, bf16[512,512]{1,0:T(8,128)(2,1)S(1)}) custom-call(bf16[512,768]{1,0:T(8,128)(2,1)S(1)} %shard_map.55.x_ref.refs_1_.refs_2_, bf16[768,1024]{1,0:T(8,128)(2,1)S(1)} %copy-done), custom_call_target="tpu_custom_call" | custom-call | flops 1000000 | bytes 3407872 | tf_op jit(solution)/shard_map/pallas_call | solution.py:28
  65.8 0.6 collective-permute-start.29
  66.3 0.1 collective-permute-start.30
  66.4 0.4 collective-permute-start.31
  66.9 0.1 collective-permute-start.32
  66.9 1.2 %shard_map.65.sum_ref = f32[512,768]{1,0:T(8,128)S(1)} custom-call(s32[8]{0:T(128)S(1)} %broadcast_xor_fusion.at_ref, bf16[512,512]{1,0:T(8,128)(2,1)S(1)} %get-tuple-element.24.c_ref, bf16[64,768]{1,0:T(8,128)(2,1)S(1)} %shard_map.64.refs_0_, bf16[64,768]{1,0:T(8,128)(2,1)S(1)} %collective-permute-done.10.refs_1_, ...), custom_call_target="tpu_custom_call" | custom-call | flops 99999997952 | bytes 2097152 | tf_op jit(solution)/shard_map/pallas_call | solution.py:28
  68.1 0.0 collective-permute-done.32.refs_7_
  68.2 2.0 %last_mix.1 = bf16[512,768]{1,0:T(8,128)(2,1)} custom-call(s32[8]{0:T(128)S(1)} %broadcast_xor_fusion.at_ref, bf16[512,512]{1,0:T(8,128)(2,1)S(1)} %get-tuple-element.23.c_ref, f32[512,768]{1,0:T(8,128)S(1)} %shard_map.65.sum_ref, bf16[64,768]{1,0:T(8,128)(2,1)S(1)} %shard_map.68.refs_0_, bf16[64,768]{1,0:T(8,128)(2,1)S(1)} %collective-permute-done.26.refs_1_, ...), custom_call_target="tpu_custom_call" | custom-call | tf_op jit(solution)/shard_map/last_mix/pallas_call | solution.py:266
  (46 shorter events, 0.1 us)
Async XLA Ops:
  0.0 2.9 %copy-start = (bf16[768,1024]{1,0:T(8,128)(2,1)S(1)}, bf16[768,1024]{1,0:T(8,128)(2,1)}, u32[]{:S(2)}) copy-start(bf16[768,1024]{1,0:T(8,128)(2,1)} %refs_3_.3) | copy-start | bytes 4718596
  0.0 2.6 %collective-permute-start = (bf16[512,768]{1,0:T(8,128)(2,1)}, bf16[512,768]{1,0:T(8,128)(2,1)S(1)}, u32[]{:S(2)}, u32[]{:S(2)}) collective-permute-start(bf16[512,768]{1,0:T(8,128)(2,1)} %x_ref.1), channel_id=1, source_target_pairs={{0,1},{1,0},{2,3},{3,2},{4,5},{5,4},{6,7},{7,6},{8,9},{9,8},{10,11... | collective-permute-start | bytes 2359304 | tf_op jit(solution)/shard_map/ppermute | solution.py:294
  0.5 1.1 %copy-start.1 = (bf16[512,768]{1,0:T(8,128)(2,1)S(1)}, bf16[512,768]{1,0:T(8,128)(2,1)}, u32[]{:S(2)}) copy-start(bf16[512,768]{1,0:T(8,128)(2,1)} %x_ref.1) | copy-start | bytes 2359300
  4.1 9.6 %collective-permute-start.1 = (bf16[72,768]{1,0:T(8,128)(2,1)S(1)}, bf16[72,768]{1,0:T(8,128)(2,1)S(1)}, u32[]{:S(2)}, u32[]{:S(2)}) collective-permute-start(bf16[72,768]{1,0:T(8,128)(2,1)S(1)} %get-tuple-element.25), channel_id=1, source_target_pairs={{0,6},{1,7},{2,4},{3,5},{4,2},{5,3},{6,0},{7,1},{8,14},{9,15},{10,... | collective-permute-start | bytes 331784 | tf_op jit(solution)/shard_map/ppermute | solution.py:294
  9.6 5.3 %collective-permute-start.2 = (bf16[72,768]{1,0:T(8,128)(2,1)S(1)}, bf16[72,768]{1,0:T(8,128)(2,1)S(1)}, u32[]{:S(2)}, u32[]{:S(2)}) collective-permute-start(bf16[72,768]{1,0:T(8,128)(2,1)S(1)} %get-tuple-element.26), channel_id=1, source_target_pairs={{0,4},{1,5},{2,6},{3,7},{4,0},{5,1},{6,2},{7,3},{8,12},{9,13},{10,... | collective-permute-start | bytes 331784 | tf_op jit(solution)/shard_map/ppermute | solution.py:294
  10.1 5.9 %collective-permute-start.3 = (bf16[72,768]{1,0:T(8,128)(2,1)S(1)}, bf16[72,768]{1,0:T(8,128)(2,1)S(1)}, u32[]{:S(2)}, u32[]{:S(2)}) collective-permute-start(bf16[72,768]{1,0:T(8,128)(2,1)S(1)} %get-tuple-element.27), channel_id=1, source_target_pairs={{0,2},{1,3},{2,0},{3,1},{4,6},{5,7},{6,4},{7,5},{8,10},{9,11},{10,... | collective-permute-start | bytes 331784 | tf_op jit(solution)/shard_map/ppermute | solution.py:294
  10.2 10.2 %collective-permute-start.17 = (bf16[72,768]{1,0:T(8,128)(2,1)S(1)}, bf16[72,768]{1,0:T(8,128)(2,1)S(1)}, u32[]{:S(2)}, u32[]{:S(2)}) collective-permute-start(bf16[72,768]{1,0:T(8,128)(2,1)S(1)} %get-tuple-element.33), channel_id=1, source_target_pairs={{0,6},{1,7},{2,4},{3,5},{4,2},{5,3},{6,0},{7,1},{8,14},{9,15},{10,... | collective-permute-start | bytes 331784 | tf_op jit(solution)/shard_map/ppermute | solution.py:294
  13.1 7.4 %collective-permute-start.18 = (bf16[72,768]{1,0:T(8,128)(2,1)S(1)}, bf16[72,768]{1,0:T(8,128)(2,1)S(1)}, u32[]{:S(2)}, u32[]{:S(2)}) collective-permute-start(bf16[72,768]{1,0:T(8,128)(2,1)S(1)} %get-tuple-element.34), channel_id=1, source_target_pairs={{0,4},{1,5},{2,6},{3,7},{4,0},{5,1},{6,2},{7,3},{8,12},{9,13},{10,... | collective-permute-start | bytes 331784 | tf_op jit(solution)/shard_map/ppermute | solution.py:294
  13.6 6.9 %collective-permute-start.19 = (bf16[72,768]{1,0:T(8,128)(2,1)S(1)}, bf16[72,768]{1,0:T(8,128)(2,1)S(1)}, u32[]{:S(2)}, u32[]{:S(2)}) collective-permute-start(bf16[72,768]{1,0:T(8,128)(2,1)S(1)} %get-tuple-element.35), channel_id=1, source_target_pairs={{0,2},{1,3},{2,0},{3,1},{4,6},{5,7},{6,4},{7,5},{8,10},{9,11},{10,... | collective-permute-start | bytes 331784 | tf_op jit(solution)/shard_map/ppermute | solution.py:294
  16.2 24.0 %collective-permute-start.4 = (bf16[64,768]{1,0:T(8,128)(2,1)S(1)}, bf16[64,768]{1,0:T(8,128)(2,1)S(1)}, u32[]{:S(2)}, u32[]{:S(2)}) collective-permute-start(bf16[64,768]{1,0:T(8,128)(2,1)S(1)} %shard_map.61.x_ref.refs_0_), channel_id=1, source_target_pairs={{0,8},{8,0},{16,24},{24,16},{1,9},{9,1},{17,25},{25,17},{2,10},{10... | collective-permute-start | bytes 294920 | tf_op jit(solution)/shard_map/ppermute | solution.py:297
  17.9 7.4 %collective-permute-start.5 = (bf16[64,768]{1,0:T(8,128)(2,1)S(1)}, bf16[64,768]{1,0:T(8,128)(2,1)S(1)}, u32[]{:S(2)}, u32[]{:S(2)}) collective-permute-start(bf16[64,768]{1,0:T(8,128)(2,1)S(1)} %shard_map.61.x_ref.refs_0_), channel_id=1, source_target_pairs={{0,16},{8,24},{16,0},{24,8},{1,17},{9,25},{17,1},{25,9},{2,18},{10... | collective-permute-start | bytes 294920 | tf_op jit(solution)/shard_map/ppermute | solution.py:297
  20.5 11.1 %slice-start = ((s8[18874368]{0:T(1024)(128)(4,1)}), s8[4194304]{0:T(1024)(128)(4,1)S(1)}, s32[]{:S(2)}) async-start(s8[18874368]{0:T(1024)(128)(4,1)} %bitcast.4), calls=%async_computation | async-start | bytes 8388608
  20.5 11.1 %slice-start.5 = ((s8[18874368]{0:T(1024)(128)(4,1)}), s8[2097152]{0:T(1024)(128)(4,1)S(1)}, s32[]{:S(2)}) async-start(s8[18874368]{0:T(1024)(128)(4,1)} %bitcast.6), calls=%async_computation.5 | async-start | bytes 4194304
  20.7 10.9 %slice-start.1 = ((s8[18874368]{0:T(1024)(128)(4,1)}), s8[4194304]{0:T(1024)(128)(4,1)S(1)}, s32[]{:S(2)}) async-start(s8[18874368]{0:T(1024)(128)(4,1)} %bitcast.4), calls=%async_computation.1 | async-start | bytes 8388608
  20.7 10.9 %slice-start.2 = ((s8[18874368]{0:T(1024)(128)(4,1)}), s8[4194304]{0:T(1024)(128)(4,1)S(1)}, s32[]{:S(2)}) async-start(s8[18874368]{0:T(1024)(128)(4,1)} %bitcast.4), calls=%async_computation.2 | async-start | bytes 8388608
  20.7 10.9 %slice-start.3 = ((s8[18874368]{0:T(1024)(128)(4,1)}), s8[4194304]{0:T(1024)(128)(4,1)S(1)}, s32[]{:S(2)}) async-start(s8[18874368]{0:T(1024)(128)(4,1)} %bitcast.4), calls=%async_computation.3 | async-start | bytes 8388608
  20.7 10.9 %slice-start.4 = ((s8[18874368]{0:T(1024)(128)(4,1)}), s8[2097152]{0:T(1024)(128)(4,1)S(1)}, s32[]{:S(2)}) async-start(s8[18874368]{0:T(1024)(128)(4,1)} %bitcast.4), calls=%async_computation.4 | async-start | bytes 4194304
  20.7 10.9 %slice-start.6 = ((s8[18874368]{0:T(1024)(128)(4,1)}), s8[4194304]{0:T(1024)(128)(4,1)S(1)}, s32[]{:S(2)}) async-start(s8[18874368]{0:T(1024)(128)(4,1)} %bitcast.6), calls=%async_computation.6 | async-start | bytes 8388608
  20.7 10.9 %slice-start.7 = ((s8[18874368]{0:T(1024)(128)(4,1)}), s8[4194304]{0:T(1024)(128)(4,1)S(1)}, s32[]{:S(2)}) async-start(s8[18874368]{0:T(1024)(128)(4,1)} %bitcast.6), calls=%async_computation.7 | async-start | bytes 8388608
  20.8 10.9 %slice-start.8 = ((s8[18874368]{0:T(1024)(128)(4,1)}), s8[4194304]{0:T(1024)(128)(4,1)S(1)}, s32[]{:S(2)}) async-start(s8[18874368]{0:T(1024)(128)(4,1)} %bitcast.6), calls=%async_computation.8 | async-start | bytes 8388608
  20.8 11.6 %slice-start.9 = ((s8[18874368]{0:T(1024)(128)(4,1)}), s8[4194304]{0:T(1024)(128)(4,1)S(1)}, s32[]{:S(2)}) async-start(s8[18874368]{0:T(1024)(128)(4,1)} %bitcast.6), calls=%async_computation.9 | async-start | bytes 8388608
  20.8 7.6 %collective-permute-start.20 = (bf16[64,768]{1,0:T(8,128)(2,1)S(1)}, bf16[64,768]{1,0:T(8,128)(2,1)S(1)}, u32[]{:S(2)}, u32[]{:S(2)}) collective-permute-start(bf16[64,768]{1,0:T(8,128)(2,1)S(1)} %shard_map.66.refs_0_), channel_id=1, source_target_pairs={{0,8},{8,0},{16,24},{24,16},{1,9},{9,1},{17,25},{25,17},{2,10},{10... | collective-permute-start | bytes 294920 | tf_op jit(solution)/shard_map/ppermute | solution.py:297
  21.4 10.2 %collective-permute-start.21 = (bf16[64,768]{1,0:T(8,128)(2,1)S(1)}, bf16[64,768]{1,0:T(8,128)(2,1)S(1)}, u32[]{:S(2)}, u32[]{:S(2)}) collective-permute-start(bf16[64,768]{1,0:T(8,128)(2,1)S(1)} %shard_map.66.refs_0_), channel_id=1, source_target_pairs={{0,16},{8,24},{16,0},{24,8},{1,17},{9,25},{17,1},{25,9},{2,18},{10... | collective-permute-start | bytes 294920 | tf_op jit(solution)/shard_map/ppermute | solution.py:297
  23.9 7.7 %collective-permute-start.22 = (bf16[64,768]{1,0:T(8,128)(2,1)S(1)}, bf16[64,768]{1,0:T(8,128)(2,1)S(1)}, u32[]{:S(2)}, u32[]{:S(2)}) collective-permute-start(bf16[64,768]{1,0:T(8,128)(2,1)S(1)} %shard_map.66.refs_0_), channel_id=1, source_target_pairs={{0,24},{8,16},{16,8},{24,0},{1,25},{9,17},{17,9},{25,1},{2,26},{10... | collective-permute-start | bytes 294920 | tf_op jit(solution)/shard_map/ppermute | solution.py:297
  25.2 15.0 %collective-permute-start.6 = (bf16[64,768]{1,0:T(8,128)(2,1)S(1)}, bf16[64,768]{1,0:T(8,128)(2,1)S(1)}, u32[]{:S(2)}, u32[]{:S(2)}) collective-permute-start(bf16[64,768]{1,0:T(8,128)(2,1)S(1)} %collective-permute-done.5.refs_2_), channel_id=1, source_target_pairs={{0,8},{8,0},{16,24},{24,16},{1,9},{9,1},{17,25},{25,17},{2,10},{10... | collective-permute-start | bytes 294920 | tf_op jit(solution)/shard_map/ppermute | solution.py:297
  35.8 11.0 %collective-permute-start.23 = (bf16[64,768]{1,0:T(8,128)(2,1)S(1)}, bf16[64,768]{1,0:T(8,128)(2,1)S(1)}, u32[]{:S(2)}, u32[]{:S(2)}) collective-permute-start(bf16[64,768]{1,0:T(8,128)(2,1)S(1)} %get-tuple-element.38), channel_id=1, source_target_pairs={{0,8},{8,0},{16,24},{24,16},{1,9},{9,1},{17,25},{25,17},{2,10},{10... | collective-permute-start | bytes 294920 | tf_op jit(solution)/shard_map/ppermute | solution.py:297
  37.0 11.4 %collective-permute-start.24 = (bf16[64,768]{1,0:T(8,128)(2,1)S(1)}, bf16[64,768]{1,0:T(8,128)(2,1)S(1)}, u32[]{:S(2)}, u32[]{:S(2)}) collective-permute-start(bf16[64,768]{1,0:T(8,128)(2,1)S(1)} %get-tuple-element.39), channel_id=1, source_target_pairs={{0,16},{8,24},{16,0},{24,8},{1,17},{9,25},{17,1},{25,9},{2,18},{10... | collective-permute-start | bytes 294920 | tf_op jit(solution)/shard_map/ppermute | solution.py:297
  39.0 9.4 %collective-permute-start.25 = (bf16[64,768]{1,0:T(8,128)(2,1)S(1)}, bf16[64,768]{1,0:T(8,128)(2,1)S(1)}, u32[]{:S(2)}, u32[]{:S(2)}) collective-permute-start(bf16[64,768]{1,0:T(8,128)(2,1)S(1)} %get-tuple-element.40), channel_id=1, source_target_pairs={{0,24},{8,16},{16,8},{24,0},{1,25},{9,17},{17,9},{25,1},{2,26},{10... | collective-permute-start | bytes 294920 | tf_op jit(solution)/shard_map/ppermute | solution.py:297
  43.7 6.9 %collective-permute-start.7 = (bf16[64,768]{1,0:T(8,128)(2,1)S(1)}, bf16[64,768]{1,0:T(8,128)(2,1)S(1)}, u32[]{:S(2)}, u32[]{:S(2)}) collective-permute-start(bf16[64,768]{1,0:T(8,128)(2,1)S(1)} %get-tuple-element.30), channel_id=1, source_target_pairs={{0,8},{8,0},{16,24},{24,16},{1,9},{9,1},{17,25},{25,17},{2,10},{10... | collective-permute-start | bytes 294920 | tf_op jit(solution)/shard_map/ppermute | solution.py:297
  44.0 11.4 %collective-permute-start.8 = (bf16[64,768]{1,0:T(8,128)(2,1)S(1)}, bf16[64,768]{1,0:T(8,128)(2,1)S(1)}, u32[]{:S(2)}, u32[]{:S(2)}) collective-permute-start(bf16[64,768]{1,0:T(8,128)(2,1)S(1)} %get-tuple-element.31), channel_id=1, source_target_pairs={{0,16},{8,24},{16,0},{24,8},{1,17},{9,25},{17,1},{25,9},{2,18},{10... | collective-permute-start | bytes 294920 | tf_op jit(solution)/shard_map/ppermute | solution.py:297
  46.9 8.6 %collective-permute-start.9 = (bf16[64,768]{1,0:T(8,128)(2,1)S(1)}, bf16[64,768]{1,0:T(8,128)(2,1)S(1)}, u32[]{:S(2)}, u32[]{:S(2)}) collective-permute-start(bf16[64,768]{1,0:T(8,128)(2,1)S(1)} %get-tuple-element.32), channel_id=1, source_target_pairs={{0,24},{8,16},{16,8},{24,0},{1,25},{9,17},{17,9},{25,1},{2,26},{10... | collective-permute-start | bytes 294920 | tf_op jit(solution)/shard_map/ppermute | solution.py:297
  48.5 10.6 %collective-permute-start.26 = (bf16[64,768]{1,0:T(8,128)(2,1)S(1)}, bf16[64,768]{1,0:T(8,128)(2,1)S(1)}, u32[]{:S(2)}, u32[]{:S(2)}) collective-permute-start(bf16[64,768]{1,0:T(8,128)(2,1)S(1)} %shard_map.68.refs_0_), channel_id=1, source_target_pairs={{0,2},{1,3},{2,0},{3,1},{4,6},{5,7},{6,4},{7,5},{8,10},{9,11},{10,... | collective-permute-start | bytes 294920 | tf_op jit(solution)/shard_map/ppermute | solution.py:294
  49.3 12.0 %collective-permute-start.27 = (bf16[64,768]{1,0:T(8,128)(2,1)S(1)}, bf16[64,768]{1,0:T(8,128)(2,1)S(1)}, u32[]{:S(2)}, u32[]{:S(2)}) collective-permute-start(bf16[64,768]{1,0:T(8,128)(2,1)S(1)} %shard_map.68.refs_0_), channel_id=1, source_target_pairs={{0,4},{1,5},{2,6},{3,7},{4,0},{5,1},{6,2},{7,3},{8,12},{9,13},{10,... | collective-permute-start | bytes 294920 | tf_op jit(solution)/shard_map/ppermute | solution.py:294
  55.5 8.4 %copy-start.2 = (s32[8]{0:T(128)S(1)}, s32[8]{0:T(128)}, u32[]{:S(2)}) copy-start(s32[8]{0:T(128)} %constant.12.clone) | copy-start | bytes 100
  55.5 5.7 %collective-permute-start.10 = (bf16[64,768]{1,0:T(8,128)(2,1)S(1)}, bf16[64,768]{1,0:T(8,128)(2,1)S(1)}, u32[]{:S(2)}, u32[]{:S(2)}) collective-permute-start(bf16[64,768]{1,0:T(8,128)(2,1)S(1)} %shard_map.64.refs_0_), channel_id=1, source_target_pairs={{0,2},{1,3},{2,0},{3,1},{4,6},{5,7},{6,4},{7,5},{8,10},{9,11},{10,... | collective-permute-start | bytes 294920 | tf_op jit(solution)/shard_map/ppermute | solution.py:294
  56.3 5.8 %collective-permute-start.11 = (bf16[64,768]{1,0:T(8,128)(2,1)S(1)}, bf16[64,768]{1,0:T(8,128)(2,1)S(1)}, u32[]{:S(2)}, u32[]{:S(2)}) collective-permute-start(bf16[64,768]{1,0:T(8,128)(2,1)S(1)} %shard_map.64.refs_0_), channel_id=1, source_target_pairs={{0,4},{1,5},{2,6},{3,7},{4,0},{5,1},{6,2},{7,3},{8,12},{9,13},{10,... | collective-permute-start | bytes 294920 | tf_op jit(solution)/shard_map/ppermute | solution.py:294
  58.3 5.5 %collective-permute-start.12 = (bf16[64,768]{1,0:T(8,128)(2,1)S(1)}, bf16[64,768]{1,0:T(8,128)(2,1)S(1)}, u32[]{:S(2)}, u32[]{:S(2)}) collective-permute-start(bf16[64,768]{1,0:T(8,128)(2,1)S(1)} %shard_map.64.refs_0_), channel_id=1, source_target_pairs={{0,6},{1,7},{2,4},{3,5},{4,2},{5,3},{6,0},{7,1},{8,14},{9,15},{10,... | collective-permute-start | bytes 294920 | tf_op jit(solution)/shard_map/ppermute | solution.py:294
  59.1 6.7 %collective-permute-start.28 = (bf16[64,768]{1,0:T(8,128)(2,1)S(1)}, bf16[64,768]{1,0:T(8,128)(2,1)S(1)}, u32[]{:S(2)}, u32[]{:S(2)}) collective-permute-start(bf16[64,768]{1,0:T(8,128)(2,1)S(1)} %shard_map.68.refs_0_), channel_id=1, source_target_pairs={{0,6},{1,7},{2,4},{3,5},{4,2},{5,3},{6,0},{7,1},{8,14},{9,15},{10,... | collective-permute-start | bytes 294920 | tf_op jit(solution)/shard_map/ppermute | solution.py:294
  61.2 5.1 %collective-permute-start.13 = (bf16[64,768]{1,0:T(8,128)(2,1)S(1)}, bf16[64,768]{1,0:T(8,128)(2,1)S(1)}, u32[]{:S(2)}, u32[]{:S(2)}) collective-permute-start(bf16[64,768]{1,0:T(8,128)(2,1)S(1)} %shard_map.64.refs_0_), channel_id=1, source_target_pairs={{0,1},{1,0},{2,3},{3,2},{4,5},{5,4},{6,7},{7,6},{8,9},{9,8},{10,11... | collective-permute-start | bytes 294920 | tf_op jit(solution)/shard_map/ppermute | solution.py:294
  61.3 5.2 %collective-permute-start.14 = (bf16[64,768]{1,0:T(8,128)(2,1)S(1)}, bf16[64,768]{1,0:T(8,128)(2,1)S(1)}, u32[]{:S(2)}, u32[]{:S(2)}) collective-permute-start(bf16[64,768]{1,0:T(8,128)(2,1)S(1)} %collective-permute-done.10.refs_1_), channel_id=1, source_target_pairs={{0,1},{1,0},{2,3},{3,2},{4,5},{5,4},{6,7},{7,6},{8,9},{9,8},{10,11... | collective-permute-start | bytes 294920 | tf_op jit(solution)/shard_map/ppermute | solution.py:294
  62.1 4.7 %collective-permute-start.15 = (bf16[64,768]{1,0:T(8,128)(2,1)S(1)}, bf16[64,768]{1,0:T(8,128)(2,1)S(1)}, u32[]{:S(2)}, u32[]{:S(2)}) collective-permute-start(bf16[64,768]{1,0:T(8,128)(2,1)S(1)} %collective-permute-done.11.refs_2_), channel_id=1, source_target_pairs={{0,1},{1,0},{2,3},{3,2},{4,5},{5,4},{6,7},{7,6},{8,9},{9,8},{10,11... | collective-permute-start | bytes 294920 | tf_op jit(solution)/shard_map/ppermute | solution.py:294
  63.8 3.1 %collective-permute-start.16 = (bf16[64,768]{1,0:T(8,128)(2,1)S(1)}, bf16[64,768]{1,0:T(8,128)(2,1)S(1)}, u32[]{:S(2)}, u32[]{:S(2)}) collective-permute-start(bf16[64,768]{1,0:T(8,128)(2,1)S(1)} %collective-permute-done.12.refs_3_), channel_id=1, source_target_pairs={{0,1},{1,0},{2,3},{3,2},{4,5},{5,4},{6,7},{7,6},{8,9},{9,8},{10,11... | collective-permute-start | bytes 294920 | tf_op jit(solution)/shard_map/ppermute | solution.py:294
  65.8 2.4 %collective-permute-start.29 = (bf16[64,768]{1,0:T(8,128)(2,1)S(1)}, bf16[64,768]{1,0:T(8,128)(2,1)S(1)}, u32[]{:S(2)}, u32[]{:S(2)}) collective-permute-start(bf16[64,768]{1,0:T(8,128)(2,1)S(1)} %shard_map.68.refs_0_), channel_id=1, source_target_pairs={{0,1},{1,0},{2,3},{3,2},{4,5},{5,4},{6,7},{7,6},{8,9},{9,8},{10,11... | collective-permute-start | bytes 294920 | tf_op jit(solution)/shard_map/ppermute | solution.py:294
  66.3 1.8 %collective-permute-start.30 = (bf16[64,768]{1,0:T(8,128)(2,1)S(1)}, bf16[64,768]{1,0:T(8,128)(2,1)S(1)}, u32[]{:S(2)}, u32[]{:S(2)}) collective-permute-start(bf16[64,768]{1,0:T(8,128)(2,1)S(1)} %collective-permute-done.26.refs_1_), channel_id=1, source_target_pairs={{0,1},{1,0},{2,3},{3,2},{4,5},{5,4},{6,7},{7,6},{8,9},{9,8},{10,11... | collective-permute-start | bytes 294920 | tf_op jit(solution)/shard_map/ppermute | solution.py:294
  66.4 1.7 %collective-permute-start.31 = (bf16[64,768]{1,0:T(8,128)(2,1)S(1)}, bf16[64,768]{1,0:T(8,128)(2,1)S(1)}, u32[]{:S(2)}, u32[]{:S(2)}) collective-permute-start(bf16[64,768]{1,0:T(8,128)(2,1)S(1)} %collective-permute-done.27.refs_2_), channel_id=1, source_target_pairs={{0,1},{1,0},{2,3},{3,2},{4,5},{5,4},{6,7},{7,6},{8,9},{9,8},{10,11... | collective-permute-start | bytes 294920 | tf_op jit(solution)/shard_map/ppermute | solution.py:294
  66.9 1.3 %collective-permute-start.32 = (bf16[64,768]{1,0:T(8,128)(2,1)S(1)}, bf16[64,768]{1,0:T(8,128)(2,1)S(1)}, u32[]{:S(2)}, u32[]{:S(2)}) collective-permute-start(bf16[64,768]{1,0:T(8,128)(2,1)S(1)} %collective-permute-done.28.refs_3_), channel_id=1, source_target_pairs={{0,1},{1,0},{2,3},{3,2},{4,5},{5,4},{6,7},{7,6},{8,9},{9,8},{10,11... | collective-permute-start | bytes 294920 | tf_op jit(solution)/shard_map/ppermute | solution.py:294
